TPU v7x, 32 devices: a whole 2x2x4 slice. The times are simulated.
32 devices in a mesh: fx: 2 (over y), fy: 4 (over x, core), st: 4 (over z).
Axes of the slice: x: 2, y: 2, z: 4, core: 2. Of those that a mesh axis runs over, the one named last changes fastest.
Arguments:
- tangent_rhs: bfloat16 [4, 6, 64, 2, 4, 128], P('st', None, None, 'fx', 'fy'), may hold values from -6 to 6
- adjoint_rhs: bfloat16 [4, 6, 64, 2, 4, 128], P('st', None, None, 'fx', 'fy'), may hold values from -6 to 6
- jacobians: bfloat16 [3, 6, 6, 2, 4, 128], P(None, None, None, 'fx', 'fy'), may hold values from -0.75 to 0.75
- deriv: bfloat16 [3, 64, 64], replicated, may hold values from -0.75 to 0.75
- penalty: float32 [6], replicated, may hold values from 0.1 to 0.4
- second_order: float32 [6, 2, 4, 128], P(None, 'fx', 'fy'), may hold values from -4 to 4
- coupling: bfloat16 [6, 384], replicated, may hold values from -2.5 to 2.5
- shell_inverse: bfloat16 [16, 384, 384], P('st')
- shell_load: float32 [4, 16, 384], P(None, 'st'), may hold values from -6 to 6
- shell_adjoint_rhs: float32 [4, 16, 384], P(None, 'st'), may hold values from -6 to 6
- iface_elem: int32 [8, 128], P(('fx', 'fy')), may hold values from 0 to 127
- iface_node: int32 [8, 128], P(('fx', 'fy')), may hold values from 0 to 1023
- iface_weight: float32 [8, 128], P(('fx', 'fy')), may hold values from 0.5 to 2
- iface_count: int32 [8], P(('fx', 'fy')), may hold values from 0 to 128, as said below
Outputs:
- tangent_flow: bfloat16 [4, 6, 64, 2, 4, 128], P('st', None, None, 'fx', 'fy')
- adjoint_flow: bfloat16 [4, 6, 64, 2, 4, 128], P('st', None, None, 'fx', 'fy')
- shell_tangent: float32 [4, 16, 384], P(None, 'st')
- shell_adjoint: float32 [4, 16, 384], P(None, 'st')
Inputs may be any that keep to these rules, and one draw needn't show every extreme that they name: `iface_count`: at most 128 live slots in one flow block; some block has exactly 128.
All inputs are finite; a program needn't handle non-finite values.
Results may differ from a plain program's by a relative error of at most 0.0069.
Values may be sent and summed in bfloat16 or wider, within the bound.
No kernel may reach another device: no remote copies, remote signals or barrier semaphores. Data moves between devices by JAX's collectives and lax.ppermute only.
A program may use at most 64 MiB of HBM per device.

v0:
```python
import jax
import jax.numpy as jnp
from jax import lax
from jax.sharding import PartitionSpec as P

SDOF = 6
PN = 64
FSWEEP = 3
ROUNDS = 2


SIGMA = 0.5


def with_halo(value, sides, width):
    for axis, dim in sides:
        peers, length = (lax.axis_size(axis), value.shape[dim])
        up = [(i, (i + 1) % peers) for i in range(peers - 1)]
        down = [(j, i) for i, j in up]
        last = lax.slice_in_dim(value, length - width, length, axis=dim)
        initial = lax.slice_in_dim(value, 0, width, axis=dim)
        before = lax.ppermute(last, axis, up)
        after = lax.ppermute(initial, axis, down)
        value = jnp.concatenate([before, value, after], axis=dim)
    return value


def face_pair(lower_face, upper_face, below, above, axis):
    length = lower_face.shape[axis]
    beyond_upper = jnp.concatenate(
        [lax.slice_in_dim(lower_face, 1, length, axis=axis), above], axis=axis
    )
    beyond_lower = jnp.concatenate(
        [below, lax.slice_in_dim(upper_face, 0, length - 1, axis=axis)], axis=axis
    )
    return (lower_face - beyond_lower, upper_face - beyond_upper)


def place_faces(jump_low, jump_high, axis):
    middle_shape = list(jump_low.shape)
    middle_shape.insert(axis, 2)
    middle = jnp.zeros(middle_shape, jump_low.dtype)
    return jnp.concatenate(
        [jnp.expand_dims(jump_low, axis), middle, jnp.expand_dims(jump_high, axis)], axis=axis
    )


def as_cube(values):
    members, variables, points, size_x, size_y, size_z = values.shape
    return values.reshape(members, variables, 4, 4, 4, size_x, size_y, size_z)


def face_edges(values):
    cube = as_cube(values)
    received = []
    for node_axis in (2, 3):
        elem_axis = node_axis + 2
        lower_face = jnp.take(cube, 0, axis=node_axis)
        upper_face = jnp.take(cube, 3, axis=node_axis)
        edges = jnp.concatenate([lower_face, upper_face], axis=elem_axis)
        if node_axis == 2:
            extended = with_halo(edges, (("fx", 4),), 1)
        else:
            extended = with_halo(edges, (("fy", 5),), 1)
        below = lax.slice_in_dim(extended, 0, 1, axis=elem_axis)
        above = lax.slice_in_dim(extended, 3, 4, axis=elem_axis)
        received.append((below, above))
    return received


def flow_jumps(values, received):
    cube = as_cube(values)
    result = jnp.zeros(cube.shape, jnp.float32)
    for node_axis in (2, 3, 4):
        elem_axis = node_axis + 2
        lower_face = jnp.take(cube, 0, axis=node_axis).astype(jnp.float32)
        upper_face = jnp.take(cube, 3, axis=node_axis).astype(jnp.float32)
        if received is None or node_axis == 4:
            below = jnp.zeros_like(lax.slice_in_dim(lower_face, 0, 1, axis=elem_axis))
            above = below
        else:
            below = received[node_axis - 2][0].astype(jnp.float32)
            above = received[node_axis - 2][1].astype(jnp.float32)
        jump_low, jump_high = face_pair(lower_face, upper_face, below, above, elem_axis)
        result = result + place_faces(jump_low, jump_high, node_axis)
    return result.reshape(values.shape)


def volume(values, deriv_mats, jac_mats):
    grads = jnp.einsum("kpq,vqxyz->kvpxyz", deriv_mats, values, preferred_element_type=jnp.float32)
    result = jnp.sum(jac_mats[0][:, :, None] * grads[0][None], axis=1)
    for axis_index in (1, 2):
        result = result + jnp.sum(
            jac_mats[axis_index][:, :, None] * grads[axis_index][None], axis=1
        )
    return result


def operator(states, operator_kinds, penalty):
    values = lax.optimization_barrier(states.astype(jnp.bfloat16))
    received = face_edges(values)
    jumps = flow_jumps(values, received)
    volumes = jnp.stack(
        [
            volume(values[member], operator_kinds[member][0], operator_kinds[member][1])
            for member in range(len(operator_kinds))
        ]
    )
    return states + volumes + penalty[None, :, None, None, None, None] * jumps


def body(
    tangent_rhs,
    adjoint_rhs,
    jacobians,
    deriv,
    penalty,
    second_order,
    coupling,
    shell_inverse,
    shell_load,
    shell_adjoint_rhs,
    iface_elem,
    iface_node,
    iface_weight,
    iface_count,
):
    state_shape = tangent_rhs.shape
    variables = state_shape[1]
    points = state_shape[2]
    elements = state_shape[3] * state_shape[4] * state_shape[5]
    slots = iface_elem.shape[1]
    live = (jnp.arange(slots, dtype=jnp.int32) < iface_count[0]).astype(jnp.float32)
    weights = iface_weight[0] * live
    elem_index = iface_elem[0]
    node_index = iface_node[0]
    dof_rows = jnp.arange(SDOF, dtype=jnp.int32)[:, None]
    columns = (node_index // PN)[None, :] * (SDOF * PN) + dof_rows * PN + (node_index % PN)[None, :]
    forward_jac = jacobians.astype(jnp.float32)
    forward_kind = (deriv, forward_jac)
    backward_kind = (jnp.swapaxes(deriv, 1, 2), jnp.swapaxes(forward_jac, 1, 2))
    coupling_cols = coupling.T

    def shell_solve(rhs):
        return jnp.einsum(
            "pab,dpb->dpa",
            shell_inverse,
            rhs.astype(jnp.bfloat16),
            preferred_element_type=jnp.float32,
        )

    shell_tangent = shell_solve(shell_load)
    shell_adjoint = jnp.zeros(shell_load.shape, jnp.float32)
    tangent = jnp.zeros(state_shape, jnp.float32)
    adjoint = jnp.zeros(state_shape, jnp.float32)
    for round_index in range(ROUNDS):
        received = lax.all_to_all(
            shell_tangent.astype(jnp.bfloat16), "st", split_axis=0, concat_axis=1, tiled=True
        )
        picked = received.reshape(-1)[columns]
        pushed_cols = (
            jnp.dot(coupling_cols, picked, preferred_element_type=jnp.float32) * weights[None, :]
        )
        pushed = (
            jnp.zeros((variables * points, elements), jnp.float32)
            .at[:, elem_index]
            .add(pushed_cols)
        )
        force = tangent_rhs.astype(jnp.float32) - pushed.reshape(state_shape)
        adjoint_source = adjoint_rhs.astype(jnp.float32) + second_order[None, :, None] * tangent
        paired = jnp.concatenate([tangent, adjoint])
        sources = jnp.concatenate([force, adjoint_source])
        for sweep in range(FSWEEP):
            paired = paired + SIGMA * (
                sources - operator(paired, (forward_kind, backward_kind), penalty)
            )
        tangent = paired[:1]
        adjoint = paired[1:]
        adjoint_values = adjoint.astype(jnp.bfloat16).reshape(variables * points, elements)
        gathered = adjoint_values[:, elem_index]
        loads = jnp.dot(coupling, gathered, preferred_element_type=jnp.float32) * weights[None, :]
        panels = received.shape[1]
        partial_loads = jnp.zeros((panels * SDOF * PN,), jnp.float32).at[columns].add(loads)
        partial_loads = partial_loads.reshape(1, panels, SDOF * PN)
        summed = lax.psum(partial_loads, ("fx", "fy"))
        owned = lax.all_to_all(summed, "st", split_axis=1, concat_axis=0, tiled=True)
        shell_adjoint = shell_solve(shell_adjoint_rhs - owned)
        shell_tangent = shell_solve(shell_load + shell_adjoint)
    return (
        tangent.astype(jnp.bfloat16),
        adjoint.astype(jnp.bfloat16),
        shell_tangent,
        shell_adjoint,
    )


def solution(mesh):
    in_specs = (
        P("st", None, None, "fx", "fy", None),
        P("st", None, None, "fx", "fy", None),
        P(None, None, None, "fx", "fy", None),
        P(),
        P(),
        P(None, "fx", "fy", None),
        P(),
        P("st", None, None),
        P(None, "st", None),
        P(None, "st", None),
        P(("fx", "fy"), None),
        P(("fx", "fy"), None),
        P(("fx", "fy"), None),
        P(("fx", "fy")),
    )
    out_specs = (
        P("st", None, None, "fx", "fy", None),
        P("st", None, None, "fx", "fy", None),
        P(None, "st", None),
        P(None, "st", None),
    )
    return jax.shard_map(body, mesh=mesh, in_specs=in_specs, out_specs=out_specs, check_vma=False)
```

profile of v0, /device:TPU:0, one launch (start us, length us, event | category | flops | bytes accessed | tf_op | source)
XLA Modules:
  0.0 207.5 jit_solution(6584082621477791752)
XLA Ops:
  0.7 5.0 %collective-permute-start = (bf16[2,6,4,4,1,1,128]{6,3,2,1,0,5,4:T(4,128)(2,1)S(1)}, bf16[2,6,4,4,1,1,128]{6,3,2,1,0,5,4:T(4,128)(2,1)S(1)}, u32[]{:S(2)}, u32[]{:S(2)}) collective-permute-start(bf16[2,6,4,4,1,1,128]{6,3,2,1,0,5,4:T(4,128)(2,1)S(1)} %get-tuple-element.197), channel_id=1, source_target_pairs={{0,16},{1,17},{2,18},{3,19},{4,20},{5,21},{6,22},{7,23},{8,24},{9,... | collective-permute-start | bytes 147464 | tf_op jit(solution)/shard_map/ppermute | solution.py:22
  5.8 1.3 collective-permute-start.1
  7.1 1.5 collective-permute-start.2
  8.6 1.3 collective-permute-start.3
  11.7 4.9 %all-to-all-start = ((bf16[4,4,384]{2,1,0:T(4,128)(2,1)}), bf16[4,4,384]{2,1,0:T(4,128)(2,1)S(1)}, u32[]{:S(2)}, u32[]{:S(2)}) async-start(bf16[4,4,384]{2,1,0:T(4,128)(2,1)} %copy.260), calls=%async_computation | async-start | bytes 24576 | tf_op jit(solution)/shard_map/all_to_all | solution.py:157
  21.0 1.2 all-to-all-done
  22.2 5.0 %gather_fusion = bf16[768]{0:T(1024)(128)(2,1)S(1)} fusion(bf16[6144]{0:T(1024)(128)(2,1)S(1)} %reshape.2599, s32[1024]{0:T(1024)S(1)} %pad_clamp_fusion.1), kind=kCustom, calls=%fused_computation | custom fusion | bytes 6144 | tf_op jit(solution)/shard_map/gather | solution.py:160
  27.5 1.4 scatter_custom_fusion
  31.5 4.4 %collective-permute-start.4 = (bf16[2,6,4,4,1,1,128]{6,3,2,1,0,5,4:T(4,128)(2,1)S(1)}, bf16[2,6,4,4,1,1,128]{6,3,2,1,0,5,4:T(4,128)(2,1)S(1)}, u32[]{:S(2)}, u32[]{:S(2)}) collective-permute-start(bf16[2,6,4,4,1,1,128]{6,3,2,1,0,5,4:T(4,128)(2,1)S(1)} %get-tuple-element.187), channel_id=1, source_target_pairs={{0,16},{1,17},{2,18},{3,19},{4,20},{5,21},{6,22},{7,23},{8,24},{9,... | collective-permute-start | bytes 147464 | tf_op jit(solution)/shard_map/ppermute | solution.py:22
  35.9 1.3 collective-permute-start.5
  37.2 3.0 %collective-permute-start.6 = (bf16[2,6,4,4,1,1,128]{6,3,2,1,0,5,4:T(4,128)(2,1)S(1)}, bf16[2,6,4,4,1,1,128]{6,3,2,1,0,5,4:T(4,128)(2,1)S(1)}, u32[]{:S(2)}, u32[]{:S(2)}) collective-permute-start(bf16[2,6,4,4,1,1,128]{6,3,2,1,0,5,4:T(4,128)(2,1)S(1)} %get-tuple-element.185), channel_id=1, source_target_pairs={{0,4},{4,8},{8,12},{1,5},{5,9},{9,13},{2,6},{6,10},{10,14},{3,7},{... | collective-permute-start | bytes 147464 | tf_op jit(solution)/shard_map/ppermute | solution.py:22
  40.3 1.3 collective-permute-start.7
  42.3 4.1 %collective-permute-done.7 = bf16[2,6,4,4,1,1,128]{6,3,2,1,0,5,4:T(4,128)(2,1)S(1)} collective-permute-done((bf16[2,6,4,4,1,1,128]{6,3,2,1,0,5,4:T(4,128)(2,1)S(1)}, bf16[2,6,4,4,1,1,128]{6,3,2,1,0,5,4:T(4,128)(2,1)S(1)}, u32[]{:S(2)}, u32[]{:S(2)}) %collective-permute-start.7) | collective-permute-done | bytes 49184 | tf_op jit(solution)/shard_map/ppermute | solution.py:23
  48.7 4.7 %collective-permute-start.10 = (bf16[2,6,4,4,1,1,128]{6,3,2,1,0,5,4:T(4,128)(2,1)S(1)}, bf16[2,6,4,4,1,1,128]{6,3,2,1,0,5,4:T(4,128)(2,1)S(1)}, u32[]{:S(2)}, u32[]{:S(2)}) collective-permute-start(bf16[2,6,4,4,1,1,128]{6,3,2,1,0,5,4:T(4,128)(2,1)S(1)} %get-tuple-element.175), channel_id=1, source_target_pairs={{0,4},{4,8},{8,12},{1,5},{5,9},{9,13},{2,6},{6,10},{10,14},{3,7},{... | collective-permute-start | bytes 147464 | tf_op jit(solution)/shard_map/ppermute | solution.py:22
  53.4 1.3 collective-permute-start.11
  54.7 4.5 %collective-permute-start.8 = (bf16[2,6,4,4,1,1,128]{6,3,2,1,0,5,4:T(4,128)(2,1)S(1)}, bf16[2,6,4,4,1,1,128]{6,3,2,1,0,5,4:T(4,128)(2,1)S(1)}, u32[]{:S(2)}, u32[]{:S(2)}) collective-permute-start(bf16[2,6,4,4,1,1,128]{6,3,2,1,0,5,4:T(4,128)(2,1)S(1)} %get-tuple-element.177), channel_id=1, source_target_pairs={{0,16},{1,17},{2,18},{3,19},{4,20},{5,21},{6,22},{7,23},{8,24},{9,... | collective-permute-start | bytes 147464 | tf_op jit(solution)/shard_map/ppermute | solution.py:22
  59.3 1.3 collective-permute-start.9
  61.2 4.4 %collective-permute-done.9 = bf16[2,6,4,4,1,1,128]{6,3,2,1,0,5,4:T(4,128)(2,1)S(1)} collective-permute-done((bf16[2,6,4,4,1,1,128]{6,3,2,1,0,5,4:T(4,128)(2,1)S(1)}, bf16[2,6,4,4,1,1,128]{6,3,2,1,0,5,4:T(4,128)(2,1)S(1)}, u32[]{:S(2)}, u32[]{:S(2)}) %collective-permute-start.9) | collective-permute-done | bytes 49184 | tf_op jit(solution)/shard_map/ppermute | solution.py:23
  71.2 2.1 collective-permute-start.12
  73.4 1.1 gather_fusion.1
  75.3 4.8 %scatter_custom_fusion.1 = f32[6144]{0:T(1024)S(1)} fusion(s32[768]{0:T(1024)} %copy-done.12, f32[768]{0:T(1024)S(1)} %fusion.5, f32[]{:T(128)} %constant.129.clone.1), kind=kCustom, calls=%fused_computation.296 | custom fusion | flops 768 | bytes 25088 | tf_op jit(solution)/shard_map/scatter-add | solution.py:183
  80.0 23.1 %psum.14 = f32[1,16,384]{2,0,1:T(1,128)} all-reduce(f32[1,16,384]{2,0,1:T(1,128)S(1)} %bitcast.739), channel_id=1, replica_groups=mesh['fx'=2,'fy'=4,'st'=4] {'fx','fy'}, use_global_device_ids=true, to_apply=%region_20.27 | all-reduce | flops 6144 | bytes 49152 | tf_op jit(solution)/shard_map/psum | solution.py:185
  103.2 3.9 %all-to-all-start.1 = ((f32[1,16,384]{2,0,1:T(1,128)}), f32[1,16,384]{2,0,1:T(1,128)}, u32[]{:S(2)}, u32[]{:S(2)}) async-start(f32[1,16,384]{2,0,1:T(1,128)} %psum.14), calls=%async_computation.1 | async-start | bytes 49152 | tf_op jit(solution)/shard_map/all_to_all | solution.py:186
  108.1 1.0 add_bitcast_fusion.4
  109.0 0.9 pad_subtract_fusion.4
  110.0 1.3 collective-permute-start.13
  111.3 1.3 collective-permute-start.14
  112.6 1.3 collective-permute-start.15
  115.4 1.5 fusion.3
  117.6 5.1 %all-to-all-start.2 = ((bf16[4,4,384]{2,1,0:T(4,128)(2,1)}), bf16[4,4,384]{2,1,0:T(4,128)(2,1)S(1)}, u32[]{:S(2)}, u32[]{:S(2)}) async-start(bf16[4,4,384]{2,1,0:T(4,128)(2,1)} %copy.301), calls=%async_computation.2 | async-start | bytes 24576 | tf_op jit(solution)/shard_map/all_to_all | solution.py:157
  123.9 4.4 %all-to-all-done.2 = bf16[4,4,384]{2,1,0:T(4,128)(2,1)S(1)} async-done(((bf16[4,4,384]{2,1,0:T(4,128)(2,1)}), bf16[4,4,384]{2,1,0:T(4,128)(2,1)S(1)}, u32[]{:S(2)}, u32[]{:S(2)}) %all-to-all-start.2) | async-done | bytes 12320 | tf_op jit(solution)/shard_map/all_to_all | solution.py:157
  128.3 5.0 %gather_fusion.2 = bf16[768]{0:T(1024)(128)(2,1)S(1)} fusion(bf16[6144]{0:T(1024)(128)(2,1)S(1)} %reshape.2612, s32[1024]{0:T(1024)S(1)} %pad_clamp_fusion.1), kind=kCustom, calls=%fused_computation.2 | custom fusion | bytes 6144 | tf_op jit(solution)/shard_map/gather | solution.py:160
  133.6 1.5 scatter_custom_fusion.2
  137.1 4.5 %collective-permute-start.16 = (bf16[2,6,4,4,1,1,128]{6,3,2,1,0,5,4:T(4,128)(2,1)S(1)}, bf16[2,6,4,4,1,1,128]{6,3,2,1,0,5,4:T(4,128)(2,1)S(1)}, u32[]{:S(2)}, u32[]{:S(2)}) collective-permute-start(bf16[2,6,4,4,1,1,128]{6,3,2,1,0,5,4:T(4,128)(2,1)S(1)} %get-tuple-element.157), channel_id=1, source_target_pairs={{0,16},{1,17},{2,18},{3,19},{4,20},{5,21},{6,22},{7,23},{8,24},{9,... | collective-permute-start | bytes 147464 | tf_op jit(solution)/shard_map/ppermute | solution.py:22
  141.7 1.3 collective-permute-start.17
  143.0 1.3 collective-permute-start.18
  144.3 1.3 collective-permute-start.19
  145.7 1.9 collective-permute-done.17
  147.6 1.9 collective-permute-done.19
  151.2 4.5 %collective-permute-start.20 = (bf16[2,6,4,4,1,1,128]{6,3,2,1,0,5,4:T(4,128)(2,1)S(1)}, bf16[2,6,4,4,1,1,128]{6,3,2,1,0,5,4:T(4,128)(2,1)S(1)}, u32[]{:S(2)}, u32[]{:S(2)}) collective-permute-start(bf16[2,6,4,4,1,1,128]{6,3,2,1,0,5,4:T(4,128)(2,1)S(1)} %get-tuple-element.147), channel_id=1, source_target_pairs={{0,16},{1,17},{2,18},{3,19},{4,20},{5,21},{6,22},{7,23},{8,24},{9,... | collective-permute-start | bytes 147464 | tf_op jit(solution)/shard_map/ppermute | solution.py:22
  155.7 1.3 collective-permute-start.21
  157.0 4.4 %collective-permute-start.22 = (bf16[2,6,4,4,1,1,128]{6,3,2,1,0,5,4:T(4,128)(2,1)S(1)}, bf16[2,6,4,4,1,1,128]{6,3,2,1,0,5,4:T(4,128)(2,1)S(1)}, u32[]{:S(2)}, u32[]{:S(2)}) collective-permute-start(bf16[2,6,4,4,1,1,128]{6,3,2,1,0,5,4:T(4,128)(2,1)S(1)} %get-tuple-element.145), channel_id=1, source_target_pairs={{0,4},{4,8},{8,12},{1,5},{5,9},{9,13},{2,6},{6,10},{10,14},{3,7},{... | collective-permute-start | bytes 147464 | tf_op jit(solution)/shard_map/ppermute | solution.py:22
  161.4 1.3 collective-permute-start.23
  163.5 1.0 collective-permute-done.23
  166.0 1.1 gather_fusion.3
  167.3 4.8 %scatter_custom_fusion.3 = f32[6144]{0:T(1024)S(1)} fusion(s32[768]{0:T(1024)} %copy-done.12, f32[768]{0:T(1024)S(1)} %fusion.4, f32[]{:T(128)} %constant.129.clone.1), kind=kCustom, calls=%fused_computation.294 | custom fusion | flops 768 | bytes 25088 | tf_op jit(solution)/shard_map/scatter-add | solution.py:183
  172.0 25.3 %psum.15 = f32[1,16,384]{2,0,1:T(1,128)S(1)} all-reduce(f32[1,16,384]{2,0,1:T(1,128)S(1)} %bitcast.738), channel_id=1, replica_groups=mesh['fx'=2,'fy'=4,'st'=4] {'fx','fy'}, use_global_device_ids=true, to_apply=%region_41.48 | all-reduce | flops 6144 | bytes 49152 | tf_op jit(solution)/shard_map/psum | solution.py:185
  197.3 8.0 %all_to_all.42 = f32[1,16,384]{2,0,1:T(1,128)S(1)} all-to-all(f32[1,16,384]{2,0,1:T(1,128)S(1)} %psum.15), channel_id=1, replica_groups=mesh['fx'=2,'fy'=4,'st'=4] {'st'}, dimensions={1} | all-to-all | bytes 49152 | tf_op jit(solution)/shard_map/all_to_all | solution.py:186
  (240 shorter events, 30.6 us)
Async XLA Ops:
  0.6 10.0 %copy-start = (bf16[4,384,384]{2,1,0:T(8,128)(2,1)S(1)}, bf16[4,384,384]{2,1,0:T(8,128)(2,1)}, u32[]{:S(2)}) copy-start(bf16[4,384,384]{2,1,0:T(8,128)(2,1)} %param.33) | copy-start | bytes 3538948
  0.6 16.1 %copy-start.1 = (bf16[3,64,64]{2,1,0:T(8,128)(2,1)S(1)}, bf16[3,64,64]{2,1,0:T(8,128)(2,1)}, u32[]{:S(2)}) copy-start(bf16[3,64,64]{2,1,0:T(8,128)(2,1)} %param.29) | copy-start | bytes 73732
  0.7 28.4 %collective-permute-start = (bf16[2,6,4,4,1,1,128]{6,3,2,1,0,5,4:T(4,128)(2,1)S(1)}, bf16[2,6,4,4,1,1,128]{6,3,2,1,0,5,4:T(4,128)(2,1)S(1)}, u32[]{:S(2)}, u32[]{:S(2)}) collective-permute-start(bf16[2,6,4,4,1,1,128]{6,3,2,1,0,5,4:T(4,128)(2,1)S(1)} %get-tuple-element.197), channel_id=1, source_target_pairs={{0,16},{1,17},{2,18},{3,19},{4,20},{5,21},{6,22},{7,23},{8,24},{9,... | collective-permute-start | bytes 147464 | tf_op jit(solution)/shard_map/ppermute | solution.py:22
  5.8 23.3 %collective-permute-start.1 = (bf16[2,6,4,4,1,1,128]{6,3,2,1,0,5,4:T(4,128)(2,1)S(1)}, bf16[2,6,4,4,1,1,128]{6,3,2,1,0,5,4:T(4,128)(2,1)S(1)}, u32[]{:S(2)}, u32[]{:S(2)}) collective-permute-start(bf16[2,6,4,4,1,1,128]{6,3,2,1,0,5,4:T(4,128)(2,1)S(1)} %get-tuple-element.198), channel_id=1, source_target_pairs={{16,0},{17,1},{18,2},{19,3},{20,4},{21,5},{22,6},{23,7},{24,8},{25... | collective-permute-start | bytes 147464 | tf_op jit(solution)/shard_map/ppermute | solution.py:23
  7.1 22.0 %collective-permute-start.2 = (bf16[2,6,4,4,1,1,128]{6,3,2,1,0,5,4:T(4,128)(2,1)S(1)}, bf16[2,6,4,4,1,1,128]{6,3,2,1,0,5,4:T(4,128)(2,1)S(1)}, u32[]{:S(2)}, u32[]{:S(2)}) collective-permute-start(bf16[2,6,4,4,1,1,128]{6,3,2,1,0,5,4:T(4,128)(2,1)S(1)} %get-tuple-element.195), channel_id=1, source_target_pairs={{0,4},{4,8},{8,12},{1,5},{5,9},{9,13},{2,6},{6,10},{10,14},{3,7},{... | collective-permute-start | bytes 147464 | tf_op jit(solution)/shard_map/ppermute | solution.py:22
  8.6 20.5 %collective-permute-start.3 = (bf16[2,6,4,4,1,1,128]{6,3,2,1,0,5,4:T(4,128)(2,1)S(1)}, bf16[2,6,4,4,1,1,128]{6,3,2,1,0,5,4:T(4,128)(2,1)S(1)}, u32[]{:S(2)}, u32[]{:S(2)}) collective-permute-start(bf16[2,6,4,4,1,1,128]{6,3,2,1,0,5,4:T(4,128)(2,1)S(1)} %get-tuple-element.196), channel_id=1, source_target_pairs={{4,0},{8,4},{12,8},{5,1},{9,5},{13,9},{6,2},{10,6},{14,10},{7,3},{... | collective-permute-start | bytes 147464 | tf_op jit(solution)/shard_map/ppermute | solution.py:23
  11.7 10.5 %all-to-all-start = ((bf16[4,4,384]{2,1,0:T(4,128)(2,1)}), bf16[4,4,384]{2,1,0:T(4,128)(2,1)S(1)}, u32[]{:S(2)}, u32[]{:S(2)}) async-start(bf16[4,4,384]{2,1,0:T(4,128)(2,1)} %copy.260), calls=%async_computation | async-start | bytes 24576 | tf_op jit(solution)/shard_map/all_to_all | solution.py:157
  16.6 0.8 copy-start.9
  17.5 0.7 copy-start.17
  17.5 1.4 copy-start.18
  17.5 1.4 copy-start.13
  17.6 1.6 copy-start.19
  18.2 1.1 copy-start.12
  18.9 8.6 %copy-start.16 = (s32[128]{0:T(128)}, s32[128]{0:T(128)S(1)}, u32[]{:S(2)}) copy-start(s32[128]{0:T(128)S(1)} %fusion.77) | copy-start | bytes 1540
  19.2 8.0 %copy-start.14 = (f32[128]{0:T(128)}, f32[128]{0:T(128)S(1)}, u32[]{:S(2)}) copy-start(f32[128]{0:T(128)S(1)} %fusion.76) | copy-start | bytes 1540
  19.7 7.5 %copy-start.7 = (bf16[6,384]{1,0:T(8,128)(2,1)S(1)}, bf16[6,384]{1,0:T(8,128)(2,1)}, u32[]{:S(2)}) copy-start(bf16[6,384]{1,0:T(8,128)(2,1)} %param.32) | copy-start | bytes 13828
  22.2 6.8 %copy-start.3 = (bf16[1,6,64,1,1,128]{5,2,4,3,1,0:T(8,128)(2,1)S(1)}, bf16[1,6,64,1,1,128]{5,2,4,3,1,0:T(8,128)(2,1)}, u32[]{:S(2)}) copy-start(bf16[1,6,64,1,1,128]{5,2,4,3,1,0:T(8,128)(2,1)} %param.27) | copy-start | bytes 294916
  22.2 6.8 %copy-start.4 = (bf16[1,6,64,1,1,128]{5,2,4,3,1,0:T(8,128)(2,1)S(1)}, bf16[1,6,64,1,1,128]{5,2,4,3,1,0:T(8,128)(2,1)}, u32[]{:S(2)}) copy-start(bf16[1,6,64,1,1,128]{5,2,4,3,1,0:T(8,128)(2,1)} %param.26) | copy-start | bytes 294916
  29.0 0.7 copy-start.10
  31.5 10.2 %collective-permute-start.4 = (bf16[2,6,4,4,1,1,128]{6,3,2,1,0,5,4:T(4,128)(2,1)S(1)}, bf16[2,6,4,4,1,1,128]{6,3,2,1,0,5,4:T(4,128)(2,1)S(1)}, u32[]{:S(2)}, u32[]{:S(2)}) collective-permute-start(bf16[2,6,4,4,1,1,128]{6,3,2,1,0,5,4:T(4,128)(2,1)S(1)} %get-tuple-element.187), channel_id=1, source_target_pairs={{0,16},{1,17},{2,18},{3,19},{4,20},{5,21},{6,22},{7,23},{8,24},{9,... | collective-permute-start | bytes 147464 | tf_op jit(solution)/shard_map/ppermute | solution.py:22
  35.9 6.3 %collective-permute-start.5 = (bf16[2,6,4,4,1,1,128]{6,3,2,1,0,5,4:T(4,128)(2,1)S(1)}, bf16[2,6,4,4,1,1,128]{6,3,2,1,0,5,4:T(4,128)(2,1)S(1)}, u32[]{:S(2)}, u32[]{:S(2)}) collective-permute-start(bf16[2,6,4,4,1,1,128]{6,3,2,1,0,5,4:T(4,128)(2,1)S(1)} %get-tuple-element.188), channel_id=1, source_target_pairs={{16,0},{17,1},{18,2},{19,3},{20,4},{21,5},{22,6},{23,7},{24,8},{25... | collective-permute-start | bytes 147464 | tf_op jit(solution)/shard_map/ppermute | solution.py:23
  37.2 5.0 %collective-permute-start.6 = (bf16[2,6,4,4,1,1,128]{6,3,2,1,0,5,4:T(4,128)(2,1)S(1)}, bf16[2,6,4,4,1,1,128]{6,3,2,1,0,5,4:T(4,128)(2,1)S(1)}, u32[]{:S(2)}, u32[]{:S(2)}) collective-permute-start(bf16[2,6,4,4,1,1,128]{6,3,2,1,0,5,4:T(4,128)(2,1)S(1)} %get-tuple-element.185), channel_id=1, source_target_pairs={{0,4},{4,8},{8,12},{1,5},{5,9},{9,13},{2,6},{6,10},{10,14},{3,7},{... | collective-permute-start | bytes 147464 | tf_op jit(solution)/shard_map/ppermute | solution.py:22
  40.3 6.1 %collective-permute-start.7 = (bf16[2,6,4,4,1,1,128]{6,3,2,1,0,5,4:T(4,128)(2,1)S(1)}, bf16[2,6,4,4,1,1,128]{6,3,2,1,0,5,4:T(4,128)(2,1)S(1)}, u32[]{:S(2)}, u32[]{:S(2)}) collective-permute-start(bf16[2,6,4,4,1,1,128]{6,3,2,1,0,5,4:T(4,128)(2,1)S(1)} %get-tuple-element.186), channel_id=1, source_target_pairs={{4,0},{8,4},{12,8},{5,1},{9,5},{13,9},{6,2},{10,6},{14,10},{7,3},{... | collective-permute-start | bytes 147464 | tf_op jit(solution)/shard_map/ppermute | solution.py:23
  48.7 12.0 %collective-permute-start.10 = (bf16[2,6,4,4,1,1,128]{6,3,2,1,0,5,4:T(4,128)(2,1)S(1)}, bf16[2,6,4,4,1,1,128]{6,3,2,1,0,5,4:T(4,128)(2,1)S(1)}, u32[]{:S(2)}, u32[]{:S(2)}) collective-permute-start(bf16[2,6,4,4,1,1,128]{6,3,2,1,0,5,4:T(4,128)(2,1)S(1)} %get-tuple-element.175), channel_id=1, source_target_pairs={{0,4},{4,8},{8,12},{1,5},{5,9},{9,13},{2,6},{6,10},{10,14},{3,7},{... | collective-permute-start | bytes 147464 | tf_op jit(solution)/shard_map/ppermute | solution.py:22
  53.4 7.3 %collective-permute-start.11 = (bf16[2,6,4,4,1,1,128]{6,3,2,1,0,5,4:T(4,128)(2,1)S(1)}, bf16[2,6,4,4,1,1,128]{6,3,2,1,0,5,4:T(4,128)(2,1)S(1)}, u32[]{:S(2)}, u32[]{:S(2)}) collective-permute-start(bf16[2,6,4,4,1,1,128]{6,3,2,1,0,5,4:T(4,128)(2,1)S(1)} %get-tuple-element.176), channel_id=1, source_target_pairs={{4,0},{8,4},{12,8},{5,1},{9,5},{13,9},{6,2},{10,6},{14,10},{7,3},{... | collective-permute-start | bytes 147464 | tf_op jit(solution)/shard_map/ppermute | solution.py:23
  54.7 6.5 %collective-permute-start.8 = (bf16[2,6,4,4,1,1,128]{6,3,2,1,0,5,4:T(4,128)(2,1)S(1)}, bf16[2,6,4,4,1,1,128]{6,3,2,1,0,5,4:T(4,128)(2,1)S(1)}, u32[]{:S(2)}, u32[]{:S(2)}) collective-permute-start(bf16[2,6,4,4,1,1,128]{6,3,2,1,0,5,4:T(4,128)(2,1)S(1)} %get-tuple-element.177), channel_id=1, source_target_pairs={{0,16},{1,17},{2,18},{3,19},{4,20},{5,21},{6,22},{7,23},{8,24},{9,... | collective-permute-start | bytes 147464 | tf_op jit(solution)/shard_map/ppermute | solution.py:22
  59.3 6.4 %collective-permute-start.9 = (bf16[2,6,4,4,1,1,128]{6,3,2,1,0,5,4:T(4,128)(2,1)S(1)}, bf16[2,6,4,4,1,1,128]{6,3,2,1,0,5,4:T(4,128)(2,1)S(1)}, u32[]{:S(2)}, u32[]{:S(2)}) collective-permute-start(bf16[2,6,4,4,1,1,128]{6,3,2,1,0,5,4:T(4,128)(2,1)S(1)} %get-tuple-element.178), channel_id=1, source_target_pairs={{16,0},{17,1},{18,2},{19,3},{20,4},{21,5},{22,6},{23,7},{24,8},{25... | collective-permute-start | bytes 147464 | tf_op jit(solution)/shard_map/ppermute | solution.py:23
  71.2 51.5 %collective-permute-start.12 = (bf16[2,6,4,4,1,1,128]{6,3,2,1,0,5,4:T(4,128)(2,1)}, bf16[2,6,4,4,1,1,128]{6,3,2,1,0,5,4:T(4,128)(2,1)}, u32[]{:S(2)}, u32[]{:S(2)}) collective-permute-start(bf16[2,6,4,4,1,1,128]{6,3,2,1,0,5,4:T(4,128)(2,1)} %get-tuple-element.167), channel_id=1, source_target_pairs={{0,16},{1,17},{2,18},{3,19},{4,20},{5,21},{6,22},{7,23},{8,24},{9,... | collective-permute-start | bytes 147464 | tf_op jit(solution)/shard_map/ppermute | solution.py:22
  73.3 34.7 %copy-start.2 = (f32[6,64,128]{2,1,0:T(8,128)S(1)}, f32[6,64,128]{2,1,0:T(8,128)}, u32[]{:S(2)}) copy-start(f32[6,64,128]{2,1,0:T(8,128)} %multiply_reduce_fusion.12) | copy-start | bytes 589828
  103.2 10.7 %all-to-all-start.1 = ((f32[1,16,384]{2,0,1:T(1,128)}), f32[1,16,384]{2,0,1:T(1,128)}, u32[]{:S(2)}, u32[]{:S(2)}) async-start(f32[1,16,384]{2,0,1:T(1,128)} %psum.14), calls=%async_computation.1 | async-start | bytes 49152 | tf_op jit(solution)/shard_map/all_to_all | solution.py:186
  110.0 12.7 %collective-permute-start.13 = (bf16[2,6,4,4,1,1,128]{6,3,2,1,0,5,4:T(4,128)(2,1)}, bf16[2,6,4,4,1,1,128]{6,3,2,1,0,5,4:T(4,128)(2,1)S(1)}, u32[]{:S(2)}, u32[]{:S(2)}) collective-permute-start(bf16[2,6,4,4,1,1,128]{6,3,2,1,0,5,4:T(4,128)(2,1)} %get-tuple-element.168), channel_id=1, source_target_pairs={{16,0},{17,1},{18,2},{19,3},{20,4},{21,5},{22,6},{23,7},{24,8},{25... | collective-permute-start | bytes 147464 | tf_op jit(solution)/shard_map/ppermute | solution.py:23
  111.3 11.4 %collective-permute-start.14 = (bf16[2,6,4,4,1,1,128]{6,3,2,1,0,5,4:T(4,128)(2,1)}, bf16[2,6,4,4,1,1,128]{6,3,2,1,0,5,4:T(4,128)(2,1)S(1)}, u32[]{:S(2)}, u32[]{:S(2)}) collective-permute-start(bf16[2,6,4,4,1,1,128]{6,3,2,1,0,5,4:T(4,128)(2,1)} %get-tuple-element.165), channel_id=1, source_target_pairs={{0,4},{4,8},{8,12},{1,5},{5,9},{9,13},{2,6},{6,10},{10,14},{3,7},{... | collective-permute-start | bytes 147464 | tf_op jit(solution)/shard_map/ppermute | solution.py:22
  112.6 10.1 %collective-permute-start.15 = (bf16[2,6,4,4,1,1,128]{6,3,2,1,0,5,4:T(4,128)(2,1)}, bf16[2,6,4,4,1,1,128]{6,3,2,1,0,5,4:T(4,128)(2,1)S(1)}, u32[]{:S(2)}, u32[]{:S(2)}) collective-permute-start(bf16[2,6,4,4,1,1,128]{6,3,2,1,0,5,4:T(4,128)(2,1)} %get-tuple-element.166), channel_id=1, source_target_pairs={{4,0},{8,4},{12,8},{5,1},{9,5},{13,9},{6,2},{10,6},{14,10},{7,3},{... | collective-permute-start | bytes 147464 | tf_op jit(solution)/shard_map/ppermute | solution.py:23
  117.6 10.7 %all-to-all-start.2 = ((bf16[4,4,384]{2,1,0:T(4,128)(2,1)}), bf16[4,4,384]{2,1,0:T(4,128)(2,1)S(1)}, u32[]{:S(2)}, u32[]{:S(2)}) async-start(bf16[4,4,384]{2,1,0:T(4,128)(2,1)} %copy.301), calls=%async_computation.2 | async-start | bytes 24576 | tf_op jit(solution)/shard_map/all_to_all | solution.py:157
  123.9 9.4 %copy-start.15 = (f32[128]{0:T(128)S(1)}, f32[128]{0:T(128)}, u32[]{:S(2)}) copy-start(f32[128]{0:T(128)} %copy-done.14) | copy-start | bytes 1540
  128.3 6.9 %copy-start.5 = (bf16[1,6,64,1,1,128]{5,2,4,3,1,0:T(8,128)(2,1)S(1)}, bf16[1,6,64,1,1,128]{5,2,4,3,1,0:T(8,128)(2,1)}, u32[]{:S(2)}) copy-start(bf16[1,6,64,1,1,128]{5,2,4,3,1,0:T(8,128)(2,1)} %param.26) | copy-start | bytes 294916
  128.3 7.0 %copy-start.11 = (f32[6]{0:T(128)S(1)}, f32[6]{0:T(128)}, u32[]{:S(2)}) copy-start(f32[6]{0:T(128)} %param.30) | copy-start | bytes 76
  137.1 8.6 %collective-permute-start.16 = (bf16[2,6,4,4,1,1,128]{6,3,2,1,0,5,4:T(4,128)(2,1)S(1)}, bf16[2,6,4,4,1,1,128]{6,3,2,1,0,5,4:T(4,128)(2,1)S(1)}, u32[]{:S(2)}, u32[]{:S(2)}) collective-permute-start(bf16[2,6,4,4,1,1,128]{6,3,2,1,0,5,4:T(4,128)(2,1)S(1)} %get-tuple-element.157), channel_id=1, source_target_pairs={{0,16},{1,17},{2,18},{3,19},{4,20},{5,21},{6,22},{7,23},{8,24},{9,... | collective-permute-start | bytes 147464 | tf_op jit(solution)/shard_map/ppermute | solution.py:22
  141.7 6.0 %collective-permute-start.17 = (bf16[2,6,4,4,1,1,128]{6,3,2,1,0,5,4:T(4,128)(2,1)S(1)}, bf16[2,6,4,4,1,1,128]{6,3,2,1,0,5,4:T(4,128)(2,1)S(1)}, u32[]{:S(2)}, u32[]{:S(2)}) collective-permute-start(bf16[2,6,4,4,1,1,128]{6,3,2,1,0,5,4:T(4,128)(2,1)S(1)} %get-tuple-element.158), channel_id=1, source_target_pairs={{16,0},{17,1},{18,2},{19,3},{20,4},{21,5},{22,6},{23,7},{24,8},{25... | collective-permute-start | bytes 147464 | tf_op jit(solution)/shard_map/ppermute | solution.py:23
  143.0 4.7 %collective-permute-start.18 = (bf16[2,6,4,4,1,1,128]{6,3,2,1,0,5,4:T(4,128)(2,1)S(1)}, bf16[2,6,4,4,1,1,128]{6,3,2,1,0,5,4:T(4,128)(2,1)S(1)}, u32[]{:S(2)}, u32[]{:S(2)}) collective-permute-start(bf16[2,6,4,4,1,1,128]{6,3,2,1,0,5,4:T(4,128)(2,1)S(1)} %get-tuple-element.155), channel_id=1, source_target_pairs={{0,4},{4,8},{8,12},{1,5},{5,9},{9,13},{2,6},{6,10},{10,14},{3,7},{... | collective-permute-start | bytes 147464 | tf_op jit(solution)/shard_map/ppermute | solution.py:22
  144.3 5.3 %collective-permute-start.19 = (bf16[2,6,4,4,1,1,128]{6,3,2,1,0,5,4:T(4,128)(2,1)S(1)}, bf16[2,6,4,4,1,1,128]{6,3,2,1,0,5,4:T(4,128)(2,1)S(1)}, u32[]{:S(2)}, u32[]{:S(2)}) collective-permute-start(bf16[2,6,4,4,1,1,128]{6,3,2,1,0,5,4:T(4,128)(2,1)S(1)} %get-tuple-element.156), channel_id=1, source_target_pairs={{4,0},{8,4},{12,8},{5,1},{9,5},{13,9},{6,2},{10,6},{14,10},{7,3},{... | collective-permute-start | bytes 147464 | tf_op jit(solution)/shard_map/ppermute | solution.py:23
  151.2 12.3 %collective-permute-start.20 = (bf16[2,6,4,4,1,1,128]{6,3,2,1,0,5,4:T(4,128)(2,1)S(1)}, bf16[2,6,4,4,1,1,128]{6,3,2,1,0,5,4:T(4,128)(2,1)S(1)}, u32[]{:S(2)}, u32[]{:S(2)}) collective-permute-start(bf16[2,6,4,4,1,1,128]{6,3,2,1,0,5,4:T(4,128)(2,1)S(1)} %get-tuple-element.147), channel_id=1, source_target_pairs={{0,16},{1,17},{2,18},{3,19},{4,20},{5,21},{6,22},{7,23},{8,24},{9,... | collective-permute-start | bytes 147464 | tf_op jit(solution)/shard_map/ppermute | solution.py:22
  155.7 7.8 %collective-permute-start.21 = (bf16[2,6,4,4,1,1,128]{6,3,2,1,0,5,4:T(4,128)(2,1)S(1)}, bf16[2,6,4,4,1,1,128]{6,3,2,1,0,5,4:T(4,128)(2,1)S(1)}, u32[]{:S(2)}, u32[]{:S(2)}) collective-permute-start(bf16[2,6,4,4,1,1,128]{6,3,2,1,0,5,4:T(4,128)(2,1)S(1)} %get-tuple-element.148), channel_id=1, source_target_pairs={{16,0},{17,1},{18,2},{19,3},{20,4},{21,5},{22,6},{23,7},{24,8},{25... | collective-permute-start | bytes 147464 | tf_op jit(solution)/shard_map/ppermute | solution.py:23
  157.0 6.5 %collective-permute-start.22 = (bf16[2,6,4,4,1,1,128]{6,3,2,1,0,5,4:T(4,128)(2,1)S(1)}, bf16[2,6,4,4,1,1,128]{6,3,2,1,0,5,4:T(4,128)(2,1)S(1)}, u32[]{:S(2)}, u32[]{:S(2)}) collective-permute-start(bf16[2,6,4,4,1,1,128]{6,3,2,1,0,5,4:T(4,128)(2,1)S(1)} %get-tuple-element.145), channel_id=1, source_target_pairs={{0,4},{4,8},{8,12},{1,5},{5,9},{9,13},{2,6},{6,10},{10,14},{3,7},{... | collective-permute-start | bytes 147464 | tf_op jit(solution)/shard_map/ppermute | solution.py:22
  161.4 3.1 %collective-permute-start.23 = (bf16[2,6,4,4,1,1,128]{6,3,2,1,0,5,4:T(4,128)(2,1)S(1)}, bf16[2,6,4,4,1,1,128]{6,3,2,1,0,5,4:T(4,128)(2,1)S(1)}, u32[]{:S(2)}, u32[]{:S(2)}) collective-permute-start(bf16[2,6,4,4,1,1,128]{6,3,2,1,0,5,4:T(4,128)(2,1)S(1)} %get-tuple-element.146), channel_id=1, source_target_pairs={{4,0},{8,4},{12,8},{5,1},{9,5},{13,9},{6,2},{10,6},{14,10},{7,3},{... | collective-permute-start | bytes 147464 | tf_op jit(solution)/shard_map/ppermute | solution.py:23
  165.1 40.2 %copy-start.8 = (f32[4,4,384]{2,1,0:T(4,128)S(1)}, f32[4,4,384]{2,1,0:T(4,128)}, u32[]{:S(2)}) copy-start(f32[4,4,384]{2,1,0:T(4,128)} %param.35) | copy-start | bytes 73732
  166.0 39.8 %copy-start.6 = (f32[4,4,384]{2,1,0:T(4,128)S(1)}, f32[4,4,384]{2,1,0:T(4,128)}, u32[]{:S(2)}) copy-start(f32[4,4,384]{2,1,0:T(4,128)} %param.34) | copy-start | bytes 73732
where the time goes:
time: 209 us; the launch traced here: 208 us
  starting transfers between devices  70.7 us (34%)
  blocking collectives  56.4 us (27%)
  other arithmetic  28.5 us (14%)
  local copies, waits for them, and re-layouts  21.8 us (10%)
  waiting for transfers between devices  20 us (10%)
  matrix products  7.17 us (3%)
  between operations  2.87 us (1%)
    psum x2, blocking collectives, body(): summed = lax.psum(partial_loads, ('fx', 'fy'))  48.4 us
    ppermute x12, starting transfers between devices, with_halo(): before = lax.ppermute(last, axis, up)  41.3 us
    ppermute x12, starting transfers between devices, with_halo(): after = lax.ppermute(initial, axis, down)  15.5 us
    ppermute x12, waiting for transfers between devices, with_halo(): after = lax.ppermute(initial, axis, down)  13.9 us
    gather x2, local copies, waits for them, and re-layouts, body(): picked = received.reshape(-1)[columns]  10 us
    all_to_all x2, starting transfers between devices, body(): lax.all_to_all(shell_tangent.astype(jnp.bfloat16), 'st', split_axis=0, co...  9.96 us
    scatter-add x2, other arithmetic, body(): jnp.zeros((panels * SDOF * PN,), jnp.float32).at[columns].add(loads)  9.51 us
    all_to_all x1, blocking collectives, body(): lax.all_to_all(summed, 'st', split_axis=1, concat_axis=0, tiled=True)  7.97 us
  transfers between devices with their start and end apart: 27, of which 9 were waited for; matrix products, arithmetic and copies ran while one was open for 13% of the time, Pallas kernels for 0%

commit v1 on v0

--- a/solution.py
+++ b/solution.py
@@ -1,12 +1,21 @@
+import functools
+
 import jax
 import jax.numpy as jnp
 from jax import lax
+from jax.experimental import pallas as pl
+from jax.experimental.pallas import tpu as pltpu
 from jax.sharding import PartitionSpec as P
 
 SDOF = 6
 PN = 64
+NP = 64
 FSWEEP = 3
 ROUNDS = 2
+LANES = 128
+KERNEL_VMEM = 32 * 1024 * 1024
+F32 = jnp.float32
+BF16 = jnp.bfloat16
 
 
 SIGMA = 0.5
@@ -109,7 +118,7 @@
     return states + volumes + penalty[None, :, None, None, None, None] * jumps
 
 
-def body(
+def halo_body(
     tangent_rhs,
     adjoint_rhs,
     jacobians,
@@ -194,6 +203,571 @@
     )
 
 
+def _iota(shape, dim):
+    return lax.broadcasted_iota(jnp.int32, shape, dim)
+
+
+def _flag(cond):
+    return jnp.where(cond, 1.0, 0.0)
+
+
+def _nt(a, b):
+    return lax.dot_general(a, b, (((1,), (1,)), ((), ())), preferred_element_type=F32)
+
+
+def _nn(a, b):
+    return lax.dot_general(a, b, (((1,), (0,)), ((), ())), preferred_element_type=F32)
+
+
+def _tn(a, b):
+    return lax.dot_general(a, b, (((0,), (0,)), ((), ())), preferred_element_type=F32)
+
+
+def _split(x):
+    high = x.astype(BF16)
+    low = (x - high.astype(F32)).astype(BF16)
+    return jnp.concatenate([high, low], axis=0)
+
+
+def _fold(x):
+    half = x.shape[0] // 2
+    return x[:half] + x[half:]
+
+
+def _roll(x, shift):
+    shift = shift % LANES
+    return x if shift == 0 else pltpu.roll(x, shift, 1)
+
+
+class Plan:
+    def __init__(self, nx, ny, ns, nv, span, panels, width):
+        self.nx, self.ny, self.ns, self.nv = nx, ny, ns, nv
+        self.span, self.panels, self.width = span, panels, width
+        self.groups = nx * ny
+        self.own = span // self.groups
+        self.window = LANES // ny
+        self.halo = (self.window - self.own) // 2
+        self.held = panels // ns
+        self.nodes = panels * PN
+        self.tiles = width // LANES
+        self.narrow = LANES // self.groups
+        self.deps = 3 * nv * nv
+        self.granules = 3 * nv + 1
+        self.per = -(-self.granules // 4)
+        self.field_rows = nv * 16
+        self.rows = 2 * self.field_rows + self.per * 8 + 8
+        self.depth = 7 * NP + 32
+        self.slots = ny * LANES
+
+    def rank(self):
+        return lax.axis_index("fx") * self.ny + lax.axis_index("fy")
+
+
+def fits(nx, ny, ns, local_shape, slots, panels, width):
+    members, nv, points, size_x, size_y, span = local_shape
+    groups = nx * ny
+    if members != 1 or (size_x, size_y) != (1, 1) or points != NP or nv > 8 or nv % 2:
+        return False
+    if span != LANES or slots != LANES or span % groups or LANES % ny or LANES % groups:
+        return False
+    own, window = span // groups, LANES // ny
+    if window * 4 != LANES or (window - own) % 2 or (window - own) // 2 < ROUNDS * FSWEEP - 1:
+        return False
+    if own * 8 != LANES or width != SDOF * PN or width % LANES or SDOF > 8:
+        return False
+    held = panels // ns
+    if panels % ns or panels != 16 or groups % held or ns > 4:
+        return False
+    return (held + 1) * (width // LANES) <= 16 and 8 % held == 0
+
+
+def shell_solve_rows(plan, rhs, inverse_ref):
+    rows = rhs.shape[0]
+    rounded = rhs.astype(BF16)
+    member = _iota((rows, plan.width), 0) % plan.held
+    result = jnp.zeros((rows, plan.width), F32)
+    for panel in range(plan.held):
+        result = jnp.where(member == panel, _nt(rounded, inverse_ref[panel]), result)
+    return result
+
+
+def stacked(ref, count):
+    return jnp.concatenate([ref[d] for d in range(count)], axis=0)
+
+
+def pack_kernel(plan, trhs, arhs, jac, second, elem, node, weight, count, out, scr):
+    nv, window = plan.nv, plan.window
+    lane = _iota((1, LANES), 1)
+    masks = []
+    for dest in range(plan.groups):
+        start = plan.own * dest - plan.halo
+        row = []
+        for k in range(4):
+            z = start + lane % window
+            row.append(_flag((lane // window == k) & (z >= 0) & (z < plan.span)))
+        masks.append(row)
+
+    def window_of(parts, dest, dtype):
+        start = plan.own * dest - plan.halo
+        total = None
+        for k in range(4):
+            term = _roll(parts[k], window * k - start) * masks[dest][k].astype(dtype)
+            total = term if total is None else total + term
+        return total
+
+    for f, ref in enumerate((trhs, arhs)):
+        for a in range(nv):
+            parts = [ref[a, pl.ds(16 * k, 16), :] for k in range(4)]
+            for dest in range(plan.groups):
+                out[dest, pl.ds((f * nv + a) * 16, 16), :] = window_of(parts, dest, BF16)
+
+    scr[...] = jnp.zeros(scr.shape, F32)
+    for k in range(3):
+        for a in range(nv):
+            scr[k * nv + a, 0:nv, :] = jac[k, a].astype(F32)
+    for a in range(nv):
+        scr[3 * nv, a : a + 1, :] = second[a]
+    quarter = [
+        scr[pl.ds(plan.per * k, plan.per)].reshape(plan.per * 8, LANES) for k in range(4)
+    ]
+    live = _flag(lane < count[0])
+    scaled = weight[...] * live
+    coarse = scaled.astype(BF16).astype(F32)
+    panel = node[...] // PN
+    upper = jnp.where(panel >= 8, 1, 0)
+    table = [
+        elem[...].astype(F32),
+        (panel - 8 * upper).astype(F32),
+        (node[...] - panel * PN + PN * upper).astype(F32),
+        coarse,
+        scaled - coarse,
+        jnp.zeros((3, LANES), F32),
+    ]
+    table = jnp.concatenate(table, axis=0)
+    for dest in range(plan.groups):
+        block = jnp.concatenate([window_of(quarter, dest, F32), table], axis=0)
+        first = 2 * plan.field_rows
+        out[dest, pl.ds(first, plan.rows - first), :] = block.astype(BF16)
+
+
+def coefficients(plan, penalty, coef, rank):
+    point = _iota((NP, LANES), 0)
+    ends = [point // 16, (point // 4) % 4, point % 4]
+    faces = sum(_flag((e == 0) | (e == 3)) for e in ends)
+    lane = _iota((1, LANES), 1)
+    z = plan.own * rank - plan.halo + lane % plan.window
+    inside = _flag((z >= 0) & (z < plan.span))
+    rows = []
+    for a in range(plan.nv):
+        coef[a] = 0.5 - (0.5 * penalty[a]) * faces
+        rows.append((penalty[a] * inside).astype(BF16))
+    return rows
+
+
+def sweeps(plan, count, state, rounded, source, table, matrix, transposed, coef, rows):
+    nv, nx, window = plan.nv, plan.nx, plan.window
+    lane = _iota((1, LANES), 1)
+    not_last = _flag(lane < LANES - window).astype(BF16)
+    not_first = _flag(lane >= window).astype(BF16)
+    for s in range(count):
+        now, later = s % 2, (s + 1) % 2
+        for h in range(nx):
+            own = [rounded[now, h, b].reshape(4, 16, LANES) for b in range(nv)]
+            for a0 in range(0, nv, 2):
+                stacks = []
+                for a in (a0, a0 + 1):
+                    parts = []
+                    for k in range(3):
+                        total = None
+                        for b in range(nv):
+                            r = (k * nv + b) * nv + a if transposed else (k * nv + a) * nv + b
+                            term = own[b] * table[h, r][None]
+                            total = term if total is None else total + term
+                        parts.append(total.reshape(NP, LANES))
+                    scaled = own[a].reshape(NP, LANES) * rows[a]
+                    parts.append(_roll(scaled, -window) * not_last)
+                    parts.append(_roll(scaled, window) * not_first)
+                    parts.append(_roll(scaled, -1))
+                    parts.append(_roll(scaled, 1))
+                    none = jnp.zeros((16, LANES), BF16)
+                    above = rounded[now, h + 1, a, 0:16, :] * rows[a] if h + 1 < nx else none
+                    below = rounded[now, h - 1, a, 48:64, :] * rows[a] if h > 0 else none
+                    parts += [above, below]
+                    stacks.append(jnp.concatenate(parts, axis=0))
+                product = _nn(matrix, jnp.concatenate(stacks, axis=1))
+                for i, a in enumerate((a0, a0 + 1)):
+                    value = coef[a] * state[h, a] + source[h, a]
+                    value = value + product[:, LANES * i : LANES * (i + 1)]
+                    state[h, a] = value
+                    rounded[later, h, a] = value.astype(BF16)
+    return count % 2
+
+
+def couple_rows(coupling):
+    wide = coupling[...].astype(F32)
+    pad = jnp.zeros((8 - SDOF, wide.shape[1]), F32)
+    return jnp.concatenate([wide, pad], axis=0).astype(BF16)
+
+
+def node_loads(plan, couple, values, incidence, places, weights, scr):
+    lane = _iota((1, LANES), 1)
+    place = lane % plan.window
+    owned = _flag((place >= plan.halo) & (place < plan.halo + plan.own))
+    picked = []
+    for h in range(plan.nx):
+        flow = _nn(couple, values[h]) * owned
+        picked.append(_fold(_nn(_split(flow), places[h])) * weights[h])
+    nodal = _fold(_nt(_split(jnp.concatenate(picked, axis=1)), incidence[...]))
+    for j in range(8):
+        scr[:, j, :] = nodal[:, LANES * j : LANES * (j + 1)]
+    left = _iota((8, LANES), 1) < PN
+    low, high = [], []
+    for t in range(plan.tiles):
+        even, odd = scr[2 * t], scr[2 * t + 1]
+        low.append(jnp.where(left, even, _roll(odd, PN)))
+        high.append(jnp.where(left, _roll(even, PN), odd))
+    return low, high
+
+
+def write_exchange(plan, low, high, solved, solved_scr, out, rank):
+    solved_scr[...] = solved
+    mine = rank // (plan.groups // plan.held)
+    for dest in range(plan.ns):
+        rows = []
+        first = dest * plan.held
+        for t in range(plan.tiles):
+            part = low[t] if first < 8 else high[t]
+            rows.append(part[first % 8 : first % 8 + plan.held])
+        line = solved_scr[pl.ds(dest * plan.held + mine, 1), :]
+        for t in range(plan.tiles):
+            rows.append(line[:, LANES * t : LANES * (t + 1)])
+        used = (plan.held + 1) * plan.tiles
+        if used < 16:
+            rows.append(jnp.zeros((16 - used, LANES), F32))
+        block = jnp.concatenate(rows, axis=0).astype(BF16)
+        for g in range(plan.groups):
+            out[g * plan.ns + dest] = block
+
+
+def read_loads(plan, received):
+    totals = []
+    for d in range(plan.ns):
+        total = received[d].astype(F32)
+        for g in range(1, plan.groups):
+            total = total + received[g * plan.ns + d].astype(F32)
+        totals.append(total)
+    tiles = []
+    for t in range(plan.tiles):
+        rows = [x[plan.held * t : plan.held * (t + 1)] for x in totals]
+        tiles.append(jnp.concatenate(rows, axis=0))
+    return jnp.concatenate(tiles, axis=1)
+
+
+def push_force(plan, received, incidence, places, weights, couple, rhs, shell_scr, scr, source):
+    span = plan.groups // plan.held
+    for s in range(plan.ns):
+        for panel in range(plan.held):
+            block = received[panel * span * plan.ns + s].astype(F32)
+            q = s * plan.held + panel
+            for t in range(plan.tiles):
+                r = plan.held * plan.tiles + t
+                shell_scr[q : q + 1, LANES * t : LANES * (t + 1)] = block[r : r + 1]
+    left = _iota((8, LANES), 1) < PN
+    for t in range(plan.tiles):
+        upper = shell_scr[0:8, LANES * t : LANES * (t + 1)]
+        lower = shell_scr[8:16, LANES * t : LANES * (t + 1)]
+        scr[2 * t] = jnp.where(left, upper, _roll(lower, PN))
+        scr[2 * t + 1] = jnp.where(left, _roll(upper, PN), lower)
+    for c in range(2 * plan.tiles, 8):
+        scr[c] = jnp.zeros((8, LANES), F32)
+    nodal = jnp.concatenate([scr[:, j, :] for j in range(8)], axis=1).astype(BF16)
+    picked = _nn(nodal, incidence[...])
+    twice = jnp.concatenate([couple, couple], axis=0)
+    for h in range(plan.nx):
+        part = picked[:, plan.slots * h : plan.slots * (h + 1)] * weights[h]
+        dofs = _fold(_nt(_split(part), places[h]))
+        push = _tn(twice, _split(dofs))
+        for a in range(plan.nv):
+            value = rhs[0, h, a].astype(F32) - push[NP * a : NP * (a + 1)]
+            source[h, a] = 0.5 * value
+
+
+def first_kernel(
+    plan, received, deriv, penalty, coupling, load, inverse,
+    adjoint, rhs, table, second, incidence, places, weights, forward, backward, out,
+    source, rounded, coef, scr, solved_scr,
+):
+    nv, window, nx, ny = plan.nv, plan.window, plan.nx, plan.ny
+    rank = plan.rank()
+    lane = _iota((1, LANES), 1)
+    group = [_flag(lane // window == y) for y in range(ny)]
+
+    def regroup(parts, k, dtype):
+        total = None
+        for y in range(ny):
+            term = _roll(parts[y], window * (y - k)) * group[y].astype(dtype)
+            total = term if total is None else total + term
+        return total
+
+    for h in range(nx):
+        for f in range(2):
+            for a in range(nv):
+                first = (f * nv + a) * 16
+                parts = [received[h * ny + y, pl.ds(first, 16), :] for y in range(ny)]
+                for k in range(4):
+                    rhs[f, h, a, pl.ds(16 * k, 16), :] = regroup(parts, k, BF16)
+        first = 2 * plan.field_rows
+        tails = [
+            received[h * ny + y, pl.ds(first, plan.rows - first), :].astype(F32)
+            for y in range(ny)
+        ]
+        for k in range(4):
+            block = regroup([x[: plan.per * 8] for x in tails], k, F32)
+            for i in range(plan.per):
+                granule = k * plan.per + i
+                part = block[8 * i : 8 * (i + 1)]
+                if granule < 3 * nv:
+                    for b in range(nv):
+                        row = jnp.broadcast_to(part[b : b + 1], (16, LANES))
+                        table[h, granule * nv + b] = row.astype(BF16)
+                elif granule == 3 * nv:
+                    second[h] = part
+        info = [x[plan.per * 8 :] for x in tails]
+        place = _iota((LANES, LANES), 0)
+        spot = _iota((plan.nodes, LANES), 0)
+        for y in range(ny):
+            at = info[y]
+            where = (at[0:1] - (plan.own * rank - plan.halo).astype(F32)).astype(jnp.int32)
+            within = (where >= 0) & (where < window)
+            target = jnp.where(within, where + y * window, -1)
+            columns = pl.ds(LANES * y, LANES)
+            places[h, :, columns] = _flag(place == target).astype(BF16)
+            weights[h, :, columns] = at[3:4] + at[4:5]
+            position = (at[1:2] * LANES + at[2:3]).astype(jnp.int32)
+            columns = pl.ds(plan.slots * h + LANES * y, LANES)
+            incidence[:, columns] = _flag(spot == position).astype(BF16)
+
+    p, c = _iota((NP, plan.depth), 0), _iota((NP, plan.depth), 1)
+    j, l = (p // 4) % 4, p % 4
+
+    def block(n, ok, shift):
+        return ok & (c - (3 + n) * NP == p + shift)
+
+    links = block(0, j == 3, -12) | block(1, j == 0, 12)
+    links = links | block(2, l == 3, -3) | block(3, l == 0, 3)
+    links = links | ((p >= 48) & (c - 7 * NP == p - 48))
+    links = links | ((p < 16) & (c - 7 * NP - 16 == p))
+    base = (0.5 * _flag(links)).astype(BF16)
+    forward[...] = base
+    backward[...] = base
+    for k in range(3):
+        part = -0.5 * deriv[k].astype(F32)
+        forward[:, NP * k : NP * (k + 1)] = part.astype(BF16)
+        backward[:, NP * k : NP * (k + 1)] = part.T.astype(BF16)
+
+    rows = coefficients(plan, penalty, coef, rank)
+    for h in range(nx):
+        for a in range(nv):
+            value = 0.5 * rhs[1, h, a].astype(F32)
+            source[h, a] = value
+            adjoint[h, a] = value
+            rounded[0, h, a] = value.astype(BF16)
+    last = sweeps(
+        plan, FSWEEP - 1, adjoint, rounded, source, table, backward[...], True, coef, rows
+    )
+    values = [rounded[last, h].reshape(nv * NP, LANES) for h in range(nx)]
+    low, high = node_loads(plan, couple_rows(coupling), values, incidence, places, weights, scr)
+    solved = shell_solve_rows(plan, stacked(load, plan.ns), inverse)
+    write_exchange(plan, low, high, solved, solved_scr, out, rank)
+
+
+def second_kernel(
+    plan, received, penalty, coupling, load, shell_rhs, inverse, adjoint_in, rhs, table, second,
+    incidence, places, weights, forward, backward,
+    tangent, adjoint_rounded, out,
+    adjoint, source, rounded, coef, scr, solved_scr, shell_scr,
+):
+    nv, nx = plan.nv, plan.nx
+    rank = plan.rank()
+    rows = coefficients(plan, penalty, coef, rank)
+    couple = couple_rows(coupling)
+    push_force(
+        plan, received, incidence, places, weights, couple, rhs, shell_scr, scr, source
+    )
+    for h in range(nx):
+        for a in range(nv):
+            value = source[h, a]
+            tangent[h, a] = value
+            rounded[0, h, a] = value.astype(BF16)
+    sweeps(plan, FSWEEP - 1, tangent, rounded, source, table, forward[...], False, coef, rows)
+    for h in range(nx):
+        for a in range(nv):
+            extra = second[h, a : a + 1, :] * tangent[h, a]
+            source[h, a] = 0.5 * (rhs[1, h, a].astype(F32) + extra)
+            value = adjoint_in[h, a]
+            adjoint[h, a] = value
+            rounded[0, h, a] = value.astype(BF16)
+    last = sweeps(
+        plan, FSWEEP, adjoint, rounded, source, table, backward[...], True, coef, rows
+    )
+    adjoint_rounded[...] = rounded[last]
+    values = [rounded[last, h].reshape(nv * NP, LANES) for h in range(nx)]
+    low, high = node_loads(plan, couple, values, incidence, places, weights, scr)
+    shell = stacked(shell_rhs, plan.ns) - read_loads(plan, received)
+    shell = shell_solve_rows(plan, shell, inverse)
+    solved = shell_solve_rows(plan, stacked(load, plan.ns) + shell, inverse)
+    write_exchange(plan, low, high, solved, solved_scr, out, rank)
+
+
+def third_kernel(
+    plan, received, penalty, coupling, load, shell_rhs, inverse, tangent_in, adjoint_rounded,
+    rhs, table, incidence, places, weights, forward,
+    out, shell_tangent, shell_adjoint,
+    tangent, source, rounded, coef, scr, shell_scr,
+):
+    nv, nx, ny, ns = plan.nv, plan.nx, plan.ny, plan.ns
+    rank = plan.rank()
+    rows = coefficients(plan, penalty, coef, rank)
+    couple = couple_rows(coupling)
+    push_force(
+        plan, received, incidence, places, weights, couple, rhs, shell_scr, scr, source
+    )
+    for h in range(nx):
+        for a in range(nv):
+            value = tangent_in[h, a]
+            tangent[h, a] = value
+            rounded[0, h, a] = value.astype(BF16)
+    last = sweeps(
+        plan, FSWEEP, tangent, rounded, source, table, forward[...], False, coef, rows
+    )
+    lane = _iota((1, LANES), 1)
+    narrow = plan.narrow
+    group = [_flag(lane // narrow == n).astype(BF16) for n in range(8)]
+    for h in range(nx):
+        for a in range(nv):
+            parts = []
+            for ref in (rounded.at[last], adjoint_rounded):
+                parts += [ref[h, a, pl.ds(16 * i, 16), :] for i in range(4)]
+            for y in range(ny):
+                total = None
+                for n in range(8):
+                    shift = narrow * n - plan.window * y - plan.halo
+                    term = _roll(parts[n], shift) * group[n]
+                    total = term if total is None else total + term
+                out[h * ny + y, pl.ds(16 * a, 16), :] = total
+    shell = stacked(shell_rhs, ns) - read_loads(plan, received)
+    shell = shell_solve_rows(plan, shell, inverse)
+    solved = shell_solve_rows(plan, stacked(load, ns) + shell, inverse)
+    for d in range(ns):
+        shell_adjoint[d] = shell[plan.held * d : plan.held * (d + 1)]
+        shell_tangent[d] = solved[plan.held * d : plan.held * (d + 1)]
+
+
+def last_kernel(plan, received, tangent, adjoint):
+    lane = _iota((1, LANES), 1)
+    narrow = plan.narrow
+    group = [_flag(lane // narrow == g).astype(BF16) for g in range(plan.groups)]
+    for a in range(plan.nv):
+        parts = [received[g, pl.ds(16 * a, 16), :] for g in range(plan.groups)]
+        for f, ref in enumerate((tangent, adjoint)):
+            for i in range(4):
+                total = None
+                for g in range(plan.groups):
+                    term = _roll(parts[g], narrow * (g - 4 * f - i)) * group[g]
+                    total = term if total is None else total + term
+                ref[a, pl.ds(16 * i, 16), :] = total
+
+
+def call(kernel, plan, out_shape, scratch, scalars, args):
+    vmem = pl.BlockSpec(memory_space=pltpu.VMEM)
+    smem = pl.BlockSpec(memory_space=pltpu.SMEM)
+    specs = [smem if i in scalars else vmem for i in range(len(args))]
+    return pl.pallas_call(
+        functools.partial(kernel, plan),
+        out_shape=[jax.ShapeDtypeStruct(s, d) for s, d in out_shape],
+        in_specs=specs,
+        out_specs=[vmem] * len(out_shape),
+        scratch_shapes=[pltpu.VMEM(s, d) for s, d in scratch],
+        compiler_params=pltpu.CompilerParams(vmem_limit_bytes=KERNEL_VMEM),
+    )(*args)
+
+
+def slab_body(
+    plan, tangent_rhs, adjoint_rhs, jacobians, deriv, penalty, second_order, coupling,
+    shell_inverse, shell_load, shell_adjoint_rhs, iface_elem, iface_node, iface_weight,
+    iface_count,
+):
+    nv, nx, ny, ns, groups = plan.nv, plan.nx, plan.ny, plan.ns, plan.groups
+    flow, everyone = ("fx", "fy"), ("fx", "fy", "st")
+    state = (nx, nv, NP, LANES)
+    rounded = ((2,) + state, BF16)
+    coef = ((nv, NP, LANES), F32)
+    scr = ((8, 8, LANES), F32)
+    shell_rows = ((plan.panels, plan.width), F32)
+    solved_rows = ((ns * plan.held, plan.width), F32)
+    trhs = tangent_rhs.reshape(nv, NP, LANES)
+    arhs = adjoint_rhs.reshape(nv, NP, LANES)
+    jac = jacobians.reshape(3, nv, nv, LANES)
+    second_rows = second_order.reshape(nv, 1, LANES)
+
+    (packed,) = call(
+        pack_kernel, plan, [((groups, plan.rows, LANES), BF16)],
+        [((4 * plan.per, 8, LANES), F32)], (7,),
+        (trhs, arhs, jac, second_rows, iface_elem, iface_node, iface_weight, iface_count),
+    )
+    slab = lax.all_to_all(packed, flow, split_axis=0, concat_axis=0, tiled=True)
+    exchange = ((groups * ns, 16, LANES), BF16)
+    adjoint, rhs, table, second, incidence, places, weights, forward, backward, sent = call(
+        first_kernel, plan,
+        [
+            (state, F32), ((2,) + state, BF16), ((nx, plan.deps, 16, LANES), BF16),
+            ((nx, 8, LANES), F32), ((plan.nodes, nx * plan.slots), BF16),
+            ((nx, LANES, plan.slots), BF16), ((nx, 1, plan.slots), F32),
+            ((NP, plan.depth), BF16), ((NP, plan.depth), BF16), exchange,
+        ],
+        [(state, F32), rounded, coef, scr, solved_rows], (2,),
+        (slab, deriv, penalty, coupling, shell_load, shell_inverse),
+    )
+    received = lax.all_to_all(sent, everyone, split_axis=0, concat_axis=0, tiled=True)
+    tangent, adjoint_rounded, sent = call(
+        second_kernel, plan, [(state, F32), (state, BF16), exchange],
+        [(state, F32), (state, F32), rounded, coef, scr, solved_rows, shell_rows], (1,),
+        (
+            received, penalty, coupling, shell_load, shell_adjoint_rhs, shell_inverse, adjoint,
+            rhs, table, second, incidence, places, weights, forward, backward,
+        ),
+    )
+    received = lax.all_to_all(sent, everyone, split_axis=0, concat_axis=0, tiled=True)
+    shell_shape = (shell_load.shape, F32)
+    sent, shell_tangent, shell_adjoint = call(
+        third_kernel, plan,
+        [((groups, plan.field_rows, LANES), BF16), shell_shape, shell_shape],
+        [(state, F32), (state, F32), rounded, coef, scr, shell_rows], (1,),
+        (
+            received, penalty, coupling, shell_load, shell_adjoint_rhs, shell_inverse, tangent,
+            adjoint_rounded, rhs, table, incidence, places, weights, forward,
+        ),
+    )
+    received = lax.all_to_all(sent, flow, split_axis=0, concat_axis=0, tiled=True)
+    tangent, adjoint = call(
+        last_kernel, plan, [((nv, NP, LANES), BF16)] * 2, [], (), (received,)
+    )
+    return (
+        tangent.reshape(tangent_rhs.shape), adjoint.reshape(adjoint_rhs.shape),
+        shell_tangent, shell_adjoint,
+    )
+
+
+def body(*args):
+    tangent_rhs, shell_inverse, shell_load, iface_elem = args[0], args[7], args[8], args[10]
+    nx, ny, ns = (lax.axis_size(name) for name in ("fx", "fy", "st"))
+    panels, width = shell_inverse.shape[0] * ns, shell_load.shape[2]
+    if fits(nx, ny, ns, tangent_rhs.shape, iface_elem.shape[1], panels, width):
+        plan = Plan(nx, ny, ns, tangent_rhs.shape[1], tangent_rhs.shape[5], panels, width)
+        return slab_body(plan, *args)
+    return halo_body(*args)
+
+
 def solution(mesh):
     in_specs = (
         P("st", None, None, "fx", "fy", None),

time: 209 us -> 71.9 us (0.34)
  starting transfers between devices: 70.7 us -> 0 us
  other arithmetic: 28.5 us -> 0 us
  waiting for transfers between devices: 20 us -> 0 us
  Pallas kernels: 0 us -> 16.6 us
  local copies, waits for them, and re-layouts: 21.8 us -> 8.09 us
  blocking collectives: 56.4 us -> 45.2 us
  matrix products: 7.17 us -> 0 us
    ppermute x24 -> x0, starting transfers between devices: 56.8 us -> none  [the longest x12 41.3 us: with_halo(): before = lax.ppermute(last, axis, up)]
    psum x2 -> x0, blocking collectives: 48.4 us -> none  [body(): summed = lax.psum(partial_loads, ('fx', 'fy'))]
    all_to_all x1 -> x4, blocking collectives: 7.97 us -> 45.2 us  [the longest x2 22.2 us: slab_body(): lax.all_to_all(sent, everyone, split_axis=0, concat_axis=0, tiled=True)]
    pallas_call x0 -> x5, Pallas kernels: none -> 16.6 us  [call(): pl.pallas_call(functools.partial(kernel, plan), out_shape=[jax.ShapeDtype...]
    ppermute x24 -> x0, waiting for transfers between devices: 14.5 us -> none  [the longest x12 13.9 us: with_halo(): after = lax.ppermute(initial, axis, down)]
    gather x16 -> x0, local copies, waits for them, and re-layouts: 13.9 us -> none  [the longest x2 10 us: body(): picked = received.reshape(-1)[columns]]
    all_to_all x3 -> x0, starting transfers between devices: 13.9 us -> none  [the longest x2 9.96 us: body(): lax.all_to_all(shell_tangent.astype(jnp.bfloat16), 'st', split_axis=0, co...]
    scatter-add x4 -> x0, other arithmetic: 12.4 us -> none  [the longest x2 9.51 us: body(): jnp.zeros((panels * SDOF * PN,), jnp.float32).at[columns].add(loads)]
  transfers between devices with their start and end apart: 27 -> 0, of which waited for: 9 -> 0; matrix products, arithmetic and copies ran while one was open for 13% -> 0% of each run, Pallas kernels for 0% -> 0%
where the time goes in v1:
time: 71.9 us; the launch traced here: 71.3 us
  blocking collectives  45.2 us (63%)
  Pallas kernels  16.6 us (23%)
  local copies, waits for them, and re-layouts  8.09 us (11%)
  between operations  1.44 us (2%)
    all_to_all x2, blocking collectives, slab_body(): lax.all_to_all(sent, everyone, split_axis=0, concat_axis=0, tiled=True)  22.2 us
    pallas_call x5, Pallas kernels, call(): pl.pallas_call(functools.partial(kernel, plan), out_shape=[jax.ShapeDtype...  16.6 us
    all_to_all x1, blocking collectives, slab_body(): slab = lax.all_to_all(packed, flow, split_axis=0, concat_axis=0, tiled=True)  14.4 us
    all_to_all x1, blocking collectives, slab_body(): lax.all_to_all(sent, flow, split_axis=0, concat_axis=0, tiled=True)  8.59 us
    unnamed x30, local copies, waits for them, and re-layouts  8.09 us

profile of v1, /device:TPU:0, one launch (start us, length us, event | category | flops | bytes accessed | tf_op | source)
XLA Modules:
  0.0 71.3 jit_solution(11208921227190379713)
XLA Ops:
  0.6 0.0 copy-start
  0.6 0.0 copy-start.3
  1.4 0.0 copy-start.4
  1.4 0.9 %copy-done.4 = bf16[1,6,64,1,1,128]{5,2,4,3,1,0:T(8,128)(2,1)S(1)} copy-done((bf16[1,6,64,1,1,128]{5,2,4,3,1,0:T(8,128)(2,1)S(1)}, bf16[1,6,64,1,1,128]{5,2,4,3,1,0:T(8,128)(2,1)}, u32[]{:S(2)}) %copy-start.4) | copy-done | bytes 98328
  2.3 0.0 copy-start.5
  2.3 0.9 %copy-done.5 = bf16[1,6,64,1,1,128]{5,2,4,3,1,0:T(8,128)(2,1)S(1)} copy-done((bf16[1,6,64,1,1,128]{5,2,4,3,1,0:T(8,128)(2,1)S(1)}, bf16[1,6,64,1,1,128]{5,2,4,3,1,0:T(8,128)(2,1)}, u32[]{:S(2)}) %copy-start.5) | copy-done | bytes 98328
  3.2 0.0 copy-start.8
  3.2 0.8 %copy-done.8 = bf16[3,6,6,1,1,128]{5,2,4,3,1,0:T(8,128)(2,1)S(1)} copy-done((bf16[3,6,6,1,1,128]{5,2,4,3,1,0:T(8,128)(2,1)S(1)}, bf16[3,6,6,1,1,128]{5,2,4,3,1,0:T(8,128)(2,1)}, u32[]{:S(2)}) %copy-start.8) | copy-done | bytes 27672
  3.9 0.0 copy-start.11
  4.0 0.7 copy-done.11
  4.6 0.0 copy-start.12
  4.6 0.7 copy-done.12
  5.3 0.0 copy-start.13
  5.3 0.7 copy-done.13
  5.9 0.0 copy-start.14
  5.9 0.7 copy-done.14
  6.6 0.0 copy-start.10
  6.6 0.6 shard_map.165
  7.2 14.4 %all_to_all.20.received = bf16[8,240,128]{2,1,0:T(8,128)(2,1)S(1)} all-to-all(bf16[8,240,128]{2,1,0:T(8,128)(2,1)S(1)} %shard_map.165), channel_id=1, replica_groups=mesh['fx'=2,'fy'=4,'st'=4] {'fx','fy'}, dimensions={0} | all-to-all | bytes 983040 | tf_op jit(solution)/shard_map/all_to_all | solution.py:718
  21.5 0.0 copy-done
  21.5 0.0 copy-start.1
  21.5 0.7 %copy-done.1 = f32[4,4,384]{2,1,0:T(4,128)S(1)} copy-done((f32[4,4,384]{2,1,0:T(4,128)S(1)}, f32[4,4,384]{2,1,0:T(4,128)}, u32[]{:S(2)}) %copy-start.1) | copy-done | bytes 24600
  22.3 0.0 copy-start.6
  22.3 0.7 copy-done.6
  23.0 0.0 copy-start.7
  23.0 0.8 %copy-done.7 = bf16[3,64,64]{2,1,0:T(8,128)(2,1)S(1)} copy-done((bf16[3,64,64]{2,1,0:T(8,128)(2,1)S(1)}, bf16[3,64,64]{2,1,0:T(8,128)(2,1)}, u32[]{:S(2)}) %copy-start.7) | copy-done | bytes 24600
  23.8 0.0 copy-start.9
  23.8 0.7 copy-done.9
  24.4 3.7 %shard_map.166 = (f32[2,6,64,128]{3,2,1,0:T(8,128)S(1)}, bf16[2,2,6,64,128]{4,3,2,1,0:T(8,128)(2,1)S(1)}, bf16[2,108,16,128]{3,2,1,0:T(8,128)(2,1)S(1)}, f32[2,8...) custom-call(bf16[8,240,128]{2,1,0:T(8,128)(2,1)S(1)} %all_to_all.20., ...), custom_call_target="tpu_custom_call" | custom-call | tf_op jit(solution)/shard_map/pallas_call | solution.py:685
  28.1 12.2 %all_to_all.21.received = bf16[32,16,128]{2,1,0:T(8,128)(2,1)S(1)} all-to-all(bf16[32,16,128]{2,1,0:T(8,128)(2,1)S(1)} %get-tuple-element.22), channel_id=1, replica_groups=mesh['fx'=2,'fy'=4,'st'=4] {'fx','fy','st'}, dimensions={0} | all-to-all | bytes 262144 | tf_op jit(solution)/shard_map/all_to_all | solution.py:731
  40.3 0.0 copy-done.3
  40.3 0.0 copy-done.10
  40.3 0.0 copy-start.2
  40.3 6.4 %shard_map.167 = (f32[2,6,64,128]{3,2,1,0:T(8,128)S(1)}, bf16[2,6,64,128]{3,2,1,0:T(8,128)(2,1)S(1)}, bf16[32,16,128]{2,1,0:T(8,128)(2,1)S(1)}) custom-call(bf16[32,16,128]{2,1,0:T(8,128)(2,1)S(1)} %all_to_all.21.received, f32[6]{0:T(128)S(1)} %copy-done.10, bf16[6,384]{1,0:T(8,128)(2,1)S(1)} %copy-done.6, f32[4,4,384]{2,1,0:T(4,128)S(1)} %copy-done.1, ...), custom_call_target="tpu_custom_call" | custom-call | tf_op jit(solution)/shard_map/pallas_call | solution.py:685
  46.7 10.1 %all_to_all.22.received = bf16[32,16,128]{2,1,0:T(8,128)(2,1)S(1)} all-to-all(bf16[32,16,128]{2,1,0:T(8,128)(2,1)S(1)} %get-tuple-element.32), channel_id=1, replica_groups=mesh['fx'=2,'fy'=4,'st'=4] {'fx','fy','st'}, dimensions={0} | all-to-all | bytes 262144 | tf_op jit(solution)/shard_map/all_to_all | solution.py:740
  56.8 0.0 copy-done.2
  56.8 4.8 %shard_map.168 = (bf16[8,96,128]{2,1,0:T(8,128)(2,1)S(1)}, f32[4,4,384]{2,1,0:T(4,128)}, f32[4,4,384]{2,1,0:T(4,128)}) custom-call(bf16[32,16,128]{2,1,0:T(8,128)(2,1)S(1)} %all_to_all.22.received, f32[6]{0:T(128)S(1)} %copy-done.10, bf16[6,384]{1,0:T(8,128)(2,1)S(1)} %copy-done.6, f32[4,4,384]{2,1,0:T(4,128)S(1)} %copy-done.2, f32[4,4,384]{2,1,0:T(4,128)S(1)} %copy-done.3, ...), custom_call_target="tpu_custom_call" | custom-call | tf_op jit(solution)/shard_map/pallas_call | solution.py:685
  61.7 8.6 %all_to_all.23.received = bf16[8,96,128]{2,1,0:T(8,128)(2,1)S(1)} all-to-all(bf16[8,96,128]{2,1,0:T(8,128)(2,1)S(1)} %get-tuple-element.35), channel_id=1, replica_groups=mesh['fx'=2,'fy'=4,'st'=4] {'fx','fy'}, dimensions={0} | all-to-all | bytes 393216 | tf_op jit(solution)/shard_map/all_to_all | solution.py:751
  70.2 1.1 %shard_map.169 = (bf16[6,64,128]{2,1,0:T(8,128)(2,1)}, bf16[6,64,128]{2,1,0:T(8,128)(2,1)}) custom-call(bf16[8,96,128]{2,1,0:T(8,128)(2,1)S(1)} %all_to_all.23.received), custom_call_target="tpu_custom_call" | custom-call | tf_op jit(solution)/shard_map/pallas_call | solution.py:685
Async XLA Ops:
  0.6 20.9 %copy-start = (bf16[4,384,384]{2,1,0:T(8,128)(2,1)S(1)}, bf16[4,384,384]{2,1,0:T(8,128)(2,1)}, u32[]{:S(2)}) copy-start(bf16[4,384,384]{2,1,0:T(8,128)(2,1)} %inverse.5) | copy-start | bytes 3538948
  0.6 39.6 %copy-start.3 = (f32[4,4,384]{2,1,0:T(4,128)S(1)}, f32[4,4,384]{2,1,0:T(4,128)}, u32[]{:S(2)}) copy-start(f32[4,4,384]{2,1,0:T(4,128)} %shell_rhs.3) | copy-start | bytes 73732
  1.4 0.9 %copy-start.4 = (bf16[1,6,64,1,1,128]{5,2,4,3,1,0:T(8,128)(2,1)S(1)}, bf16[1,6,64,1,1,128]{5,2,4,3,1,0:T(8,128)(2,1)}, u32[]{:S(2)}) copy-start(bf16[1,6,64,1,1,128]{5,2,4,3,1,0:T(8,128)(2,1)} %param.14) | copy-start | bytes 294916
  2.3 0.9 %copy-start.5 = (bf16[1,6,64,1,1,128]{5,2,4,3,1,0:T(8,128)(2,1)S(1)}, bf16[1,6,64,1,1,128]{5,2,4,3,1,0:T(8,128)(2,1)}, u32[]{:S(2)}) copy-start(bf16[1,6,64,1,1,128]{5,2,4,3,1,0:T(8,128)(2,1)} %param.15) | copy-start | bytes 294916
  3.2 0.8 %copy-start.8 = (bf16[3,6,6,1,1,128]{5,2,4,3,1,0:T(8,128)(2,1)S(1)}, bf16[3,6,6,1,1,128]{5,2,4,3,1,0:T(8,128)(2,1)}, u32[]{:S(2)}) copy-start(bf16[3,6,6,1,1,128]{5,2,4,3,1,0:T(8,128)(2,1)} %param.16) | copy-start | bytes 82948
  3.9 0.7 copy-start.11
  4.6 0.7 copy-start.12
  5.3 0.7 copy-start.13
  5.9 0.7 copy-start.14
  6.6 33.7 %copy-start.10 = (f32[6]{0:T(128)S(1)}, f32[6]{0:T(128)}, u32[]{:S(2)}) copy-start(f32[6]{0:T(128)} %penalty.5) | copy-start | bytes 76
  21.5 0.7 %copy-start.1 = (f32[4,4,384]{2,1,0:T(4,128)S(1)}, f32[4,4,384]{2,1,0:T(4,128)}, u32[]{:S(2)}) copy-start(f32[4,4,384]{2,1,0:T(4,128)} %load.5) | copy-start | bytes 73732
  22.3 0.7 copy-start.6
  23.0 0.8 %copy-start.7 = (bf16[3,64,64]{2,1,0:T(8,128)(2,1)S(1)}, bf16[3,64,64]{2,1,0:T(8,128)(2,1)}, u32[]{:S(2)}) copy-start(bf16[3,64,64]{2,1,0:T(8,128)(2,1)} %deriv.1) | copy-start | bytes 73732
  23.8 0.7 copy-start.9
  40.3 16.5 %copy-start.2 = (f32[4,4,384]{2,1,0:T(4,128)S(1)}, f32[4,4,384]{2,1,0:T(4,128)}, u32[]{:S(2)}) copy-start(f32[4,4,384]{2,1,0:T(4,128)} %load.5) | copy-start | bytes 73732

commit v2 on v1

--- a/solution.py
+++ b/solution.py
@@ -291,12 +291,39 @@
     return result
 
 
+def member_rows(plan, ref, panel):
+    rows = [ref[d, pl.ds(panel, 1), :] for d in range(plan.ns)]
+    rows.append(jnp.zeros((8 - plan.ns, plan.width), F32))
+    return jnp.concatenate(rows, axis=0)
+
+
+def fetch(pairs, sems):
+    copies = [
+        pltpu.make_async_copy(source, target, sems.at[i])
+        for i, (source, target) in enumerate(pairs)
+    ]
+    for copy in copies:
+        copy.start()
+    return copies
+
+
 def stacked(ref, count):
     return jnp.concatenate([ref[d] for d in range(count)], axis=0)
 
 
-def pack_kernel(plan, trhs, arhs, jac, second, elem, node, weight, count, out, scr):
+def pack_kernel(
+    plan, trhs_hbm, arhs_hbm, jac_hbm, second_hbm, elem_hbm, node_hbm, weight_hbm, count_hbm,
+    out, trhs, arhs, jac, second, elem, node, weight, scr, count, sems,
+):
     nv, window = plan.nv, plan.window
+    copies = fetch(
+        (
+            (trhs_hbm, trhs), (arhs_hbm, arhs), (jac_hbm, jac), (second_hbm, second),
+            (elem_hbm, elem), (node_hbm, node), (weight_hbm, weight),
+            (count_hbm, count),
+        ),
+        sems,
+    )
     lane = _iota((1, LANES), 1)
     masks = []
     for dest in range(plan.groups):
@@ -316,11 +343,14 @@
         return total
 
     for f, ref in enumerate((trhs, arhs)):
+        copies[f].wait()
         for a in range(nv):
             parts = [ref[a, pl.ds(16 * k, 16), :] for k in range(4)]
             for dest in range(plan.groups):
                 out[dest, pl.ds((f * nv + a) * 16, 16), :] = window_of(parts, dest, BF16)
 
+    for copy in copies[2:]:
+        copy.wait()
     scr[...] = jnp.zeros(scr.shape, F32)
     for k in range(3):
         for a in range(nv):
@@ -354,7 +384,7 @@
     point = _iota((NP, LANES), 0)
     ends = [point // 16, (point // 4) % 4, point % 4]
     faces = sum(_flag((e == 0) | (e == 3)) for e in ends)
-    lane = _iota((1, LANES), 1)
+    lane = _iota((16, LANES), 1)
     z = plan.own * rank - plan.halo + lane % plan.window
     inside = _flag((z >= 0) & (z < plan.span))
     rows = []
@@ -364,42 +394,49 @@
     return rows
 
 
-def sweeps(plan, count, state, rounded, source, table, matrix, transposed, coef, rows):
+def sweeps(plan, count, state, source, table, matrix, transposed, coef, rows):
     nv, nx, window = plan.nv, plan.nx, plan.window
-    lane = _iota((1, LANES), 1)
+    lane = _iota((16, LANES), 1)
     not_last = _flag(lane < LANES - window).astype(BF16)
     not_first = _flag(lane >= window).astype(BF16)
+    none = jnp.zeros((16, LANES), BF16)
+
+    def plane(now, h, a, i):
+        return state[now, h, a, pl.ds(16 * i, 16), :].astype(BF16)
+
+    def flux(h, k, a, b):
+        index, row = (k * nv + b, a) if transposed else (k * nv + a, b)
+        line = table[h, index, pl.ds(row, 1), :]
+        return jnp.broadcast_to(line, (16, LANES)).astype(BF16)
+
     for s in range(count):
         now, later = s % 2, (s + 1) % 2
         for h in range(nx):
-            own = [rounded[now, h, b].reshape(4, 16, LANES) for b in range(nv)]
+            own = [[plane(now, h, b, i) for i in range(4)] for b in range(nv)]
             for a0 in range(0, nv, 2):
                 stacks = []
                 for a in (a0, a0 + 1):
                     parts = []
                     for k in range(3):
-                        total = None
+                        total = [None] * 4
                         for b in range(nv):
-                            r = (k * nv + b) * nv + a if transposed else (k * nv + a) * nv + b
-                            term = own[b] * table[h, r][None]
-                            total = term if total is None else total + term
-                        parts.append(total.reshape(NP, LANES))
-                    scaled = own[a].reshape(NP, LANES) * rows[a]
-                    parts.append(_roll(scaled, -window) * not_last)
-                    parts.append(_roll(scaled, window) * not_first)
-                    parts.append(_roll(scaled, -1))
-                    parts.append(_roll(scaled, 1))
-                    none = jnp.zeros((16, LANES), BF16)
-                    above = rounded[now, h + 1, a, 0:16, :] * rows[a] if h + 1 < nx else none
-                    below = rounded[now, h - 1, a, 48:64, :] * rows[a] if h > 0 else none
-                    parts += [above, below]
+                            factor = flux(h, k, a, b)
+                            for i in range(4):
+                                term = own[b][i] * factor
+                                total[i] = term if b == 0 else total[i] + term
+                        parts += total
+                    scaled = [own[a][i] * rows[a] for i in range(4)]
+                    parts += [_roll(x, -window) * not_last for x in scaled]
+                    parts += [_roll(x, window) * not_first for x in scaled]
+                    parts += [_roll(x, -1) for x in scaled]
+                    parts += [_roll(x, 1) for x in scaled]
+                    parts.append(plane(now, h + 1, a, 0) * rows[a] if h + 1 < nx else none)
+                    parts.append(plane(now, h - 1, a, 3) * rows[a] if h > 0 else none)
                     stacks.append(jnp.concatenate(parts, axis=0))
                 product = _nn(matrix, jnp.concatenate(stacks, axis=1))
                 for i, a in enumerate((a0, a0 + 1)):
-                    value = coef[a] * state[h, a] + source[h, a]
-                    value = value + product[:, LANES * i : LANES * (i + 1)]
-                    state[h, a] = value
-                    rounded[later, h, a] = value.astype(BF16)
+                    value = coef[a] * state[now, h, a] + source[h, a]
+                    state[later, h, a] = value + product[:, LANES * i : LANES * (i + 1)]
     return count % 2
 
 
@@ -429,18 +466,29 @@
     return low, high
 
 
-def write_exchange(plan, low, high, solved, solved_scr, out, rank):
-    solved_scr[...] = solved
-    mine = rank // (plan.groups // plan.held)
+def first_exchange(plan, low, high, solved, out):
+    share = plan.groups // plan.held
+    for dest in range(plan.ns):
+        for panel in range(plan.held):
+            q = dest * plan.held + panel
+            rows = [(low[t] if q < 8 else high[t])[q % 8 : q % 8 + 1] for t in range(plan.tiles)]
+            line = solved[dest : dest + 1]
+            rows += [line[:, LANES * t : LANES * (t + 1)] for t in range(plan.tiles)]
+            rows.append(jnp.zeros((8 - 2 * plan.tiles, LANES), F32))
+            block = jnp.concatenate(rows, axis=0).astype(BF16)
+            for g in range(panel * share, (panel + 1) * share):
+                out[g * plan.ns + dest] = block
+
+
+def second_exchange(plan, low, high, solved, out):
     for dest in range(plan.ns):
         rows = []
         first = dest * plan.held
         for t in range(plan.tiles):
             part = low[t] if first < 8 else high[t]
             rows.append(part[first % 8 : first % 8 + plan.held])
-        line = solved_scr[pl.ds(dest * plan.held + mine, 1), :]
-        for t in range(plan.tiles):
-            rows.append(line[:, LANES * t : LANES * (t + 1)])
+        line = solved[dest : dest + 1]
+        rows += [line[:, LANES * t : LANES * (t + 1)] for t in range(plan.tiles)]
         used = (plan.held + 1) * plan.tiles
         if used < 16:
             rows.append(jnp.zeros((16 - used, LANES), F32))
@@ -449,13 +497,27 @@
             out[g * plan.ns + dest] = block
 
 
-def read_loads(plan, received):
+def summed(plan, received):
     totals = []
     for d in range(plan.ns):
         total = received[d].astype(F32)
         for g in range(1, plan.groups):
             total = total + received[g * plan.ns + d].astype(F32)
         totals.append(total)
+    return totals
+
+
+def read_own_loads(plan, received):
+    totals = summed(plan, received)
+    tiles = []
+    for t in range(plan.tiles):
+        rows = [x[t : t + 1] for x in totals] + [jnp.zeros((8 - plan.ns, LANES), F32)]
+        tiles.append(jnp.concatenate(rows, axis=0))
+    return jnp.concatenate(tiles, axis=1)
+
+
+def read_loads(plan, received):
+    totals = summed(plan, received)
     tiles = []
     for t in range(plan.tiles):
         rows = [x[plan.held * t : plan.held * (t + 1)] for x in totals]
@@ -463,15 +525,17 @@
     return jnp.concatenate(tiles, axis=1)
 
 
-def push_force(plan, received, incidence, places, weights, couple, rhs, shell_scr, scr, source):
+def push_force(
+    plan, received, first, incidence, places, weights, couple, rhs, shell_scr, scr, source
+):
     span = plan.groups // plan.held
     for s in range(plan.ns):
         for panel in range(plan.held):
             block = received[panel * span * plan.ns + s].astype(F32)
             q = s * plan.held + panel
             for t in range(plan.tiles):
-                r = plan.held * plan.tiles + t
-                shell_scr[q : q + 1, LANES * t : LANES * (t + 1)] = block[r : r + 1]
+                line = block[first + t : first + t + 1]
+                shell_scr[q : q + 1, LANES * t : LANES * (t + 1)] = line
     left = _iota((8, LANES), 1) < PN
     for t in range(plan.tiles):
         upper = shell_scr[0:8, LANES * t : LANES * (t + 1)]
@@ -492,12 +556,42 @@
             source[h, a] = 0.5 * value
 
 
+def prepare_kernel(
+    plan, deriv_hbm, load_hbm, inverse_hbm, forward, backward, solved, deriv, load, inverse, sems
+):
+    mine = plan.rank() // (plan.groups // plan.held)
+    copies = fetch(
+        ((deriv_hbm, deriv), (load_hbm, load), (inverse_hbm.at[mine], inverse)), sems
+    )
+    p, c = _iota((NP, plan.depth), 0), _iota((NP, plan.depth), 1)
+    j, l = (p // 4) % 4, p % 4
+
+    def block(n, ok, shift):
+        return ok & (c - (3 + n) * NP == p + shift)
+
+    links = block(0, j == 3, -12) | block(1, j == 0, 12)
+    links = links | block(2, l == 3, -3) | block(3, l == 0, 3)
+    links = links | ((p >= 48) & (c - 7 * NP == p - 48))
+    links = links | ((p < 16) & (c - 7 * NP - 16 == p))
+    base = (0.5 * _flag(links)).astype(BF16)
+    forward[...] = base
+    backward[...] = base
+    for copy in copies:
+        copy.wait()
+    for k in range(3):
+        part = -0.5 * deriv[k].astype(F32)
+        forward[:, NP * k : NP * (k + 1)] = part.astype(BF16)
+        backward[:, NP * k : NP * (k + 1)] = part.T.astype(BF16)
+    solved[...] = _nt(member_rows(plan, load, mine).astype(BF16), inverse[...])
+
+
 def first_kernel(
-    plan, received, deriv, penalty, coupling, load, inverse,
-    adjoint, rhs, table, second, incidence, places, weights, forward, backward, out,
-    source, rounded, coef, scr, solved_scr,
+    plan, received, backward, solved, coupling_hbm, penalty,
+    adjoint, rhs, table, incidence, places, weights, out,
+    state, source, coef, scr, coupling, sems,
 ):
     nv, window, nx, ny = plan.nv, plan.window, plan.nx, plan.ny
+    copies = fetch(((coupling_hbm, coupling),), sems)
     rank = plan.rank()
     lane = _iota((1, LANES), 1)
     group = [_flag(lane // window == y) for y in range(ny)]
@@ -524,14 +618,7 @@
         for k in range(4):
             block = regroup([x[: plan.per * 8] for x in tails], k, F32)
             for i in range(plan.per):
-                granule = k * plan.per + i
-                part = block[8 * i : 8 * (i + 1)]
-                if granule < 3 * nv:
-                    for b in range(nv):
-                        row = jnp.broadcast_to(part[b : b + 1], (16, LANES))
-                        table[h, granule * nv + b] = row.astype(BF16)
-                elif granule == 3 * nv:
-                    second[h] = part
+                table[h, k * plan.per + i] = block[8 * i : 8 * (i + 1)]
         info = [x[plan.per * 8 :] for x in tails]
         place = _iota((LANES, LANES), 0)
         spot = _iota((plan.nodes, LANES), 0)
@@ -547,107 +634,95 @@
             columns = pl.ds(plan.slots * h + LANES * y, LANES)
             incidence[:, columns] = _flag(spot == position).astype(BF16)
 
-    p, c = _iota((NP, plan.depth), 0), _iota((NP, plan.depth), 1)
-    j, l = (p // 4) % 4, p % 4
-
-    def block(n, ok, shift):
-        return ok & (c - (3 + n) * NP == p + shift)
-
-    links = block(0, j == 3, -12) | block(1, j == 0, 12)
-    links = links | block(2, l == 3, -3) | block(3, l == 0, 3)
-    links = links | ((p >= 48) & (c - 7 * NP == p - 48))
-    links = links | ((p < 16) & (c - 7 * NP - 16 == p))
-    base = (0.5 * _flag(links)).astype(BF16)
-    forward[...] = base
-    backward[...] = base
-    for k in range(3):
-        part = -0.5 * deriv[k].astype(F32)
-        forward[:, NP * k : NP * (k + 1)] = part.astype(BF16)
-        backward[:, NP * k : NP * (k + 1)] = part.T.astype(BF16)
-
     rows = coefficients(plan, penalty, coef, rank)
     for h in range(nx):
         for a in range(nv):
             value = 0.5 * rhs[1, h, a].astype(F32)
             source[h, a] = value
-            adjoint[h, a] = value
-            rounded[0, h, a] = value.astype(BF16)
-    last = sweeps(
-        plan, FSWEEP - 1, adjoint, rounded, source, table, backward[...], True, coef, rows
-    )
-    values = [rounded[last, h].reshape(nv * NP, LANES) for h in range(nx)]
+            state[0, h, a] = value
+    last = sweeps(plan, FSWEEP - 1, state, source, table, backward[...], True, coef, rows)
+    values = [state[last, h].reshape(nv * NP, LANES).astype(BF16) for h in range(nx)]
+    copies[0].wait()
     low, high = node_loads(plan, couple_rows(coupling), values, incidence, places, weights, scr)
-    solved = shell_solve_rows(plan, stacked(load, plan.ns), inverse)
-    write_exchange(plan, low, high, solved, solved_scr, out, rank)
+    first_exchange(plan, low, high, solved[...], out)
+    adjoint[...] = state[last]
 
 
 def second_kernel(
-    plan, received, penalty, coupling, load, shell_rhs, inverse, adjoint_in, rhs, table, second,
-    incidence, places, weights, forward, backward,
+    plan, received, adjoint_in, rhs, table, incidence, places, weights, forward, backward,
+    coupling_hbm, load_hbm, shell_rhs_hbm, inverse_hbm, penalty,
     tangent, adjoint_rounded, out,
-    adjoint, source, rounded, coef, scr, solved_scr, shell_scr,
+    state, source, coef, scr, shell_scr, coupling, load, shell_rhs, inverse, sems,
 ):
     nv, nx = plan.nv, plan.nx
     rank = plan.rank()
+    mine = rank // (plan.groups // plan.held)
+    copies = fetch(
+        (
+            (coupling_hbm, coupling), (load_hbm, load), (shell_rhs_hbm, shell_rhs),
+            (inverse_hbm.at[mine], inverse),
+        ),
+        sems,
+    )
     rows = coefficients(plan, penalty, coef, rank)
+    for copy in copies:
+        copy.wait()
+    shell = member_rows(plan, shell_rhs, mine) - read_own_loads(plan, received)
+    shell = _nt(shell.astype(BF16), inverse[...])
+    shell = member_rows(plan, load, mine) + shell
+    solved = _nt(shell.astype(BF16), inverse[...])
     couple = couple_rows(coupling)
     push_force(
-        plan, received, incidence, places, weights, couple, rhs, shell_scr, scr, source
+        plan, received, plan.tiles, incidence, places, weights, couple, rhs, shell_scr, scr, source
     )
     for h in range(nx):
         for a in range(nv):
-            value = source[h, a]
-            tangent[h, a] = value
-            rounded[0, h, a] = value.astype(BF16)
-    sweeps(plan, FSWEEP - 1, tangent, rounded, source, table, forward[...], False, coef, rows)
+            state[0, h, a] = source[h, a]
+    last = sweeps(plan, FSWEEP - 1, state, source, table, forward[...], False, coef, rows)
+    tangent[...] = state[last]
     for h in range(nx):
         for a in range(nv):
-            extra = second[h, a : a + 1, :] * tangent[h, a]
+            extra = table[h, 3 * nv, a : a + 1, :] * state[last, h, a]
             source[h, a] = 0.5 * (rhs[1, h, a].astype(F32) + extra)
-            value = adjoint_in[h, a]
-            adjoint[h, a] = value
-            rounded[0, h, a] = value.astype(BF16)
-    last = sweeps(
-        plan, FSWEEP, adjoint, rounded, source, table, backward[...], True, coef, rows
-    )
-    adjoint_rounded[...] = rounded[last]
-    values = [rounded[last, h].reshape(nv * NP, LANES) for h in range(nx)]
-    low, high = node_loads(plan, couple, values, incidence, places, weights, scr)
-    shell = stacked(shell_rhs, plan.ns) - read_loads(plan, received)
-    shell = shell_solve_rows(plan, shell, inverse)
-    solved = shell_solve_rows(plan, stacked(load, plan.ns) + shell, inverse)
-    write_exchange(plan, low, high, solved, solved_scr, out, rank)
-
-
-def third_kernel(
-    plan, received, penalty, coupling, load, shell_rhs, inverse, tangent_in, adjoint_rounded,
-    rhs, table, incidence, places, weights, forward,
-    out, shell_tangent, shell_adjoint,
-    tangent, source, rounded, coef, scr, shell_scr,
-):
-    nv, nx, ny, ns = plan.nv, plan.nx, plan.ny, plan.ns
-    rank = plan.rank()
-    rows = coefficients(plan, penalty, coef, rank)
-    couple = couple_rows(coupling)
-    push_force(
-        plan, received, incidence, places, weights, couple, rhs, shell_scr, scr, source
-    )
     for h in range(nx):
         for a in range(nv):
-            value = tangent_in[h, a]
-            tangent[h, a] = value
-            rounded[0, h, a] = value.astype(BF16)
-    last = sweeps(
-        plan, FSWEEP, tangent, rounded, source, table, forward[...], False, coef, rows
-    )
-    lane = _iota((1, LANES), 1)
+            state[0, h, a] = adjoint_in[h, a]
+    last = sweeps(plan, FSWEEP, state, source, table, backward[...], True, coef, rows)
+    values = []
+    for h in range(nx):
+        value = state[last, h].reshape(nv * NP, LANES).astype(BF16)
+        adjoint_rounded[h] = value
+        values.append(value)
+    low, high = node_loads(plan, couple, values, incidence, places, weights, scr)
+    second_exchange(plan, low, high, solved, out)
+
+
+def third_kernel(
+    plan, received, tangent_in, adjoint_rounded, rhs, table, incidence, places, weights, forward,
+    coupling_hbm, penalty,
+    out,
+    state, source, coef, scr, shell_scr, coupling, sems,
+):
+    nv, nx, ny = plan.nv, plan.nx, plan.ny
+    rank = plan.rank()
+    copies = fetch(((coupling_hbm, coupling),), sems)
+    rows = coefficients(plan, penalty, coef, rank)
+    copies[0].wait()
+    push_force(
+        plan, received, plan.held * plan.tiles, incidence, places, weights, couple_rows(coupling),
+        rhs, shell_scr, scr, source,
+    )
+    for h in range(nx):
+        for a in range(nv):
+            state[0, h, a] = tangent_in[h, a]
+    last = sweeps(plan, FSWEEP, state, source, table, forward[...], False, coef, rows)
+    lane = _iota((16, LANES), 1)
     narrow = plan.narrow
     group = [_flag(lane // narrow == n).astype(BF16) for n in range(8)]
     for h in range(nx):
         for a in range(nv):
-            parts = []
-            for ref in (rounded.at[last], adjoint_rounded):
-                parts += [ref[h, a, pl.ds(16 * i, 16), :] for i in range(4)]
+            parts = [state[last, h, a, pl.ds(16 * i, 16), :].astype(BF16) for i in range(4)]
+            parts += [adjoint_rounded[h, pl.ds(a * NP + 16 * i, 16), :] for i in range(4)]
             for y in range(ny):
                 total = None
                 for n in range(8):
@@ -655,16 +730,27 @@
                     term = _roll(parts[n], shift) * group[n]
                     total = term if total is None else total + term
                 out[h * ny + y, pl.ds(16 * a, 16), :] = total
-    shell = stacked(shell_rhs, ns) - read_loads(plan, received)
+
+
+def shell_kernel(
+    plan, received, load_hbm, shell_rhs_hbm, inverse_hbm, shell_tangent, shell_adjoint,
+    load, shell_rhs, inverse, sems,
+):
+    copies = fetch(
+        ((load_hbm, load), (shell_rhs_hbm, shell_rhs), (inverse_hbm, inverse)), sems
+    )
+    for copy in copies:
+        copy.wait()
+    shell = stacked(shell_rhs, plan.ns) - read_loads(plan, received)
     shell = shell_solve_rows(plan, shell, inverse)
-    solved = shell_solve_rows(plan, stacked(load, ns) + shell, inverse)
-    for d in range(ns):
+    solved = shell_solve_rows(plan, stacked(load, plan.ns) + shell, inverse)
+    for d in range(plan.ns):
         shell_adjoint[d] = shell[plan.held * d : plan.held * (d + 1)]
         shell_tangent[d] = solved[plan.held * d : plan.held * (d + 1)]
 
 
 def last_kernel(plan, received, tangent, adjoint):
-    lane = _iota((1, LANES), 1)
+    lane = _iota((16, LANES), 1)
     narrow = plan.narrow
     group = [_flag(lane // narrow == g).astype(BF16) for g in range(plan.groups)]
     for a in range(plan.nv):
@@ -678,18 +764,22 @@
                 ref[a, pl.ds(16 * i, 16), :] = total
 
 
-def call(kernel, plan, out_shape, scratch, scalars, args):
+def call(kernel, plan, out_shape, scratch, copies, on_chip, in_hbm, scalars, limit=KERNEL_VMEM):
     vmem = pl.BlockSpec(memory_space=pltpu.VMEM)
+    hbm = pl.BlockSpec(memory_space=pltpu.HBM)
     smem = pl.BlockSpec(memory_space=pltpu.SMEM)
-    specs = [smem if i in scalars else vmem for i in range(len(args))]
+    specs = [vmem] * len(on_chip) + [hbm] * len(in_hbm) + [smem] * len(scalars)
+    scratch_shapes = [x if isinstance(x, pl.MemoryRef) else pltpu.VMEM(*x) for x in scratch]
+    if copies:
+        scratch_shapes.append(pltpu.SemaphoreType.DMA((copies,)))
     return pl.pallas_call(
         functools.partial(kernel, plan),
         out_shape=[jax.ShapeDtypeStruct(s, d) for s, d in out_shape],
         in_specs=specs,
         out_specs=[vmem] * len(out_shape),
-        scratch_shapes=[pltpu.VMEM(s, d) for s, d in scratch],
-        compiler_params=pltpu.CompilerParams(vmem_limit_bytes=KERNEL_VMEM),
-    )(*args)
+        scratch_shapes=scratch_shapes,
+        compiler_params=pltpu.CompilerParams(vmem_limit_bytes=limit),
+    )(*on_chip, *in_hbm, *scalars)
 
 
 def slab_body(
@@ -697,60 +787,70 @@
     shell_inverse, shell_load, shell_adjoint_rhs, iface_elem, iface_node, iface_weight,
     iface_count,
 ):
-    nv, nx, ny, ns, groups = plan.nv, plan.nx, plan.ny, plan.ns, plan.groups
+    nv, nx, ns, groups = plan.nv, plan.nx, plan.ns, plan.groups
     flow, everyone = ("fx", "fy"), ("fx", "fy", "st")
-    state = (nx, nv, NP, LANES)
-    rounded = ((2,) + state, BF16)
+    state = ((nx, nv, NP, LANES), F32)
+    both = ((2, nx, nv, NP, LANES), F32)
     coef = ((nv, NP, LANES), F32)
     scr = ((8, 8, LANES), F32)
     shell_rows = ((plan.panels, plan.width), F32)
-    solved_rows = ((ns * plan.held, plan.width), F32)
-    trhs = tangent_rhs.reshape(nv, NP, LANES)
-    arhs = adjoint_rhs.reshape(nv, NP, LANES)
-    jac = jacobians.reshape(3, nv, nv, LANES)
-    second_rows = second_order.reshape(nv, 1, LANES)
-
+    matrix = ((NP, plan.depth), BF16)
+
+    def like(*arrays):
+        return [(x.shape, x.dtype) for x in arrays]
+
+    one_panel = (shell_inverse.shape[1:], BF16)
+    inputs = (
+        tangent_rhs.reshape(nv, NP, LANES), adjoint_rhs.reshape(nv, NP, LANES),
+        jacobians.reshape(3, nv, nv, LANES), second_order.reshape(nv, 1, LANES),
+        iface_elem, iface_node, iface_weight,
+    )
     (packed,) = call(
         pack_kernel, plan, [((groups, plan.rows, LANES), BF16)],
-        [((4 * plan.per, 8, LANES), F32)], (7,),
-        (trhs, arhs, jac, second_rows, iface_elem, iface_node, iface_weight, iface_count),
+        like(*inputs)
+        + [((4 * plan.per, 8, LANES), F32), pltpu.SMEM(iface_count.shape, iface_count.dtype)],
+        len(inputs) + 1, (), inputs + (iface_count,), (), None,
     )
     slab = lax.all_to_all(packed, flow, split_axis=0, concat_axis=0, tiled=True)
-    exchange = ((groups * ns, 16, LANES), BF16)
-    adjoint, rhs, table, second, incidence, places, weights, forward, backward, sent = call(
+    forward, backward, solved = call(
+        prepare_kernel, plan, [matrix, matrix, ((8, plan.width), F32)],
+        like(deriv, shell_load) + [one_panel], 3, (), (deriv, shell_load, shell_inverse), (),
+    )
+    adjoint, rhs, table, incidence, places, weights, sent = call(
         first_kernel, plan,
         [
-            (state, F32), ((2,) + state, BF16), ((nx, plan.deps, 16, LANES), BF16),
-            ((nx, 8, LANES), F32), ((plan.nodes, nx * plan.slots), BF16),
-            ((nx, LANES, plan.slots), BF16), ((nx, 1, plan.slots), F32),
-            ((NP, plan.depth), BF16), ((NP, plan.depth), BF16), exchange,
+            state, ((2,) + state[0], BF16), ((nx, 4 * plan.per, 8, LANES), F32),
+            ((plan.nodes, nx * plan.slots), BF16), ((nx, LANES, plan.slots), BF16),
+            ((nx, 1, plan.slots), F32), ((groups * ns, 8, LANES), BF16),
         ],
-        [(state, F32), rounded, coef, scr, solved_rows], (2,),
-        (slab, deriv, penalty, coupling, shell_load, shell_inverse),
+        [both, state, coef, scr] + like(coupling), 1,
+        (slab, backward, solved), (coupling,), (penalty,),
     )
     received = lax.all_to_all(sent, everyone, split_axis=0, concat_axis=0, tiled=True)
     tangent, adjoint_rounded, sent = call(
-        second_kernel, plan, [(state, F32), (state, BF16), exchange],
-        [(state, F32), (state, F32), rounded, coef, scr, solved_rows, shell_rows], (1,),
-        (
-            received, penalty, coupling, shell_load, shell_adjoint_rhs, shell_inverse, adjoint,
-            rhs, table, second, incidence, places, weights, forward, backward,
-        ),
+        second_kernel, plan,
+        [state, ((nx, nv * NP, LANES), BF16), ((groups * ns, 16, LANES), BF16)],
+        [both, state, coef, scr, shell_rows]
+        + like(coupling, shell_load, shell_adjoint_rhs) + [one_panel], 4,
+        (received, adjoint, rhs, table, incidence, places, weights, forward, backward),
+        (coupling, shell_load, shell_adjoint_rhs, shell_inverse), (penalty,),
     )
     received = lax.all_to_all(sent, everyone, split_axis=0, concat_axis=0, tiled=True)
+    (sent,) = call(
+        third_kernel, plan, [((groups, plan.field_rows, LANES), BF16)],
+        [both, state, coef, scr, shell_rows] + like(coupling), 1,
+        (received, tangent, adjoint_rounded, rhs, table, incidence, places, weights, forward),
+        (coupling,), (penalty,),
+    )
     shell_shape = (shell_load.shape, F32)
-    sent, shell_tangent, shell_adjoint = call(
-        third_kernel, plan,
-        [((groups, plan.field_rows, LANES), BF16), shell_shape, shell_shape],
-        [(state, F32), (state, F32), rounded, coef, scr, shell_rows], (1,),
-        (
-            received, penalty, coupling, shell_load, shell_adjoint_rhs, shell_inverse, tangent,
-            adjoint_rounded, rhs, table, incidence, places, weights, forward,
-        ),
+    shell_tangent, shell_adjoint = call(
+        shell_kernel, plan, [shell_shape, shell_shape],
+        like(shell_load, shell_adjoint_rhs, shell_inverse), 3,
+        (received,), (shell_load, shell_adjoint_rhs, shell_inverse), (),
     )
     received = lax.all_to_all(sent, flow, split_axis=0, concat_axis=0, tiled=True)
     tangent, adjoint = call(
-        last_kernel, plan, [((nv, NP, LANES), BF16)] * 2, [], (), (received,)
+        last_kernel, plan, [((nv, NP, LANES), BF16)] * 2, [], 0, (received,), (), ()
     )
     return (
         tangent.reshape(tangent_rhs.shape), adjoint.reshape(adjoint_rhs.shape),

time: 71.9 us -> 63.6 us (0.88)
  blocking collectives: 45.2 us -> 21.4 us
  waiting for transfers between devices: 0 us -> 11.7 us
  starting transfers between devices: 0 us -> 8.61 us
  local copies, waits for them, and re-layouts: 8.09 us -> 1.55 us
  Pallas kernels: 16.6 us -> 18.4 us
    all_to_all x2 -> x0, blocking collectives: 22.9 us -> none  [the longest x1 14.4 us: slab_body(): slab = lax.all_to_all(packed, flow, split_axis=0, concat_axis=0, tiled=True)]
    all_to_all x0 -> x2, waiting for transfers between devices: none -> 11.7 us  [the longest x1 7.4 us: slab_body(): slab = lax.all_to_all(packed, flow, split_axis=0, concat_axis=0, tiled=True)]
    all_to_all x0 -> x2, starting transfers between devices: none -> 8.61 us  [the longest x1 5.21 us: slab_body(): slab = lax.all_to_all(packed, flow, split_axis=0, concat_axis=0, tiled=True)]
    unnamed x30 -> x14, local copies, waits for them, and re-layouts: 8.09 us -> 1.55 us
    pallas_call x5 -> x7, Pallas kernels: 16.6 us -> 18.4 us  [call(): pl.pallas_call(functools.partial(kernel, plan), out_shape=[jax.ShapeDtype...]
    all_to_all x2, blocking collectives: 22.2 us -> 21.4 us  [slab_body(): lax.all_to_all(sent, everyone, split_axis=0, concat_axis=0, tiled=True)]
  transfers between devices with their start and end apart: 0 -> 2, of which waited for: 0 -> 2; matrix products, arithmetic and copies ran while one was open for 0% -> 0% of each run, Pallas kernels for 0% -> 4%
where the time goes in v2:
time: 63.6 us; the launch traced here: 63.1 us
  blocking collectives  21.4 us (34%)
  Pallas kernels  18.4 us (29%)
  waiting for transfers between devices  11.7 us (18%)
  starting transfers between devices  8.61 us (14%)
  local copies, waits for them, and re-layouts  1.55 us (2%)
  between operations  1.48 us (2%)
    all_to_all x2, blocking collectives, slab_body(): lax.all_to_all(sent, everyone, split_axis=0, concat_axis=0, tiled=True)  21.4 us
    pallas_call x7, Pallas kernels, call(): pl.pallas_call(functools.partial(kernel, plan), out_shape=[jax.ShapeDtype...  18.4 us
    all_to_all x1, waiting for transfers between devices, slab_body(): slab = lax.all_to_all(packed, flow, split_axis=0, concat_axis=0, tiled=True)  7.4 us
    all_to_all x1, starting transfers between devices, slab_body(): slab = lax.all_to_all(packed, flow, split_axis=0, concat_axis=0, tiled=True)  5.21 us
    all_to_all x1, waiting for transfers between devices, slab_body(): lax.all_to_all(sent, flow, split_axis=0, concat_axis=0, tiled=True)  4.3 us
    all_to_all x1, starting transfers between devices, slab_body(): lax.all_to_all(sent, flow, split_axis=0, concat_axis=0, tiled=True)  3.4 us
    unnamed x14, local copies, waits for them, and re-layouts  1.55 us
  transfers between devices with their start and end apart: 2, of which 2 were waited for; matrix products, arithmetic and copies ran while one was open for 0% of the time, Pallas kernels for 4%

profile of v2, /device:TPU:0, one launch (start us, length us, event | category | flops | bytes accessed | tf_op | source)
XLA Modules:
  0.0 63.1 jit_solution(3932861948531130047)
XLA Ops:
  0.6 0.0 copy-start.2
  0.6 0.0 copy-start
  0.7 0.0 copy-start.4
  0.7 0.0 copy-start.6
  0.7 0.0 copy-start.3
  1.4 2.5 %shard_map.165 = bf16[8,240,128]{2,1,0:T(8,128)(2,1)} custom-call(bf16[6,64,128]{2,1,0:T(8,128)(2,1)} %bitcast.10, bf16[6,64,128]{2,1,0:T(8,128)(2,1)} %bitcast.11, bf16[3,6,6,128]{3,2,1,0:T(8,128)(2,1)} %bitcast.12, f32[6,1,128]{2,1,0:T(1,128)} %bitcast.13, s32[1,128]{1,0:T(1,128)} %elem_hbm.1, s32[1,128]{1,0:T(1,128)} %node_hbm.1, f32[1,128]{1,0:T(1,128)} %weight_hbm.1, ...), custom_call_target="tpu_custom_call" | custom-call | tf_op jit(solution)/shard_map/pallas_call | solution.py:775
  3.9 5.2 %all-to-all-start = ((bf16[8,240,128]{2,1,0:T(8,128)(2,1)}), bf16[8,240,128]{2,1,0:T(8,128)(2,1)S(1)}, u32[]{:S(2)}, u32[]{:S(2)}) async-start(bf16[8,240,128]{2,1,0:T(8,128)(2,1)} %shard_map.165), calls=%async_computation | async-start | bytes 983040 | tf_op jit(solution)/shard_map/all_to_all | solution.py:814
  9.1 0.0 copy-done
  9.1 0.0 copy-start.1
  9.1 0.7 %copy-done.1 = f32[4,4,384]{2,1,0:T(4,128)S(1)} copy-done((f32[4,4,384]{2,1,0:T(4,128)S(1)}, f32[4,4,384]{2,1,0:T(4,128)}, u32[]{:S(2)}) %copy-start.1) | copy-done | bytes 24600
  9.9 0.0 copy-start.5
  9.9 0.8 %copy-done.5 = bf16[3,64,64]{2,1,0:T(8,128)(2,1)S(1)} copy-done((bf16[3,64,64]{2,1,0:T(8,128)(2,1)S(1)}, bf16[3,64,64]{2,1,0:T(8,128)(2,1)}, u32[]{:S(2)}) %copy-start.5) | copy-done | bytes 24600
  10.7 0.4 shard_map.166
  11.1 7.4 %all-to-all-done.received = bf16[8,240,128]{2,1,0:T(8,128)(2,1)S(1)} async-done(((bf16[8,240,128]{2,1,0:T(8,128)(2,1)}), bf16[8,240,128]{2,1,0:T(8,128)(2,1)S(1)}, u32[]{:S(2)}, u32[]{:S(2)}) %all-to-all-start) | async-done | bytes 491552 | tf_op jit(solution)/shard_map/all_to_all | solution.py:814
  18.5 0.0 copy-done.4
  18.5 0.0 copy-done.6
  18.5 4.3 %shard_map.167 = (f32[2,6,64,128]{3,2,1,0:T(8,128)S(1)}, bf16[2,2,6,64,128]{4,3,2,1,0:T(8,128)(2,1)S(1)}, f32[2,20,8,128]{3,2,1,0:T(8,128)S(1)}, bf16[1024,1024]...) custom-call(bf16[8,240,128]{2,1,0:T(8,128)(2,1)S(1)} %all-to-all-don, ...), custom_call_target="tpu_custom_call" | custom-call | tf_op jit(solution)/shard_map/pallas_call | solution.py:775
  22.8 11.3 %all_to_all.20.received = bf16[32,8,128]{2,1,0:T(8,128)(2,1)S(1)} all-to-all(bf16[32,8,128]{2,1,0:T(8,128)(2,1)S(1)} %get-tuple-element.23), channel_id=1, replica_groups=mesh['fx'=2,'fy'=4,'st'=4] {'fx','fy','st'}, dimensions={0} | all-to-all | bytes 131072 | tf_op jit(solution)/shard_map/all_to_all | solution.py:829
  34.1 0.0 copy-done.2
  34.1 0.0 copy-done.3
  34.1 4.8 %shard_map.168 = (f32[2,6,64,128]{3,2,1,0:T(8,128)S(1)}, bf16[2,384,128]{2,1,0:T(8,128)(2,1)S(1)}, bf16[32,16,128]{2,1,0:T(8,128)(2,1)S(1)}) custom-call(bf16[32,8,128]{2,1,0:T(8,128)(2,1)S(1)} %all_to_all.20.received, f32[2,6,64,128]{3,2,1,0:T(8,128)S(1)} %get-tuple-element.24.adjoint_in, bf16[2,2,6,64,128]{4,3,2,1,0:T(8,128)(2,1)S(1)} %get-tuple-element.25.rhs, ...), custom_call_target="tpu_custom_call" | custom-call | tf_op jit(solution)/shard_map/pallas_call | solution.py:775
  38.9 10.1 %all_to_all.21.received = bf16[32,16,128]{2,1,0:T(8,128)(2,1)S(1)} all-to-all(bf16[32,16,128]{2,1,0:T(8,128)(2,1)S(1)} %get-tuple-element.31), channel_id=1, replica_groups=mesh['fx'=2,'fy'=4,'st'=4] {'fx','fy','st'}, dimensions={0} | all-to-all | bytes 262144 | tf_op jit(solution)/shard_map/all_to_all | solution.py:838
  49.0 3.4 %shard_map.169 = bf16[8,96,128]{2,1,0:T(8,128)(2,1)} custom-call(bf16[32,16,128]{2,1,0:T(8,128)(2,1)S(1)} %all_to_all.21.received, f32[2,6,64,128]{3,2,1,0:T(8,128)S(1)} %get-tuple-element.32.tangent_in, bf16[2,384,128]{2,1,0:T(8,128)(2,1)S(1)} %get-tuple-element.33.adjoint_rounded, bf16[2,2,6,64,128]{4,3,2,1,0:T(8,128)(2,1)S(1)} %get-tuple-element.25.rhs, ...), custom_call_target="tpu_custom_call" | custom-call | tf_op jit(solution)/shard_map/pallas_call | solution.py:775
  52.4 3.4 %all-to-all-start.3 = ((bf16[8,96,128]{2,1,0:T(8,128)(2,1)}), bf16[8,96,128]{2,1,0:T(8,128)(2,1)S(1)}, u32[]{:S(2)}, u32[]{:S(2)}) async-start(bf16[8,96,128]{2,1,0:T(8,128)(2,1)} %shard_map.169), calls=%async_computation.3 | async-start | bytes 393216 | tf_op jit(solution)/shard_map/all_to_all | solution.py:851
  55.9 1.8 %shard_map.171 = (f32[4,4,384]{2,1,0:T(4,128)}, f32[4,4,384]{2,1,0:T(4,128)}) custom-call(bf16[32,16,128]{2,1,0:T(8,128)(2,1)S(1)} %all_to_all.21.received, f32[4,4,384]{2,1,0:T(4,128)S(1)} %copy-done.2, f32[4,4,384]{2,1,0:T(4,128)S(1)} %copy-done.3, bf16[4,384,384]{2,1,0:T(8,128)(2,1)S(1)} %copy-done), custom_call_target="tpu_custom_call" | custom-call | tf_op jit(solution)/shard_map/pallas_call | solution.py:775
  57.7 4.3 %all-to-all-done.3.received = bf16[8,96,128]{2,1,0:T(8,128)(2,1)S(1)} async-done(((bf16[8,96,128]{2,1,0:T(8,128)(2,1)}), bf16[8,96,128]{2,1,0:T(8,128)(2,1)S(1)}, u32[]{:S(2)}, u32[]{:S(2)}) %all-to-all-start.3) | async-done | bytes 196640 | tf_op jit(solution)/shard_map/all_to_all | solution.py:851
  62.0 1.1 %shard_map.170 = (bf16[6,64,128]{2,1,0:T(8,128)(2,1)}, bf16[6,64,128]{2,1,0:T(8,128)(2,1)}) custom-call(bf16[8,96,128]{2,1,0:T(8,128)(2,1)S(1)} %all-to-all-done.3.received), custom_call_target="tpu_custom_call" | custom-call | tf_op jit(solution)/shard_map/pallas_call | solution.py:775
Async XLA Ops:
  0.6 33.4 %copy-start.2 = (f32[4,4,384]{2,1,0:T(4,128)S(1)}, f32[4,4,384]{2,1,0:T(4,128)}, u32[]{:S(2)}) copy-start(f32[4,4,384]{2,1,0:T(4,128)} %load_hbm.5) | copy-start | bytes 73732
  0.6 8.5 %copy-start = (bf16[4,384,384]{2,1,0:T(8,128)(2,1)S(1)}, bf16[4,384,384]{2,1,0:T(8,128)(2,1)}, u32[]{:S(2)}) copy-start(bf16[4,384,384]{2,1,0:T(8,128)(2,1)} %inverse_hbm.5) | copy-start | bytes 3538948
  0.7 17.8 %copy-start.4 = (bf16[6,384]{1,0:T(8,128)(2,1)S(1)}, bf16[6,384]{1,0:T(8,128)(2,1)}, u32[]{:S(2)}) copy-start(bf16[6,384]{1,0:T(8,128)(2,1)} %coupling_hbm.5) | copy-start | bytes 13828
  0.7 17.8 %copy-start.6 = (f32[6]{0:T(128)S(1)}, f32[6]{0:T(128)}, u32[]{:S(2)}) copy-start(f32[6]{0:T(128)} %penalty.5) | copy-start | bytes 76
  0.7 33.4 %copy-start.3 = (f32[4,4,384]{2,1,0:T(4,128)S(1)}, f32[4,4,384]{2,1,0:T(4,128)}, u32[]{:S(2)}) copy-start(f32[4,4,384]{2,1,0:T(4,128)} %shell_rhs_hbm.3) | copy-start | bytes 73732
  3.9 14.6 %all-to-all-start = ((bf16[8,240,128]{2,1,0:T(8,128)(2,1)}), bf16[8,240,128]{2,1,0:T(8,128)(2,1)S(1)}, u32[]{:S(2)}, u32[]{:S(2)}) async-start(bf16[8,240,128]{2,1,0:T(8,128)(2,1)} %shard_map.165), calls=%async_computation | async-start | bytes 983040 | tf_op jit(solution)/shard_map/all_to_all | solution.py:814
  9.1 0.7 %copy-start.1 = (f32[4,4,384]{2,1,0:T(4,128)S(1)}, f32[4,4,384]{2,1,0:T(4,128)}, u32[]{:S(2)}) copy-start(f32[4,4,384]{2,1,0:T(4,128)} %load_hbm.5) | copy-start | bytes 73732
  9.9 0.8 %copy-start.5 = (bf16[3,64,64]{2,1,0:T(8,128)(2,1)S(1)}, bf16[3,64,64]{2,1,0:T(8,128)(2,1)}, u32[]{:S(2)}) copy-start(bf16[3,64,64]{2,1,0:T(8,128)(2,1)} %deriv_hbm.1) | copy-start | bytes 73732
  52.4 9.5 %all-to-all-start.3 = ((bf16[8,96,128]{2,1,0:T(8,128)(2,1)}), bf16[8,96,128]{2,1,0:T(8,128)(2,1)S(1)}, u32[]{:S(2)}, u32[]{:S(2)}) async-start(bf16[8,96,128]{2,1,0:T(8,128)(2,1)} %shard_map.169), calls=%async_computation.3 | async-start | bytes 393216 | tf_op jit(solution)/shard_map/all_to_all | solution.py:851

commit v3 on v2

--- a/solution.py
+++ b/solution.py
@@ -313,7 +313,7 @@
 
 def pack_kernel(
     plan, trhs_hbm, arhs_hbm, jac_hbm, second_hbm, elem_hbm, node_hbm, weight_hbm, count_hbm,
-    out, trhs, arhs, jac, second, elem, node, weight, scr, count, sems,
+    out_hbm, trhs, arhs, jac, second, elem, node, weight, count, scr, out, sems,
 ):
     nv, window = plan.nv, plan.window
     copies = fetch(
@@ -342,12 +342,21 @@
             total = term if total is None else total + term
         return total
 
+    sent = []
+
+    def send(first, count):
+        part = pl.ds(first, count)
+        sem = sems.at[len(copies) + len(sent)]
+        sent.append(pltpu.make_async_copy(out.at[:, part], out_hbm.at[:, part], sem))
+        sent[-1].start()
+
     for f, ref in enumerate((trhs, arhs)):
         copies[f].wait()
         for a in range(nv):
             parts = [ref[a, pl.ds(16 * k, 16), :] for k in range(4)]
             for dest in range(plan.groups):
                 out[dest, pl.ds((f * nv + a) * 16, 16), :] = window_of(parts, dest, BF16)
+        send(f * plan.field_rows, plan.field_rows)
 
     for copy in copies[2:]:
         copy.wait()
@@ -360,7 +369,7 @@
     quarter = [
         scr[pl.ds(plan.per * k, plan.per)].reshape(plan.per * 8, LANES) for k in range(4)
     ]
-    live = _flag(lane < count[0])
+    live = _flag(lane < jnp.broadcast_to(count[...], (1, LANES)))
     scaled = weight[...] * live
     coarse = scaled.astype(BF16).astype(F32)
     panel = node[...] // PN
@@ -378,6 +387,9 @@
         block = jnp.concatenate([window_of(quarter, dest, F32), table], axis=0)
         first = 2 * plan.field_rows
         out[dest, pl.ds(first, plan.rows - first), :] = block.astype(BF16)
+    send(2 * plan.field_rows, plan.rows - 2 * plan.field_rows)
+    for copy in sent:
+        copy.wait()
 
 
 def coefficients(plan, penalty, coef, rank):
@@ -446,21 +458,21 @@
     return jnp.concatenate([wide, pad], axis=0).astype(BF16)
 
 
-def node_loads(plan, couple, values, incidence, places, weights, scr):
+def node_loads(plan, couple, values, hot, tile_hot, places, weights):
     lane = _iota((1, LANES), 1)
     place = lane % plan.window
     owned = _flag((place >= plan.halo) & (place < plan.halo + plan.own))
     picked = []
     for h in range(plan.nx):
         flow = _nn(couple, values[h]) * owned
-        picked.append(_fold(_nn(_split(flow), places[h])) * weights[h])
-    nodal = _fold(_nt(_split(jnp.concatenate(picked, axis=1)), incidence[...]))
-    for j in range(8):
-        scr[:, j, :] = nodal[:, LANES * j : LANES * (j + 1)]
+        picked.append(_fold(_nn(_split(flow), places[h])))
+    picked = jnp.concatenate(picked, axis=1) * weights[...]
+    spread = [picked[c : c + 1] * tile_hot[...] for c in range(SDOF)]
+    nodal = _fold(_nt(_split(jnp.concatenate(spread, axis=0)), hot[...]))
     left = _iota((8, LANES), 1) < PN
     low, high = [], []
     for t in range(plan.tiles):
-        even, odd = scr[2 * t], scr[2 * t + 1]
+        even, odd = nodal[16 * t : 16 * t + 8], nodal[16 * t + 8 : 16 * t + 16]
         low.append(jnp.where(left, even, _roll(odd, PN)))
         high.append(jnp.where(left, _roll(even, PN), odd))
     return low, high
@@ -526,7 +538,7 @@
 
 
 def push_force(
-    plan, received, first, incidence, places, weights, couple, rhs, shell_scr, scr, source
+    plan, received, first, hot, tile_hot, places, weights, couple, rhs, shell_scr, scr, source
 ):
     span = plan.groups // plan.held
     for s in range(plan.ns):
@@ -544,11 +556,13 @@
         scr[2 * t + 1] = jnp.where(left, _roll(upper, PN), lower)
     for c in range(2 * plan.tiles, 8):
         scr[c] = jnp.zeros((8, LANES), F32)
-    nodal = jnp.concatenate([scr[:, j, :] for j in range(8)], axis=1).astype(BF16)
-    picked = _nn(nodal, incidence[...])
+    nodal = jnp.concatenate([scr[:, j, :] for j in range(8)], axis=0).astype(BF16)
+    spread = _nn(nodal, hot[...])
+    picked = sum(spread[8 * j : 8 * (j + 1)] * tile_hot[j : j + 1, :] for j in range(8))
+    picked = picked * weights[...]
     twice = jnp.concatenate([couple, couple], axis=0)
     for h in range(plan.nx):
-        part = picked[:, plan.slots * h : plan.slots * (h + 1)] * weights[h]
+        part = picked[:, plan.slots * h : plan.slots * (h + 1)]
         dofs = _fold(_nt(_split(part), places[h]))
         push = _tn(twice, _split(dofs))
         for a in range(plan.nv):
@@ -556,13 +570,8 @@
             source[h, a] = 0.5 * value
 
 
-def prepare_kernel(
-    plan, deriv_hbm, load_hbm, inverse_hbm, forward, backward, solved, deriv, load, inverse, sems
-):
+def prepare_kernel(plan, deriv, load, inverse, forward, backward, solved):
     mine = plan.rank() // (plan.groups // plan.held)
-    copies = fetch(
-        ((deriv_hbm, deriv), (load_hbm, load), (inverse_hbm.at[mine], inverse)), sems
-    )
     p, c = _iota((NP, plan.depth), 0), _iota((NP, plan.depth), 1)
     j, l = (p // 4) % 4, p % 4
 
@@ -576,22 +585,19 @@
     base = (0.5 * _flag(links)).astype(BF16)
     forward[...] = base
     backward[...] = base
-    for copy in copies:
-        copy.wait()
     for k in range(3):
         part = -0.5 * deriv[k].astype(F32)
         forward[:, NP * k : NP * (k + 1)] = part.astype(BF16)
         backward[:, NP * k : NP * (k + 1)] = part.T.astype(BF16)
-    solved[...] = _nt(member_rows(plan, load, mine).astype(BF16), inverse[...])
+    solved[...] = _nt(member_rows(plan, load, mine).astype(BF16), inverse[mine])
 
 
 def first_kernel(
-    plan, received, backward, solved, coupling_hbm, penalty,
-    adjoint, rhs, table, incidence, places, weights, out,
-    state, source, coef, scr, coupling, sems,
+    plan, received, backward, solved, coupling, penalty,
+    adjoint, rhs, table, hot, tile_hot, places, weights, out,
+    state, source, coef,
 ):
     nv, window, nx, ny = plan.nv, plan.window, plan.nx, plan.ny
-    copies = fetch(((coupling_hbm, coupling),), sems)
     rank = plan.rank()
     lane = _iota((1, LANES), 1)
     group = [_flag(lane // window == y) for y in range(ny)]
@@ -612,16 +618,15 @@
                     rhs[f, h, a, pl.ds(16 * k, 16), :] = regroup(parts, k, BF16)
         first = 2 * plan.field_rows
         tails = [
-            received[h * ny + y, pl.ds(first, plan.rows - first), :].astype(F32)
-            for y in range(ny)
+            received[h * ny + y, pl.ds(first, plan.rows - first), :] for y in range(ny)
         ]
         for k in range(4):
-            block = regroup([x[: plan.per * 8] for x in tails], k, F32)
+            block = regroup(tails, k, BF16).astype(F32)
             for i in range(plan.per):
                 table[h, k * plan.per + i] = block[8 * i : 8 * (i + 1)]
-        info = [x[plan.per * 8 :] for x in tails]
+        info = [x.astype(F32)[plan.per * 8 :] for x in tails]
         place = _iota((LANES, LANES), 0)
-        spot = _iota((plan.nodes, LANES), 0)
+        spot = _iota((8, LANES), 0)
         for y in range(ny):
             at = info[y]
             where = (at[0:1] - (plan.own * rank - plan.halo).astype(F32)).astype(jnp.int32)
@@ -629,10 +634,10 @@
             target = jnp.where(within, where + y * window, -1)
             columns = pl.ds(LANES * y, LANES)
             places[h, :, columns] = _flag(place == target).astype(BF16)
-            weights[h, :, columns] = at[3:4] + at[4:5]
-            position = (at[1:2] * LANES + at[2:3]).astype(jnp.int32)
             columns = pl.ds(plan.slots * h + LANES * y, LANES)
-            incidence[:, columns] = _flag(spot == position).astype(BF16)
+            weights[:, columns] = at[3:4] + at[4:5]
+            tile_hot[:, columns] = _flag(spot == at[1:2].astype(jnp.int32))
+            hot[:, columns] = _flag(place == at[2:3].astype(jnp.int32)).astype(BF16)
 
     rows = coefficients(plan, penalty, coef, rank)
     for h in range(nx):
@@ -642,38 +647,29 @@
             state[0, h, a] = value
     last = sweeps(plan, FSWEEP - 1, state, source, table, backward[...], True, coef, rows)
     values = [state[last, h].reshape(nv * NP, LANES).astype(BF16) for h in range(nx)]
-    copies[0].wait()
-    low, high = node_loads(plan, couple_rows(coupling), values, incidence, places, weights, scr)
+    low, high = node_loads(plan, couple_rows(coupling), values, hot, tile_hot, places, weights)
     first_exchange(plan, low, high, solved[...], out)
     adjoint[...] = state[last]
 
 
 def second_kernel(
-    plan, received, adjoint_in, rhs, table, incidence, places, weights, forward, backward,
-    coupling_hbm, load_hbm, shell_rhs_hbm, inverse_hbm, penalty,
+    plan, received, adjoint_in, rhs, table, hot, tile_hot, places, weights, forward, backward,
+    coupling, load, shell_rhs, inverse, penalty,
     tangent, adjoint_rounded, out,
-    state, source, coef, scr, shell_scr, coupling, load, shell_rhs, inverse, sems,
+    state, source, coef, scr, shell_scr,
 ):
     nv, nx = plan.nv, plan.nx
     rank = plan.rank()
     mine = rank // (plan.groups // plan.held)
-    copies = fetch(
-        (
-            (coupling_hbm, coupling), (load_hbm, load), (shell_rhs_hbm, shell_rhs),
-            (inverse_hbm.at[mine], inverse),
-        ),
-        sems,
-    )
     rows = coefficients(plan, penalty, coef, rank)
-    for copy in copies:
-        copy.wait()
     shell = member_rows(plan, shell_rhs, mine) - read_own_loads(plan, received)
-    shell = _nt(shell.astype(BF16), inverse[...])
+    shell = _nt(shell.astype(BF16), inverse[mine])
     shell = member_rows(plan, load, mine) + shell
-    solved = _nt(shell.astype(BF16), inverse[...])
+    solved = _nt(shell.astype(BF16), inverse[mine])
     couple = couple_rows(coupling)
     push_force(
-        plan, received, plan.tiles, incidence, places, weights, couple, rhs, shell_scr, scr, source
+        plan, received, plan.tiles, hot, tile_hot, places, weights, couple, rhs, shell_scr, scr,
+        source,
     )
     for h in range(nx):
         for a in range(nv):
@@ -693,24 +689,28 @@
         value = state[last, h].reshape(nv * NP, LANES).astype(BF16)
         adjoint_rounded[h] = value
         values.append(value)
-    low, high = node_loads(plan, couple, values, incidence, places, weights, scr)
+    low, high = node_loads(plan, couple, values, hot, tile_hot, places, weights)
     second_exchange(plan, low, high, solved, out)
 
 
 def third_kernel(
-    plan, received, tangent_in, adjoint_rounded, rhs, table, incidence, places, weights, forward,
-    coupling_hbm, penalty,
-    out,
-    state, source, coef, scr, shell_scr, coupling, sems,
+    plan, received, tangent_in, adjoint_rounded, rhs, table, hot, tile_hot, places, weights, forward,
+    coupling, load, shell_rhs, inverse, penalty,
+    out, shell_tangent, shell_adjoint,
+    state, source, coef, scr, shell_scr,
 ):
     nv, nx, ny = plan.nv, plan.nx, plan.ny
     rank = plan.rank()
-    copies = fetch(((coupling_hbm, coupling),), sems)
     rows = coefficients(plan, penalty, coef, rank)
-    copies[0].wait()
+    shell = stacked(shell_rhs, plan.ns) - read_loads(plan, received)
+    shell = shell_solve_rows(plan, shell, inverse)
+    solved = shell_solve_rows(plan, stacked(load, plan.ns) + shell, inverse)
+    for d in range(plan.ns):
+        shell_adjoint[d] = shell[plan.held * d : plan.held * (d + 1)]
+        shell_tangent[d] = solved[plan.held * d : plan.held * (d + 1)]
     push_force(
-        plan, received, plan.held * plan.tiles, incidence, places, weights, couple_rows(coupling),
-        rhs, shell_scr, scr, source,
+        plan, received, plan.held * plan.tiles, hot, tile_hot, places, weights,
+        couple_rows(coupling), rhs, shell_scr, scr, source,
     )
     for h in range(nx):
         for a in range(nv):
@@ -732,23 +732,6 @@
                 out[h * ny + y, pl.ds(16 * a, 16), :] = total
 
 
-def shell_kernel(
-    plan, received, load_hbm, shell_rhs_hbm, inverse_hbm, shell_tangent, shell_adjoint,
-    load, shell_rhs, inverse, sems,
-):
-    copies = fetch(
-        ((load_hbm, load), (shell_rhs_hbm, shell_rhs), (inverse_hbm, inverse)), sems
-    )
-    for copy in copies:
-        copy.wait()
-    shell = stacked(shell_rhs, plan.ns) - read_loads(plan, received)
-    shell = shell_solve_rows(plan, shell, inverse)
-    solved = shell_solve_rows(plan, stacked(load, plan.ns) + shell, inverse)
-    for d in range(plan.ns):
-        shell_adjoint[d] = shell[plan.held * d : plan.held * (d + 1)]
-        shell_tangent[d] = solved[plan.held * d : plan.held * (d + 1)]
-
-
 def last_kernel(plan, received, tangent, adjoint):
     lane = _iota((16, LANES), 1)
     narrow = plan.narrow
@@ -764,19 +747,20 @@
                 ref[a, pl.ds(16 * i, 16), :] = total
 
 
-def call(kernel, plan, out_shape, scratch, copies, on_chip, in_hbm, scalars, limit=KERNEL_VMEM):
+def call(kernel, plan, out_shape, scratch, copies, on_chip, in_hbm, scalars, limit=KERNEL_VMEM,
+         out_space=pltpu.VMEM):
     vmem = pl.BlockSpec(memory_space=pltpu.VMEM)
     hbm = pl.BlockSpec(memory_space=pltpu.HBM)
     smem = pl.BlockSpec(memory_space=pltpu.SMEM)
     specs = [vmem] * len(on_chip) + [hbm] * len(in_hbm) + [smem] * len(scalars)
-    scratch_shapes = [x if isinstance(x, pl.MemoryRef) else pltpu.VMEM(*x) for x in scratch]
+    scratch_shapes = [pltpu.VMEM(s, d) for s, d in scratch]
     if copies:
         scratch_shapes.append(pltpu.SemaphoreType.DMA((copies,)))
     return pl.pallas_call(
         functools.partial(kernel, plan),
         out_shape=[jax.ShapeDtypeStruct(s, d) for s, d in out_shape],
         in_specs=specs,
-        out_specs=[vmem] * len(out_shape),
+        out_specs=[pl.BlockSpec(memory_space=out_space)] * len(out_shape),
         scratch_shapes=scratch_shapes,
         compiler_params=pltpu.CompilerParams(vmem_limit_bytes=limit),
     )(*on_chip, *in_hbm, *scalars)
@@ -799,54 +783,54 @@
     def like(*arrays):
         return [(x.shape, x.dtype) for x in arrays]
 
-    one_panel = (shell_inverse.shape[1:], BF16)
     inputs = (
         tangent_rhs.reshape(nv, NP, LANES), adjoint_rhs.reshape(nv, NP, LANES),
         jacobians.reshape(3, nv, nv, LANES), second_order.reshape(nv, 1, LANES),
-        iface_elem, iface_node, iface_weight,
+        iface_elem, iface_node, iface_weight, iface_count.reshape(1, 1),
     )
     (packed,) = call(
         pack_kernel, plan, [((groups, plan.rows, LANES), BF16)],
         like(*inputs)
-        + [((4 * plan.per, 8, LANES), F32), pltpu.SMEM(iface_count.shape, iface_count.dtype)],
-        len(inputs) + 1, (), inputs + (iface_count,), (), None,
+        + [((4 * plan.per, 8, LANES), F32), ((groups, plan.rows, LANES), BF16)],
+        len(inputs) + 3, (), inputs, (), None, pltpu.HBM,
     )
     slab = lax.all_to_all(packed, flow, split_axis=0, concat_axis=0, tiled=True)
     forward, backward, solved = call(
         prepare_kernel, plan, [matrix, matrix, ((8, plan.width), F32)],
-        like(deriv, shell_load) + [one_panel], 3, (), (deriv, shell_load, shell_inverse), (),
-    )
-    adjoint, rhs, table, incidence, places, weights, sent = call(
+        [], 0, (deriv, shell_load, shell_inverse), (), (),
+    )
+    adjoint, rhs, table, hot, tile_hot, places, weights, sent = call(
         first_kernel, plan,
         [
             state, ((2,) + state[0], BF16), ((nx, 4 * plan.per, 8, LANES), F32),
-            ((plan.nodes, nx * plan.slots), BF16), ((nx, LANES, plan.slots), BF16),
-            ((nx, 1, plan.slots), F32), ((groups * ns, 8, LANES), BF16),
+            ((LANES, nx * plan.slots), BF16), ((8, nx * plan.slots), F32),
+            ((nx, LANES, plan.slots), BF16), ((1, nx * plan.slots), F32),
+            ((groups * ns, 8, LANES), BF16),
         ],
-        [both, state, coef, scr] + like(coupling), 1,
-        (slab, backward, solved), (coupling,), (penalty,),
+        [both, state, coef], 0, (slab, backward, solved, coupling), (), (penalty,),
     )
     received = lax.all_to_all(sent, everyone, split_axis=0, concat_axis=0, tiled=True)
     tangent, adjoint_rounded, sent = call(
         second_kernel, plan,
         [state, ((nx, nv * NP, LANES), BF16), ((groups * ns, 16, LANES), BF16)],
-        [both, state, coef, scr, shell_rows]
-        + like(coupling, shell_load, shell_adjoint_rhs) + [one_panel], 4,
-        (received, adjoint, rhs, table, incidence, places, weights, forward, backward),
-        (coupling, shell_load, shell_adjoint_rhs, shell_inverse), (penalty,),
+        [both, state, coef, scr, shell_rows], 0,
+        (
+            received, adjoint, rhs, table, hot, tile_hot, places, weights, forward, backward,
+            coupling, shell_load, shell_adjoint_rhs, shell_inverse,
+        ),
+        (), (penalty,),
     )
     received = lax.all_to_all(sent, everyone, split_axis=0, concat_axis=0, tiled=True)
-    (sent,) = call(
-        third_kernel, plan, [((groups, plan.field_rows, LANES), BF16)],
-        [both, state, coef, scr, shell_rows] + like(coupling), 1,
-        (received, tangent, adjoint_rounded, rhs, table, incidence, places, weights, forward),
-        (coupling,), (penalty,),
-    )
     shell_shape = (shell_load.shape, F32)
-    shell_tangent, shell_adjoint = call(
-        shell_kernel, plan, [shell_shape, shell_shape],
-        like(shell_load, shell_adjoint_rhs, shell_inverse), 3,
-        (received,), (shell_load, shell_adjoint_rhs, shell_inverse), (),
+    sent, shell_tangent, shell_adjoint = call(
+        third_kernel, plan,
+        [((groups, plan.field_rows, LANES), BF16), shell_shape, shell_shape],
+        [both, state, coef, scr, shell_rows], 0,
+        (
+            received, tangent, adjoint_rounded, rhs, table, hot, tile_hot, places, weights,
+            forward, coupling, shell_load, shell_adjoint_rhs, shell_inverse,
+        ),
+        (), (penalty,),
     )
     received = lax.all_to_all(sent, flow, split_axis=0, concat_axis=0, tiled=True)
     tangent, adjoint = call(

time: 63.6 us -> 59.7 us (0.939)
  blocking collectives: 21.4 us -> 29.9 us
  Pallas kernels: 18.4 us -> 13.6 us
  starting transfers between devices: 8.61 us -> 5.21 us
  waiting for transfers between devices: 11.7 us -> 9.09 us
  local copies, waits for them, and re-layouts: 1.55 us -> 0.03 us
    all_to_all x0 -> x1, blocking collectives: none -> 8.59 us  [slab_body(): lax.all_to_all(sent, flow, split_axis=0, concat_axis=0, tiled=True)]
    pallas_call x7 -> x6, Pallas kernels: 18.4 us -> 13.6 us  [call(): pl.pallas_call(functools.partial(kernel, plan), out_shape=[jax.ShapeDtype...]
    all_to_all x1 -> x0, waiting for transfers between devices: 4.3 us -> none  [slab_body(): lax.all_to_all(sent, flow, split_axis=0, concat_axis=0, tiled=True)]
    all_to_all x1 -> x0, starting transfers between devices: 3.4 us -> none  [slab_body(): lax.all_to_all(sent, flow, split_axis=0, concat_axis=0, tiled=True)]
    all_to_all x1, waiting for transfers between devices: 7.4 us -> 9.09 us  [slab_body(): slab = lax.all_to_all(packed, flow, split_axis=0, concat_axis=0, tiled=True)]
    unnamed x14 -> x12, local copies, waits for them, and re-layouts: 1.55 us -> 0.03 us
  transfers between devices with their start and end apart: 2 -> 1, of which waited for: 2 -> 1; matrix products, arithmetic and copies ran while one was open for 0% -> 0% of each run, Pallas kernels for 4% -> 0%
where the time goes in v3:
time: 59.7 us; the launch traced here: 59.3 us
  blocking collectives  29.9 us (50%)
  Pallas kernels  13.6 us (23%)
  waiting for transfers between devices  9.09 us (15%)
  starting transfers between devices  5.21 us (9%)
  between operations  1.47 us (2%)
    all_to_all x2, blocking collectives, slab_body(): lax.all_to_all(sent, everyone, split_axis=0, concat_axis=0, tiled=True)  21.4 us
    pallas_call x6, Pallas kernels, call(): pl.pallas_call(functools.partial(kernel, plan), out_shape=[jax.ShapeDtype...  13.6 us
    all_to_all x1, waiting for transfers between devices, slab_body(): slab = lax.all_to_all(packed, flow, split_axis=0, concat_axis=0, tiled=True)  9.09 us
    all_to_all x1, blocking collectives, slab_body(): lax.all_to_all(sent, flow, split_axis=0, concat_axis=0, tiled=True)  8.59 us
    all_to_all x1, starting transfers between devices, slab_body(): slab = lax.all_to_all(packed, flow, split_axis=0, concat_axis=0, tiled=True)  5.21 us
  transfers between devices with their start and end apart: 1, of which 1 were waited for; matrix products, arithmetic and copies ran while one was open for 0% of the time, Pallas kernels for 0%

profile of v3, /device:TPU:0, one launch (start us, length us, event | category | flops | bytes accessed | tf_op | source)
XLA Modules:
  0.0 59.3 jit_solution(17500795604317748033)
XLA Ops:
  0.6 0.0 copy-start.1
  0.6 0.0 copy-start
  0.7 0.0 copy-start.4
  1.4 2.4 %shard_map.165 = bf16[8,240,128]{2,1,0:T(8,128)(2,1)} custom-call(bf16[6,64,128]{2,1,0:T(8,128)(2,1)} %bitcast.12, bf16[6,64,128]{2,1,0:T(8,128)(2,1)} %bitcast.13, bf16[3,6,6,128]{3,2,1,0:T(8,128)(2,1)} %bitcast.14, f32[6,1,128]{2,1,0:T(1,128)} %bitcast.15, s32[1,128]{1,0:T(1,128)} %elem_hbm.1, s32[1,128]{1,0:T(1,128)} %node_hbm.1, f32[1,128]{1,0:T(1,128)} %weight_hbm.1, ...), custom_call_target="tpu_custom_call" | custom-call | tf_op jit(solution)/shard_map/pallas_call | solution.py:759
  3.9 0.0 copy-start.3
  3.9 0.0 copy-start.5
  3.9 5.2 %all-to-all-start = ((bf16[8,240,128]{2,1,0:T(8,128)(2,1)}), bf16[8,240,128]{2,1,0:T(8,128)(2,1)S(1)}, u32[]{:S(2)}, u32[]{:S(2)}) async-start(bf16[8,240,128]{2,1,0:T(8,128)(2,1)} %shard_map.165), calls=%async_computation | async-start | bytes 983040 | tf_op jit(solution)/shard_map/all_to_all | solution.py:797
  9.1 0.0 copy-done.1
  9.1 0.0 copy-done
  9.1 0.0 copy-done.4
  9.1 0.0 copy-start.2
  9.1 0.2 shard_map.166
  9.4 9.1 %all-to-all-done.received = bf16[8,240,128]{2,1,0:T(8,128)(2,1)S(1)} async-done(((bf16[8,240,128]{2,1,0:T(8,128)(2,1)}), bf16[8,240,128]{2,1,0:T(8,128)(2,1)S(1)}, u32[]{:S(2)}, u32[]{:S(2)}) %all-to-all-start) | async-done | bytes 491552 | tf_op jit(solution)/shard_map/all_to_all | solution.py:797
  18.5 0.0 copy-done.3
  18.5 0.0 copy-done.5
  18.5 2.3 %shard_map.167 = (f32[2,6,64,128]{3,2,1,0:T(8,128)S(1)}, bf16[2,2,6,64,128]{4,3,2,1,0:T(8,128)(2,1)S(1)}, f32[2,20,8,128]{3,2,1,0:T(8,128)S(1)}, bf16[128,1024]{...) custom-call(bf16[8,240,128]{2,1,0:T(8,128)(2,1)S(1)} %all-to-all-don, ...), custom_call_target="tpu_custom_call" | custom-call | tf_op jit(solution)/shard_map/pallas_call | solution.py:759
  20.8 11.3 %all_to_all.20.received = bf16[32,8,128]{2,1,0:T(8,128)(2,1)S(1)} all-to-all(bf16[32,8,128]{2,1,0:T(8,128)(2,1)S(1)} %get-tuple-element.25), channel_id=1, replica_groups=mesh['fx'=2,'fy'=4,'st'=4] {'fx','fy','st'}, dimensions={0} | all-to-all | bytes 131072 | tf_op jit(solution)/shard_map/all_to_all | solution.py:812
  32.0 0.0 copy-done.2
  32.0 4.1 %shard_map.168 = (f32[2,6,64,128]{3,2,1,0:T(8,128)S(1)}, bf16[2,384,128]{2,1,0:T(8,128)(2,1)S(1)}, bf16[32,16,128]{2,1,0:T(8,128)(2,1)S(1)}) custom-call(bf16[32,8,128]{2,1,0:T(8,128)(2,1)S(1)} %all_to_all.20.received, f32[2,6,64,128]{3,2,1,0:T(8,128)S(1)} %get-tuple-element.26.adjoint_in, bf16[2,2,6,64,128]{4,3,2,1,0:T(8,128)(2,1)S(1)} %get-tuple-element.27.rhs, ...), custom_call_target="tpu_custom_call" | custom-call | tf_op jit(solution)/shard_map/pallas_call | solution.py:759
  36.1 10.1 %all_to_all.21.received = bf16[32,16,128]{2,1,0:T(8,128)(2,1)S(1)} all-to-all(bf16[32,16,128]{2,1,0:T(8,128)(2,1)S(1)} %get-tuple-element.34), channel_id=1, replica_groups=mesh['fx'=2,'fy'=4,'st'=4] {'fx','fy','st'}, dimensions={0} | all-to-all | bytes 262144 | tf_op jit(solution)/shard_map/all_to_all | solution.py:823
  46.2 3.4 %shard_map.169 = (bf16[8,96,128]{2,1,0:T(8,128)(2,1)S(1)}, f32[4,4,384]{2,1,0:T(4,128)}, f32[4,4,384]{2,1,0:T(4,128)}) custom-call(bf16[32,16,128]{2,1,0:T(8,128)(2,1)S(1)} %all_to_all.21.received, f32[2,6,64,128]{3,2,1,0:T(8,128)S(1)} %get-tuple-element.35.tangent_in, bf16[2,384,128]{2,1,0:T(8,128)(2,1)S(1)} %get-tuple-element.36.adjoint_rounded, ...), custom_call_target="tpu_custom_call" | custom-call | tf_op jit(solution)/shard_map/pallas_call | solution.py:759
  49.6 8.6 %all_to_all.22.received = bf16[8,96,128]{2,1,0:T(8,128)(2,1)S(1)} all-to-all(bf16[8,96,128]{2,1,0:T(8,128)(2,1)S(1)} %get-tuple-element.37), channel_id=1, replica_groups=mesh['fx'=2,'fy'=4,'st'=4] {'fx','fy'}, dimensions={0} | all-to-all | bytes 393216 | tf_op jit(solution)/shard_map/all_to_all | solution.py:835
  58.2 1.1 %shard_map.170 = (bf16[6,64,128]{2,1,0:T(8,128)(2,1)}, bf16[6,64,128]{2,1,0:T(8,128)(2,1)}) custom-call(bf16[8,96,128]{2,1,0:T(8,128)(2,1)S(1)} %all_to_all.22.received), custom_call_target="tpu_custom_call" | custom-call | tf_op jit(solution)/shard_map/pallas_call | solution.py:759
Async XLA Ops:
  0.6 8.5 %copy-start.1 = (f32[4,4,384]{2,1,0:T(4,128)S(1)}, f32[4,4,384]{2,1,0:T(4,128)}, u32[]{:S(2)}) copy-start(f32[4,4,384]{2,1,0:T(4,128)} %load.5) | copy-start | bytes 73732
  0.6 8.5 %copy-start = (bf16[4,384,384]{2,1,0:T(8,128)(2,1)S(1)}, bf16[4,384,384]{2,1,0:T(8,128)(2,1)}, u32[]{:S(2)}) copy-start(bf16[4,384,384]{2,1,0:T(8,128)(2,1)} %inverse.5) | copy-start | bytes 3538948
  0.7 8.5 %copy-start.4 = (bf16[3,64,64]{2,1,0:T(8,128)(2,1)S(1)}, bf16[3,64,64]{2,1,0:T(8,128)(2,1)}, u32[]{:S(2)}) copy-start(bf16[3,64,64]{2,1,0:T(8,128)(2,1)} %deriv.1) | copy-start | bytes 73732
  3.9 14.6 %copy-start.3 = (bf16[6,384]{1,0:T(8,128)(2,1)S(1)}, bf16[6,384]{1,0:T(8,128)(2,1)}, u32[]{:S(2)}) copy-start(bf16[6,384]{1,0:T(8,128)(2,1)} %coupling.5) | copy-start | bytes 13828
  3.9 14.6 %copy-start.5 = (f32[6]{0:T(128)S(1)}, f32[6]{0:T(128)}, u32[]{:S(2)}) copy-start(f32[6]{0:T(128)} %penalty.5) | copy-start | bytes 76
  3.9 14.6 %all-to-all-start = ((bf16[8,240,128]{2,1,0:T(8,128)(2,1)}), bf16[8,240,128]{2,1,0:T(8,128)(2,1)S(1)}, u32[]{:S(2)}, u32[]{:S(2)}) async-start(bf16[8,240,128]{2,1,0:T(8,128)(2,1)} %shard_map.165), calls=%async_computation | async-start | bytes 983040 | tf_op jit(solution)/shard_map/all_to_all | solution.py:797
  9.1 22.9 %copy-start.2 = (f32[4,4,384]{2,1,0:T(4,128)S(1)}, f32[4,4,384]{2,1,0:T(4,128)}, u32[]{:S(2)}) copy-start(f32[4,4,384]{2,1,0:T(4,128)} %shell_rhs.3) | copy-start | bytes 73732

commit v4 on v3

--- a/solution.py
+++ b/solution.py
@@ -239,6 +239,30 @@
     return x if shift == 0 else pltpu.roll(x, shift, 1)
 
 
+def swap_masks(count):
+    group = _iota((16, LANES), 1) // (LANES // count)
+    masks, step = [], 1
+    while step < count:
+        has = (group // step) % 2
+        masks.append((_flag(has == 0).astype(BF16), _flag(has == 1).astype(BF16)))
+        step *= 2
+    return masks
+
+
+def swap_groups(parts, masks):
+    width = LANES // len(parts)
+    for bit, (without, having) in enumerate(masks):
+        step = 1 << bit
+        swapped = list(parts)
+        for a in range(len(parts)):
+            if not a & step:
+                x, y = parts[a], parts[a | step]
+                swapped[a] = x * without + _roll(y, width * step) * having
+                swapped[a | step] = y * having + _roll(x, -width * step) * without
+        parts = swapped
+    return parts
+
+
 class Plan:
     def __init__(self, nx, ny, ns, nv, span, panels, width):
         self.nx, self.ny, self.ns, self.nv = nx, ny, ns, nv
@@ -250,14 +274,14 @@
         self.held = panels // ns
         self.nodes = panels * PN
         self.tiles = width // LANES
-        self.narrow = LANES // self.groups
         self.deps = 3 * nv * nv
         self.granules = 3 * nv + 1
         self.per = -(-self.granules // 4)
         self.field_rows = nv * 16
-        self.rows = 2 * self.field_rows + self.per * 8 + 8
+        self.rows = 2 * self.field_rows + self.per * 8
         self.depth = 7 * NP + 32
         self.slots = ny * LANES
+        self.shell_rows = 2 * ns * self.tiles
 
     def rank(self):
         return lax.axis_index("fx") * self.ny + lax.axis_index("fy")
@@ -266,7 +290,7 @@
 def fits(nx, ny, ns, local_shape, slots, panels, width):
     members, nv, points, size_x, size_y, span = local_shape
     groups = nx * ny
-    if members != 1 or (size_x, size_y) != (1, 1) or points != NP or nv > 8 or nv % 2:
+    if members != 1 or (size_x, size_y) != (1, 1) or points != NP or nv > 6 or nv % 2:
         return False
     if span != LANES or slots != LANES or span % groups or LANES % ny or LANES % groups:
         return False
@@ -276,19 +300,21 @@
     if own * 8 != LANES or width != SDOF * PN or width % LANES or SDOF > 8:
         return False
     held = panels // ns
-    if panels % ns or panels != 16 or groups % held or ns > 4:
+    if panels % ns or panels != 16 or 8 % held or groups % held or groups < 2 * held:
         return False
-    return (held + 1) * (width // LANES) <= 16 and 8 % held == 0
-
-
-def shell_solve_rows(plan, rhs, inverse_ref):
-    rows = rhs.shape[0]
-    rounded = rhs.astype(BF16)
-    member = _iota((rows, plan.width), 0) % plan.held
-    result = jnp.zeros((rows, plan.width), F32)
-    for panel in range(plan.held):
-        result = jnp.where(member == panel, _nt(rounded, inverse_ref[panel]), result)
-    return result
+    return ns <= 4 and 2 * (width // LANES) <= 8
+
+
+def solve_steps(plan, received, load, shell_rhs, inverse, mine, result):
+    def first():
+        rows = member_rows(plan, shell_rhs, mine) - read_own_loads(plan, received)
+        result.append(_nt(rows.astype(BF16), inverse[mine]))
+
+    def second():
+        rows = member_rows(plan, load, mine) + result[0]
+        result.append(_nt(rows.astype(BF16), inverse[mine]))
+
+    return [first, second]
 
 
 def member_rows(plan, ref, panel):
@@ -305,10 +331,6 @@
     for copy in copies:
         copy.start()
     return copies
-
-
-def stacked(ref, count):
-    return jnp.concatenate([ref[d] for d in range(count)], axis=0)
 
 
 def pack_kernel(
@@ -380,11 +402,13 @@
         (node[...] - panel * PN + PN * upper).astype(F32),
         coarse,
         scaled - coarse,
-        jnp.zeros((3, LANES), F32),
     ]
+    row = _iota((8, LANES), 0)
+    zero = jnp.zeros((8, LANES), F32)
+    table = [jnp.where(row == 6, line, 0.0) for line in table] + [zero] * (plan.per - len(table))
     table = jnp.concatenate(table, axis=0)
     for dest in range(plan.groups):
-        block = jnp.concatenate([window_of(quarter, dest, F32), table], axis=0)
+        block = window_of(quarter, dest, F32) + table
         first = 2 * plan.field_rows
         out[dest, pl.ds(first, plan.rows - first), :] = block.astype(BF16)
     send(2 * plan.field_rows, plan.rows - 2 * plan.field_rows)
@@ -406,7 +430,7 @@
     return rows
 
 
-def sweeps(plan, count, state, source, table, matrix, transposed, coef, rows):
+def sweeps(plan, count, state, source, table, matrix, transposed, coef, rows, steps=()):
     nv, nx, window = plan.nv, plan.nx, plan.window
     lane = _iota((16, LANES), 1)
     not_last = _flag(lane < LANES - window).astype(BF16)
@@ -424,6 +448,8 @@
     for s in range(count):
         now, later = s % 2, (s + 1) % 2
         for h in range(nx):
+            if steps:
+                steps.pop(0)()
             own = [[plane(now, h, b, i) for i in range(4)] for b in range(nv)]
             for a0 in range(0, nv, 2):
                 stacks = []
@@ -478,35 +504,23 @@
     return low, high
 
 
-def first_exchange(plan, low, high, solved, out):
-    share = plan.groups // plan.held
+def write_exchange(plan, low, high, solved, out):
+    share, tiles = plan.groups // plan.held, plan.tiles
+    row = _iota((8, LANES), 0)
     for dest in range(plan.ns):
+        tail = jnp.zeros((8, LANES), F32)
+        for t in range(tiles):
+            part = pltpu.roll(solved[:, LANES * t : LANES * (t + 1)], (tiles + t - dest) % 8, 0)
+            tail = jnp.where(row == tiles + t, part, tail)
         for panel in range(plan.held):
             q = dest * plan.held + panel
-            rows = [(low[t] if q < 8 else high[t])[q % 8 : q % 8 + 1] for t in range(plan.tiles)]
-            line = solved[dest : dest + 1]
-            rows += [line[:, LANES * t : LANES * (t + 1)] for t in range(plan.tiles)]
-            rows.append(jnp.zeros((8 - 2 * plan.tiles, LANES), F32))
-            block = jnp.concatenate(rows, axis=0).astype(BF16)
+            block = tail
+            for t in range(tiles):
+                part = pltpu.roll(low[t] if q < 8 else high[t], (t - q) % 8, 0)
+                block = jnp.where(row == t, part, block)
+            block = block.astype(BF16)
             for g in range(panel * share, (panel + 1) * share):
                 out[g * plan.ns + dest] = block
-
-
-def second_exchange(plan, low, high, solved, out):
-    for dest in range(plan.ns):
-        rows = []
-        first = dest * plan.held
-        for t in range(plan.tiles):
-            part = low[t] if first < 8 else high[t]
-            rows.append(part[first % 8 : first % 8 + plan.held])
-        line = solved[dest : dest + 1]
-        rows += [line[:, LANES * t : LANES * (t + 1)] for t in range(plan.tiles)]
-        used = (plan.held + 1) * plan.tiles
-        if used < 16:
-            rows.append(jnp.zeros((16 - used, LANES), F32))
-        block = jnp.concatenate(rows, axis=0).astype(BF16)
-        for g in range(plan.groups):
-            out[g * plan.ns + dest] = block
 
 
 def summed(plan, received):
@@ -524,15 +538,6 @@
     tiles = []
     for t in range(plan.tiles):
         rows = [x[t : t + 1] for x in totals] + [jnp.zeros((8 - plan.ns, LANES), F32)]
-        tiles.append(jnp.concatenate(rows, axis=0))
-    return jnp.concatenate(tiles, axis=1)
-
-
-def read_loads(plan, received):
-    totals = summed(plan, received)
-    tiles = []
-    for t in range(plan.tiles):
-        rows = [x[plan.held * t : plan.held * (t + 1)] for x in totals]
         tiles.append(jnp.concatenate(rows, axis=0))
     return jnp.concatenate(tiles, axis=1)
 
@@ -599,45 +604,41 @@
 ):
     nv, window, nx, ny = plan.nv, plan.window, plan.nx, plan.ny
     rank = plan.rank()
-    lane = _iota((1, LANES), 1)
-    group = [_flag(lane // window == y) for y in range(ny)]
-
-    def regroup(parts, k, dtype):
-        total = None
-        for y in range(ny):
-            term = _roll(parts[y], window * (y - k)) * group[y].astype(dtype)
-            total = term if total is None else total + term
-        return total
-
+    masks = swap_masks(ny)
     for h in range(nx):
         for f in range(2):
             for a in range(nv):
                 first = (f * nv + a) * 16
                 parts = [received[h * ny + y, pl.ds(first, 16), :] for y in range(ny)]
-                for k in range(4):
-                    rhs[f, h, a, pl.ds(16 * k, 16), :] = regroup(parts, k, BF16)
+                for k, part in enumerate(swap_groups(parts, masks)):
+                    rhs[f, h, a, pl.ds(16 * k, 16), :] = part
         first = 2 * plan.field_rows
-        tails = [
-            received[h * ny + y, pl.ds(first, plan.rows - first), :] for y in range(ny)
-        ]
-        for k in range(4):
-            block = regroup(tails, k, BF16).astype(F32)
+        count = plan.rows - first
+        tails = [received[h * ny + y, pl.ds(first, count), :] for y in range(ny)]
+        info = [x.astype(F32).reshape(plan.per, 8, LANES) for x in tails]
+        pieces = [[] for _ in range(ny)]
+        for r in range(0, count, 16):
+            size = min(16, count - r)
+            parts = [received[h * ny + y, pl.ds(first + r, size), :] for y in range(ny)]
+            short = [(a[:size], b[:size]) for a, b in masks]
+            for k, part in enumerate(swap_groups(parts, short)):
+                pieces[k] += [part.astype(F32)[i : i + 8] for i in range(0, size, 8)]
+        for k in range(ny):
             for i in range(plan.per):
-                table[h, k * plan.per + i] = block[8 * i : 8 * (i + 1)]
-        info = [x.astype(F32)[plan.per * 8 :] for x in tails]
+                table[h, k * plan.per + i] = pieces[k][i]
         place = _iota((LANES, LANES), 0)
-        spot = _iota((8, LANES), 0)
+        row = _iota((8, LANES), 0)
         for y in range(ny):
-            at = info[y]
-            where = (at[0:1] - (plan.own * rank - plan.halo).astype(F32)).astype(jnp.int32)
+            elem, tile, spot, coarse, fine = [info[y][i, 6:7, :] for i in range(5)]
+            where = (elem - (plan.own * rank - plan.halo).astype(F32)).astype(jnp.int32)
             within = (where >= 0) & (where < window)
             target = jnp.where(within, where + y * window, -1)
             columns = pl.ds(LANES * y, LANES)
             places[h, :, columns] = _flag(place == target).astype(BF16)
             columns = pl.ds(plan.slots * h + LANES * y, LANES)
-            weights[:, columns] = at[3:4] + at[4:5]
-            tile_hot[:, columns] = _flag(spot == at[1:2].astype(jnp.int32))
-            hot[:, columns] = _flag(place == at[2:3].astype(jnp.int32)).astype(BF16)
+            weights[:, columns] = coarse + fine
+            tile_hot[:, columns] = _flag(row == tile.astype(jnp.int32))
+            hot[:, columns] = _flag(place == spot.astype(jnp.int32)).astype(BF16)
 
     rows = coefficients(plan, penalty, coef, rank)
     for h in range(nx):
@@ -648,24 +649,22 @@
     last = sweeps(plan, FSWEEP - 1, state, source, table, backward[...], True, coef, rows)
     values = [state[last, h].reshape(nv * NP, LANES).astype(BF16) for h in range(nx)]
     low, high = node_loads(plan, couple_rows(coupling), values, hot, tile_hot, places, weights)
-    first_exchange(plan, low, high, solved[...], out)
+    write_exchange(plan, low, high, solved[...], out)
     adjoint[...] = state[last]
 
 
 def second_kernel(
     plan, received, adjoint_in, rhs, table, hot, tile_hot, places, weights, forward, backward,
     coupling, load, shell_rhs, inverse, penalty,
-    tangent, adjoint_rounded, out,
+    tangent, adjoint_last, out,
     state, source, coef, scr, shell_scr,
 ):
     nv, nx = plan.nv, plan.nx
     rank = plan.rank()
     mine = rank // (plan.groups // plan.held)
     rows = coefficients(plan, penalty, coef, rank)
-    shell = member_rows(plan, shell_rhs, mine) - read_own_loads(plan, received)
-    shell = _nt(shell.astype(BF16), inverse[mine])
-    shell = member_rows(plan, load, mine) + shell
-    solved = _nt(shell.astype(BF16), inverse[mine])
+    result = []
+    steps = solve_steps(plan, received, load, shell_rhs, inverse, mine, result)
     couple = couple_rows(coupling)
     push_force(
         plan, received, plan.tiles, hot, tile_hot, places, weights, couple, rhs, shell_scr, scr,
@@ -674,7 +673,7 @@
     for h in range(nx):
         for a in range(nv):
             state[0, h, a] = source[h, a]
-    last = sweeps(plan, FSWEEP - 1, state, source, table, forward[...], False, coef, rows)
+    last = sweeps(plan, FSWEEP - 1, state, source, table, forward[...], False, coef, rows, steps)
     tangent[...] = state[last]
     for h in range(nx):
         for a in range(nv):
@@ -687,64 +686,65 @@
     values = []
     for h in range(nx):
         value = state[last, h].reshape(nv * NP, LANES).astype(BF16)
-        adjoint_rounded[h] = value
+        adjoint_last[h] = value
         values.append(value)
     low, high = node_loads(plan, couple, values, hot, tile_hot, places, weights)
-    second_exchange(plan, low, high, solved, out)
+    write_exchange(plan, low, high, result[1], out)
 
 
 def third_kernel(
-    plan, received, tangent_in, adjoint_rounded, rhs, table, hot, tile_hot, places, weights, forward,
+    plan, received, tangent_in, adjoint_last, rhs, table, hot, tile_hot, places, weights, forward,
     coupling, load, shell_rhs, inverse, penalty,
-    out, shell_tangent, shell_adjoint,
+    out,
     state, source, coef, scr, shell_scr,
 ):
-    nv, nx, ny = plan.nv, plan.nx, plan.ny
-    rank = plan.rank()
+    nv, nx, ny, ns = plan.nv, plan.nx, plan.ny, plan.ns
+    rank, share = plan.rank(), plan.groups // plan.held
     rows = coefficients(plan, penalty, coef, rank)
-    shell = stacked(shell_rhs, plan.ns) - read_loads(plan, received)
-    shell = shell_solve_rows(plan, shell, inverse)
-    solved = shell_solve_rows(plan, stacked(load, plan.ns) + shell, inverse)
-    for d in range(plan.ns):
-        shell_adjoint[d] = shell[plan.held * d : plan.held * (d + 1)]
-        shell_tangent[d] = solved[plan.held * d : plan.held * (d + 1)]
+    result = []
+    steps = solve_steps(plan, received, load, shell_rhs, inverse, rank // share, result)
     push_force(
-        plan, received, plan.held * plan.tiles, hot, tile_hot, places, weights,
+        plan, received, plan.tiles, hot, tile_hot, places, weights,
         couple_rows(coupling), rhs, shell_scr, scr, source,
     )
     for h in range(nx):
         for a in range(nv):
             state[0, h, a] = tangent_in[h, a]
-    last = sweeps(plan, FSWEEP, state, source, table, forward[...], False, coef, rows)
+    last = sweeps(plan, FSWEEP, state, source, table, forward[...], False, coef, rows, steps)
+    shell = jnp.where(lax.rem(rank, share) == 0, result[0], result[1])
+    tiles = [shell[:ns, LANES * t : LANES * (t + 1)] for t in range(plan.tiles)]
+    shell = _split(jnp.concatenate(tiles, axis=0))
+    for dest in range(plan.groups):
+        out[dest, pl.ds(plan.field_rows, shell.shape[0]), :] = shell
     lane = _iota((16, LANES), 1)
-    narrow = plan.narrow
-    group = [_flag(lane // narrow == n).astype(BF16) for n in range(8)]
+    group = [_flag(lane // plan.own == n).astype(BF16) for n in range(plan.groups)]
     for h in range(nx):
         for a in range(nv):
             parts = [state[last, h, a, pl.ds(16 * i, 16), :].astype(BF16) for i in range(4)]
-            parts += [adjoint_rounded[h, pl.ds(a * NP + 16 * i, 16), :] for i in range(4)]
+            parts += [adjoint_last[h, pl.ds(a * NP + 16 * i, 16), :] for i in range(4)]
             for y in range(ny):
                 total = None
-                for n in range(8):
-                    shift = narrow * n - plan.window * y - plan.halo
+                for n in range(plan.groups):
+                    shift = plan.own * n - plan.window * y - plan.halo
                     term = _roll(parts[n], shift) * group[n]
                     total = term if total is None else total + term
                 out[h * ny + y, pl.ds(16 * a, 16), :] = total
 
 
-def last_kernel(plan, received, tangent, adjoint):
-    lane = _iota((16, LANES), 1)
-    narrow = plan.narrow
-    group = [_flag(lane // narrow == g).astype(BF16) for g in range(plan.groups)]
+def last_kernel(plan, received, tangent, adjoint, shell_tangent, shell_adjoint):
+    share, ns = plan.groups // plan.held, plan.ns
+    for panel in range(plan.held):
+        for i, ref in enumerate((shell_adjoint, shell_tangent)):
+            block = received[panel * share + i, pl.ds(plan.field_rows, plan.shell_rows), :]
+            block = _fold(block.astype(F32))
+            for t in range(plan.tiles):
+                columns = pl.ds(LANES * t, LANES)
+                ref[:, panel, columns] = block[ns * t : ns * (t + 1)]
+    masks = swap_masks(plan.groups)
     for a in range(plan.nv):
         parts = [received[g, pl.ds(16 * a, 16), :] for g in range(plan.groups)]
-        for f, ref in enumerate((tangent, adjoint)):
-            for i in range(4):
-                total = None
-                for g in range(plan.groups):
-                    term = _roll(parts[g], narrow * (g - 4 * f - i)) * group[g]
-                    total = term if total is None else total + term
-                ref[a, pl.ds(16 * i, 16), :] = total
+        for n, part in enumerate(swap_groups(parts, masks)):
+            (tangent, adjoint)[n // 4][a, pl.ds(16 * (n % 4), 16), :] = part
 
 
 def call(kernel, plan, out_shape, scratch, copies, on_chip, in_hbm, scalars, limit=KERNEL_VMEM,
@@ -810,9 +810,9 @@
         [both, state, coef], 0, (slab, backward, solved, coupling), (), (penalty,),
     )
     received = lax.all_to_all(sent, everyone, split_axis=0, concat_axis=0, tiled=True)
-    tangent, adjoint_rounded, sent = call(
+    tangent, adjoint_last, sent = call(
         second_kernel, plan,
-        [state, ((nx, nv * NP, LANES), BF16), ((groups * ns, 16, LANES), BF16)],
+        [state, ((nx, nv * NP, LANES), BF16), ((groups * ns, 8, LANES), BF16)],
         [both, state, coef, scr, shell_rows], 0,
         (
             received, adjoint, rhs, table, hot, tile_hot, places, weights, forward, backward,
@@ -821,20 +821,21 @@
         (), (penalty,),
     )
     received = lax.all_to_all(sent, everyone, split_axis=0, concat_axis=0, tiled=True)
-    shell_shape = (shell_load.shape, F32)
-    sent, shell_tangent, shell_adjoint = call(
+    (sent,) = call(
         third_kernel, plan,
-        [((groups, plan.field_rows, LANES), BF16), shell_shape, shell_shape],
+        [((groups, plan.field_rows + plan.shell_rows, LANES), BF16)],
         [both, state, coef, scr, shell_rows], 0,
         (
-            received, tangent, adjoint_rounded, rhs, table, hot, tile_hot, places, weights,
+            received, tangent, adjoint_last, rhs, table, hot, tile_hot, places, weights,
             forward, coupling, shell_load, shell_adjoint_rhs, shell_inverse,
         ),
         (), (penalty,),
     )
     received = lax.all_to_all(sent, flow, split_axis=0, concat_axis=0, tiled=True)
-    tangent, adjoint = call(
-        last_kernel, plan, [((nv, NP, LANES), BF16)] * 2, [], 0, (received,), (), ()
+    shell_shape = (shell_load.shape, F32)
+    tangent, adjoint, shell_tangent, shell_adjoint = call(
+        last_kernel, plan, [((nv, NP, LANES), BF16)] * 2 + [shell_shape] * 2, [], 0,
+        (received,), (), (),
     )
     return (
         tangent.reshape(tangent_rhs.shape), adjoint.reshape(adjoint_rhs.shape),

time: 59.7 us -> 58.2 us (0.975)
  Pallas kernels: 13.6 us -> 12.7 us
    pallas_call x6, Pallas kernels: 13.6 us -> 12.7 us  [call(): pl.pallas_call(functools.partial(kernel, plan), out_shape=[jax.ShapeDtype...]
    all_to_all x2, blocking collectives: 21.4 us -> 20.5 us  [slab_body(): lax.all_to_all(sent, everyone, split_axis=0, concat_axis=0, tiled=True)]
where the time goes in v4:
time: 58.2 us; the launch traced here: 57.9 us
  blocking collectives  29.6 us (51%)
  Pallas kernels  12.7 us (22%)
  waiting for transfers between devices  8.92 us (15%)
  starting transfers between devices  5.21 us (9%)
  between operations  1.48 us (3%)
    all_to_all x2, blocking collectives, slab_body(): lax.all_to_all(sent, everyone, split_axis=0, concat_axis=0, tiled=True)  20.5 us
    pallas_call x6, Pallas kernels, call(): pl.pallas_call(functools.partial(kernel, plan), out_shape=[jax.ShapeDtype...  12.7 us
    all_to_all x1, blocking collectives, slab_body(): lax.all_to_all(sent, flow, split_axis=0, concat_axis=0, tiled=True)  9.14 us
    all_to_all x1, waiting for transfers between devices, slab_body(): slab = lax.all_to_all(packed, flow, split_axis=0, concat_axis=0, tiled=True)  8.92 us
    all_to_all x1, starting transfers between devices, slab_body(): slab = lax.all_to_all(packed, flow, split_axis=0, concat_axis=0, tiled=True)  5.21 us
  transfers between devices with their start and end apart: 1, of which 1 were waited for; matrix products, arithmetic and copies ran while one was open for 0% of the time, Pallas kernels for 0%

profile of v4, /device:TPU:0, one launch (start us, length us, event | category | flops | bytes accessed | tf_op | source)
XLA Modules:
  0.0 57.9 jit_solution(9390407493483207346)
XLA Ops:
  0.6 0.0 copy-start.1
  0.6 0.0 copy-start
  0.7 0.0 copy-start.4
  1.4 2.5 %shard_map.165 = bf16[8,232,128]{2,1,0:T(8,128)(2,1)} custom-call(bf16[6,64,128]{2,1,0:T(8,128)(2,1)} %bitcast.12, bf16[6,64,128]{2,1,0:T(8,128)(2,1)} %bitcast.13, bf16[3,6,6,128]{3,2,1,0:T(8,128)(2,1)} %bitcast.14, f32[6,1,128]{2,1,0:T(1,128)} %bitcast.15, s32[1,128]{1,0:T(1,128)} %elem_hbm.1, s32[1,128]{1,0:T(1,128)} %node_hbm.1, f32[1,128]{1,0:T(1,128)} %weight_hbm.1, ...), custom_call_target="tpu_custom_call" | custom-call | tf_op jit(solution)/shard_map/pallas_call | solution.py:759
  3.9 0.0 copy-start.3
  3.9 0.0 copy-start.5
  3.9 5.2 %all-to-all-start = ((bf16[8,232,128]{2,1,0:T(8,128)(2,1)}), bf16[8,232,128]{2,1,0:T(8,128)(2,1)S(1)}, u32[]{:S(2)}, u32[]{:S(2)}) async-start(bf16[8,232,128]{2,1,0:T(8,128)(2,1)} %shard_map.165), calls=%async_computation | async-start | bytes 950272 | tf_op jit(solution)/shard_map/all_to_all | solution.py:797
  9.1 0.0 copy-done.1
  9.1 0.0 copy-done
  9.1 0.0 copy-done.4
  9.1 0.0 copy-start.2
  9.2 0.2 shard_map.166
  9.4 8.9 %all-to-all-done.received = bf16[8,232,128]{2,1,0:T(8,128)(2,1)S(1)} async-done(((bf16[8,232,128]{2,1,0:T(8,128)(2,1)}), bf16[8,232,128]{2,1,0:T(8,128)(2,1)S(1)}, u32[]{:S(2)}, u32[]{:S(2)}) %all-to-all-start) | async-done | bytes 475168 | tf_op jit(solution)/shard_map/all_to_all | solution.py:797
  18.3 0.0 copy-done.3
  18.3 0.0 copy-done.5
  18.3 2.4 %shard_map.167 = (f32[2,6,64,128]{3,2,1,0:T(8,128)S(1)}, bf16[2,2,6,64,128]{4,3,2,1,0:T(8,128)(2,1)S(1)}, f32[2,20,8,128]{3,2,1,0:T(8,128)S(1)}, bf16[128,1024]{...) custom-call(bf16[8,232,128]{2,1,0:T(8,128)(2,1)S(1)} %all-to-all-don, ...), custom_call_target="tpu_custom_call" | custom-call | tf_op jit(solution)/shard_map/pallas_call | solution.py:759
  20.7 11.3 %all_to_all.20.received = bf16[32,8,128]{2,1,0:T(8,128)(2,1)S(1)} all-to-all(bf16[32,8,128]{2,1,0:T(8,128)(2,1)S(1)} %get-tuple-element.24), channel_id=1, replica_groups=mesh['fx'=2,'fy'=4,'st'=4] {'fx','fy','st'}, dimensions={0} | all-to-all | bytes 131072 | tf_op jit(solution)/shard_map/all_to_all | solution.py:812
  31.9 0.0 copy-done.2
  31.9 4.0 %shard_map.168 = (f32[2,6,64,128]{3,2,1,0:T(8,128)S(1)}, bf16[2,384,128]{2,1,0:T(8,128)(2,1)S(1)}, bf16[32,8,128]{2,1,0:T(8,128)(2,1)S(1)}) custom-call(bf16[32,8,128]{2,1,0:T(8,128)(2,1)S(1)} %all_to_all.20.received, f32[2,6,64,128]{3,2,1,0:T(8,128)S(1)} %get-tuple-element.25.adjoint_in, bf16[2,2,6,64,128]{4,3,2,1,0:T(8,128)(2,1)S(1)} %get-tuple-element.26.rhs, ...), custom_call_target="tpu_custom_call" | custom-call | tf_op jit(solution)/shard_map/pallas_call | solution.py:759
  36.0 9.2 %all_to_all.21.received = bf16[32,8,128]{2,1,0:T(8,128)(2,1)S(1)} all-to-all(bf16[32,8,128]{2,1,0:T(8,128)(2,1)S(1)} %get-tuple-element.33), channel_id=1, replica_groups=mesh['fx'=2,'fy'=4,'st'=4] {'fx','fy','st'}, dimensions={0} | all-to-all | bytes 131072 | tf_op jit(solution)/shard_map/all_to_all | solution.py:823
  45.1 2.6 %shard_map.169 = bf16[8,120,128]{2,1,0:T(8,128)(2,1)S(1)} custom-call(bf16[32,8,128]{2,1,0:T(8,128)(2,1)S(1)} %all_to_all.21.received, f32[2,6,64,128]{3,2,1,0:T(8,128)S(1)} %get-tuple-element.34.tangent_in, bf16[2,384,128]{2,1,0:T(8,128)(2,1)S(1)} %get-tuple-element.35.adjoint_last, bf16[2,2,6,64,128]{4,3,2,1,0:T(8,128)(2,1)S(1)} %get-tuple-element.26.rhs, ...), custom_call_target="tpu_custom_call" | custom-call | tf_op jit(solution)/shard_map/pallas_call | solution.py:759
  47.8 9.1 %all_to_all.22.received = bf16[8,120,128]{2,1,0:T(8,128)(2,1)S(1)} all-to-all(bf16[8,120,128]{2,1,0:T(8,128)(2,1)S(1)} %shard_map.169), channel_id=1, replica_groups=mesh['fx'=2,'fy'=4,'st'=4] {'fx','fy'}, dimensions={0} | all-to-all | bytes 491520 | tf_op jit(solution)/shard_map/all_to_all | solution.py:834
  56.9 1.0 %shard_map.170 = (bf16[6,64,128]{2,1,0:T(8,128)(2,1)}, bf16[6,64,128]{2,1,0:T(8,128)(2,1)}, f32[4,4,384]{2,1,0:T(4,128)}, f32[4,4,384]{2,1,0:T(4,128)}) custom-call(bf16[8,120,128]{2,1,0:T(8,128)(2,1)S(1)} %all_to_all.22.received), custom_call_target="tpu_custom_call" | custom-call | tf_op jit(solution)/shard_map/pallas_call | solution.py:759
Async XLA Ops:
  0.6 8.5 %copy-start.1 = (f32[4,4,384]{2,1,0:T(4,128)S(1)}, f32[4,4,384]{2,1,0:T(4,128)}, u32[]{:S(2)}) copy-start(f32[4,4,384]{2,1,0:T(4,128)} %load.5) | copy-start | bytes 73732
  0.6 8.5 %copy-start = (bf16[4,384,384]{2,1,0:T(8,128)(2,1)S(1)}, bf16[4,384,384]{2,1,0:T(8,128)(2,1)}, u32[]{:S(2)}) copy-start(bf16[4,384,384]{2,1,0:T(8,128)(2,1)} %inverse.5) | copy-start | bytes 3538948
  0.7 8.5 %copy-start.4 = (bf16[3,64,64]{2,1,0:T(8,128)(2,1)S(1)}, bf16[3,64,64]{2,1,0:T(8,128)(2,1)}, u32[]{:S(2)}) copy-start(bf16[3,64,64]{2,1,0:T(8,128)(2,1)} %deriv.1) | copy-start | bytes 73732
  3.9 14.4 %copy-start.3 = (bf16[6,384]{1,0:T(8,128)(2,1)S(1)}, bf16[6,384]{1,0:T(8,128)(2,1)}, u32[]{:S(2)}) copy-start(bf16[6,384]{1,0:T(8,128)(2,1)} %coupling.5) | copy-start | bytes 13828
  3.9 14.4 %copy-start.5 = (f32[6]{0:T(128)S(1)}, f32[6]{0:T(128)}, u32[]{:S(2)}) copy-start(f32[6]{0:T(128)} %penalty.5) | copy-start | bytes 76
  3.9 14.4 %all-to-all-start = ((bf16[8,232,128]{2,1,0:T(8,128)(2,1)}), bf16[8,232,128]{2,1,0:T(8,128)(2,1)S(1)}, u32[]{:S(2)}, u32[]{:S(2)}) async-start(bf16[8,232,128]{2,1,0:T(8,128)(2,1)} %shard_map.165), calls=%async_computation | async-start | bytes 950272 | tf_op jit(solution)/shard_map/all_to_all | solution.py:797
  9.1 22.8 %copy-start.2 = (f32[4,4,384]{2,1,0:T(4,128)S(1)}, f32[4,4,384]{2,1,0:T(4,128)}, u32[]{:S(2)}) copy-start(f32[4,4,384]{2,1,0:T(4,128)} %shell_rhs.3) | copy-start | bytes 73732

commit v5 on v4

--- a/solution.py
+++ b/solution.py
@@ -416,37 +416,35 @@
         copy.wait()
 
 
-def coefficients(plan, penalty, coef, rank):
+def coefficients(plan, penalty, coef, strength):
     point = _iota((NP, LANES), 0)
     ends = [point // 16, (point // 4) % 4, point % 4]
     faces = sum(_flag((e == 0) | (e == 3)) for e in ends)
     lane = _iota((16, LANES), 1)
-    z = plan.own * rank - plan.halo + lane % plan.window
+    z = plan.own * plan.rank() - plan.halo + lane % plan.window
     inside = _flag((z >= 0) & (z < plan.span))
-    rows = []
     for a in range(plan.nv):
         coef[a] = 0.5 - (0.5 * penalty[a]) * faces
-        rows.append((penalty[a] * inside).astype(BF16))
-    return rows
-
-
-def sweeps(plan, count, state, source, table, matrix, transposed, coef, rows, steps=()):
+        strength[a] = penalty[a] * inside
+
+
+def sweeps(plan, states, source, table, matrix, transposed, coef, strength, steps=()):
     nv, nx, window = plan.nv, plan.nx, plan.window
     lane = _iota((16, LANES), 1)
     not_last = _flag(lane < LANES - window).astype(BF16)
     not_first = _flag(lane >= window).astype(BF16)
     none = jnp.zeros((16, LANES), BF16)
-
-    def plane(now, h, a, i):
-        return state[now, h, a, pl.ds(16 * i, 16), :].astype(BF16)
+    rows = [strength[a].astype(BF16) for a in range(nv)]
+
+    def plane(state, h, a, i):
+        return state[h, a, pl.ds(16 * i, 16), :].astype(BF16)
 
     def flux(h, k, a, b):
         index, row = (k * nv + b, a) if transposed else (k * nv + a, b)
         line = table[h, index, pl.ds(row, 1), :]
         return jnp.broadcast_to(line, (16, LANES)).astype(BF16)
 
-    for s in range(count):
-        now, later = s % 2, (s + 1) % 2
+    for now, later in zip(states[:-1], states[1:]):
         for h in range(nx):
             if steps:
                 steps.pop(0)()
@@ -473,9 +471,12 @@
                     stacks.append(jnp.concatenate(parts, axis=0))
                 product = _nn(matrix, jnp.concatenate(stacks, axis=1))
                 for i, a in enumerate((a0, a0 + 1)):
-                    value = coef[a] * state[now, h, a] + source[h, a]
-                    state[later, h, a] = value + product[:, LANES * i : LANES * (i + 1)]
-    return count % 2
+                    value = coef[a] * now[h, a] + source[h, a]
+                    later[h, a] = value + product[:, LANES * i : LANES * (i + 1)]
+
+
+def chain(start, refs, count):
+    return [start] + [refs[(i - count) % len(refs)] for i in range(count)]
 
 
 def couple_rows(coupling):
@@ -575,7 +576,10 @@
             source[h, a] = 0.5 * value
 
 
-def prepare_kernel(plan, deriv, load, inverse, forward, backward, solved):
+def prepare_kernel(
+    plan, deriv, load, inverse, penalty, forward, backward, solved, coef, strength
+):
+    coefficients(plan, penalty, coef, strength)
     mine = plan.rank() // (plan.groups // plan.held)
     p, c = _iota((NP, plan.depth), 0), _iota((NP, plan.depth), 1)
     j, l = (p // 4) % 4, p % 4
@@ -598,9 +602,9 @@
 
 
 def first_kernel(
-    plan, received, backward, solved, coupling, penalty,
+    plan, received, backward, solved, coupling, coef, strength,
     adjoint, rhs, table, hot, tile_hot, places, weights, out,
-    state, source, coef,
+    middle, source,
 ):
     nv, window, nx, ny = plan.nv, plan.window, plan.nx, plan.ny
     rank = plan.rank()
@@ -640,29 +644,25 @@
             tile_hot[:, columns] = _flag(row == tile.astype(jnp.int32))
             hot[:, columns] = _flag(place == spot.astype(jnp.int32)).astype(BF16)
 
-    rows = coefficients(plan, penalty, coef, rank)
     for h in range(nx):
         for a in range(nv):
-            value = 0.5 * rhs[1, h, a].astype(F32)
-            source[h, a] = value
-            state[0, h, a] = value
-    last = sweeps(plan, FSWEEP - 1, state, source, table, backward[...], True, coef, rows)
-    values = [state[last, h].reshape(nv * NP, LANES).astype(BF16) for h in range(nx)]
+            source[h, a] = 0.5 * rhs[1, h, a].astype(F32)
+    states = chain(source, [middle, adjoint], FSWEEP - 1)
+    sweeps(plan, states, source, table, backward[...], True, coef, strength)
+    values = [adjoint[h].reshape(nv * NP, LANES).astype(BF16) for h in range(nx)]
     low, high = node_loads(plan, couple_rows(coupling), values, hot, tile_hot, places, weights)
     write_exchange(plan, low, high, solved[...], out)
-    adjoint[...] = state[last]
 
 
 def second_kernel(
     plan, received, adjoint_in, rhs, table, hot, tile_hot, places, weights, forward, backward,
-    coupling, load, shell_rhs, inverse, penalty,
+    coef, strength, coupling, load, shell_rhs, inverse,
     tangent, adjoint_last, out,
-    state, source, coef, scr, shell_scr,
+    first, second, source, scr, shell_scr,
 ):
     nv, nx = plan.nv, plan.nx
     rank = plan.rank()
     mine = rank // (plan.groups // plan.held)
-    rows = coefficients(plan, penalty, coef, rank)
     result = []
     steps = solve_steps(plan, received, load, shell_rhs, inverse, mine, result)
     couple = couple_rows(coupling)
@@ -670,22 +670,18 @@
         plan, received, plan.tiles, hot, tile_hot, places, weights, couple, rhs, shell_scr, scr,
         source,
     )
+    states = chain(source, [first, tangent], FSWEEP - 1)
+    sweeps(plan, states, source, table, forward[...], False, coef, strength, steps)
     for h in range(nx):
         for a in range(nv):
-            state[0, h, a] = source[h, a]
-    last = sweeps(plan, FSWEEP - 1, state, source, table, forward[...], False, coef, rows, steps)
-    tangent[...] = state[last]
-    for h in range(nx):
-        for a in range(nv):
-            extra = table[h, 3 * nv, a : a + 1, :] * state[last, h, a]
+            extra = table[h, 3 * nv, a : a + 1, :] * tangent[h, a]
             source[h, a] = 0.5 * (rhs[1, h, a].astype(F32) + extra)
-    for h in range(nx):
-        for a in range(nv):
-            state[0, h, a] = adjoint_in[h, a]
-    last = sweeps(plan, FSWEEP, state, source, table, backward[...], True, coef, rows)
+    states = chain(adjoint_in, [second, first], FSWEEP)
+    sweeps(plan, states, source, table, backward[...], True, coef, strength)
+    adjoint = states[-1]
     values = []
     for h in range(nx):
-        value = state[last, h].reshape(nv * NP, LANES).astype(BF16)
+        value = adjoint[h].reshape(nv * NP, LANES).astype(BF16)
         adjoint_last[h] = value
         values.append(value)
     low, high = node_loads(plan, couple, values, hot, tile_hot, places, weights)
@@ -694,23 +690,21 @@
 
 def third_kernel(
     plan, received, tangent_in, adjoint_last, rhs, table, hot, tile_hot, places, weights, forward,
-    coupling, load, shell_rhs, inverse, penalty,
+    coef, strength, coupling, load, shell_rhs, inverse,
     out,
-    state, source, coef, scr, shell_scr,
+    first, second, source, scr, shell_scr,
 ):
     nv, nx, ny, ns = plan.nv, plan.nx, plan.ny, plan.ns
     rank, share = plan.rank(), plan.groups // plan.held
-    rows = coefficients(plan, penalty, coef, rank)
     result = []
     steps = solve_steps(plan, received, load, shell_rhs, inverse, rank // share, result)
     push_force(
         plan, received, plan.tiles, hot, tile_hot, places, weights,
         couple_rows(coupling), rhs, shell_scr, scr, source,
     )
-    for h in range(nx):
-        for a in range(nv):
-            state[0, h, a] = tangent_in[h, a]
-    last = sweeps(plan, FSWEEP, state, source, table, forward[...], False, coef, rows, steps)
+    states = chain(tangent_in, [first, second], FSWEEP)
+    sweeps(plan, states, source, table, forward[...], False, coef, strength, steps)
+    tangent = states[-1]
     shell = jnp.where(lax.rem(rank, share) == 0, result[0], result[1])
     tiles = [shell[:ns, LANES * t : LANES * (t + 1)] for t in range(plan.tiles)]
     shell = _split(jnp.concatenate(tiles, axis=0))
@@ -720,7 +714,7 @@
     group = [_flag(lane // plan.own == n).astype(BF16) for n in range(plan.groups)]
     for h in range(nx):
         for a in range(nv):
-            parts = [state[last, h, a, pl.ds(16 * i, 16), :].astype(BF16) for i in range(4)]
+            parts = [tangent[h, a, pl.ds(16 * i, 16), :].astype(BF16) for i in range(4)]
             parts += [adjoint_last[h, pl.ds(a * NP + 16 * i, 16), :] for i in range(4)]
             for y in range(ny):
                 total = None
@@ -774,7 +768,6 @@
     nv, nx, ns, groups = plan.nv, plan.nx, plan.ns, plan.groups
     flow, everyone = ("fx", "fy"), ("fx", "fy", "st")
     state = ((nx, nv, NP, LANES), F32)
-    both = ((2, nx, nv, NP, LANES), F32)
     coef = ((nv, NP, LANES), F32)
     scr = ((8, 8, LANES), F32)
     shell_rows = ((plan.panels, plan.width), F32)
@@ -795,9 +788,10 @@
         len(inputs) + 3, (), inputs, (), None, pltpu.HBM,
     )
     slab = lax.all_to_all(packed, flow, split_axis=0, concat_axis=0, tiled=True)
-    forward, backward, solved = call(
-        prepare_kernel, plan, [matrix, matrix, ((8, plan.width), F32)],
-        [], 0, (deriv, shell_load, shell_inverse), (), (),
+    forward, backward, solved, coef, strength = call(
+        prepare_kernel, plan,
+        [matrix, matrix, ((8, plan.width), F32), coef, ((nv, 16, LANES), F32)],
+        [], 0, (deriv, shell_load, shell_inverse), (), (penalty,),
     )
     adjoint, rhs, table, hot, tile_hot, places, weights, sent = call(
         first_kernel, plan,
@@ -807,29 +801,29 @@
             ((nx, LANES, plan.slots), BF16), ((1, nx * plan.slots), F32),
             ((groups * ns, 8, LANES), BF16),
         ],
-        [both, state, coef], 0, (slab, backward, solved, coupling), (), (penalty,),
+        [state, state], 0, (slab, backward, solved, coupling, coef, strength), (), (),
     )
     received = lax.all_to_all(sent, everyone, split_axis=0, concat_axis=0, tiled=True)
     tangent, adjoint_last, sent = call(
         second_kernel, plan,
         [state, ((nx, nv * NP, LANES), BF16), ((groups * ns, 8, LANES), BF16)],
-        [both, state, coef, scr, shell_rows], 0,
+        [state, state, state, scr, shell_rows], 0,
         (
             received, adjoint, rhs, table, hot, tile_hot, places, weights, forward, backward,
-            coupling, shell_load, shell_adjoint_rhs, shell_inverse,
+            coef, strength, coupling, shell_load, shell_adjoint_rhs, shell_inverse,
         ),
-        (), (penalty,),
+        (), (),
     )
     received = lax.all_to_all(sent, everyone, split_axis=0, concat_axis=0, tiled=True)
     (sent,) = call(
         third_kernel, plan,
         [((groups, plan.field_rows + plan.shell_rows, LANES), BF16)],
-        [both, state, coef, scr, shell_rows], 0,
+        [state, state, state, scr, shell_rows], 0,
         (
             received, tangent, adjoint_last, rhs, table, hot, tile_hot, places, weights,
-            forward, coupling, shell_load, shell_adjoint_rhs, shell_inverse,
+            forward, coef, strength, coupling, shell_load, shell_adjoint_rhs, shell_inverse,
         ),
-        (), (penalty,),
+        (), (),
     )
     received = lax.all_to_all(sent, flow, split_axis=0, concat_axis=0, tiled=True)
     shell_shape = (shell_load.shape, F32)

time: 58.2 us -> 56.5 us (0.971)
  Pallas kernels: 12.7 us -> 11.5 us
    pallas_call x6, Pallas kernels: 12.7 us -> 11.5 us  [call(): pl.pallas_call(functools.partial(kernel, plan), out_shape=[jax.ShapeDtype...]
  transfers between devices with their start and end apart: 1 -> 1, of which waited for: 1 -> 1; matrix products, arithmetic and copies ran while one was open for 0% -> 0% of each run, Pallas kernels for 0% -> 1%
where the time goes in v5:
time: 56.5 us; the launch traced here: 56.2 us
  blocking collectives  29.6 us (52%)
  Pallas kernels  11.5 us (20%)
  waiting for transfers between devices  8.36 us (15%)
  starting transfers between devices  5.21 us (9%)
  between operations  1.48 us (3%)
    all_to_all x2, blocking collectives, slab_body(): lax.all_to_all(sent, everyone, split_axis=0, concat_axis=0, tiled=True)  20.5 us
    pallas_call x6, Pallas kernels, call(): pl.pallas_call(functools.partial(kernel, plan), out_shape=[jax.ShapeDtype...  11.5 us
    all_to_all x1, blocking collectives, slab_body(): lax.all_to_all(sent, flow, split_axis=0, concat_axis=0, tiled=True)  9.14 us
    all_to_all x1, waiting for transfers between devices, slab_body(): slab = lax.all_to_all(packed, flow, split_axis=0, concat_axis=0, tiled=True)  8.36 us
    all_to_all x1, starting transfers between devices, slab_body(): slab = lax.all_to_all(packed, flow, split_axis=0, concat_axis=0, tiled=True)  5.21 us
  transfers between devices with their start and end apart: 1, of which 1 were waited for; matrix products, arithmetic and copies ran while one was open for 0% of the time, Pallas kernels for 1%

profile of v5, /device:TPU:0, one launch (start us, length us, event | category | flops | bytes accessed | tf_op | source)
XLA Modules:
  0.0 56.2 jit_solution(12047452843717813625)
XLA Ops:
  0.6 0.0 copy-start.1
  0.6 0.0 copy-start
  0.7 0.0 copy-start.5
  0.7 0.0 copy-start.4
  1.4 2.5 %shard_map.165 = bf16[8,232,128]{2,1,0:T(8,128)(2,1)} custom-call(bf16[6,64,128]{2,1,0:T(8,128)(2,1)} %bitcast.12, bf16[6,64,128]{2,1,0:T(8,128)(2,1)} %bitcast.13, bf16[3,6,6,128]{3,2,1,0:T(8,128)(2,1)} %bitcast.14, f32[6,1,128]{2,1,0:T(1,128)} %bitcast.15, s32[1,128]{1,0:T(1,128)} %elem_hbm.1, s32[1,128]{1,0:T(1,128)} %node_hbm.1, f32[1,128]{1,0:T(1,128)} %weight_hbm.1, ...), custom_call_target="tpu_custom_call" | custom-call | tf_op jit(solution)/shard_map/pallas_call | solution.py:753
  3.9 0.0 copy-start.3
  3.9 5.2 %all-to-all-start = ((bf16[8,232,128]{2,1,0:T(8,128)(2,1)}), bf16[8,232,128]{2,1,0:T(8,128)(2,1)S(1)}, u32[]{:S(2)}, u32[]{:S(2)}) async-start(bf16[8,232,128]{2,1,0:T(8,128)(2,1)} %shard_map.165), calls=%async_computation | async-start | bytes 950272 | tf_op jit(solution)/shard_map/all_to_all | solution.py:790
  9.1 0.0 copy-done.1
  9.1 0.0 copy-done
  9.1 0.0 copy-done.5
  9.1 0.0 copy-done.4
  9.1 0.0 copy-start.2
  9.2 0.8 %shard_map.166 = (bf16[64,480]{1,0:T(8,128)(2,1)S(1)}, bf16[64,480]{1,0:T(8,128)(2,1)S(1)}, f32[8,384]{1,0:T(8,128)S(1)}, f32[6,64,128]{2,1,0:T(8,128)S(1)}, f32[6,16,128]{2,1,0:T(8,128)S(1)}) custom-call(bf16[3,64,64]{2,1,0:T(8,128)(2,1)S(1)} %copy-done.4, f32[4,4,384]{2,1,0:T(4,128)S(1)} %copy-done.1, bf16[4,384,384]{2,1,0:T(8,128)(2,1)S(1)} %copy-done, ...), custom_call_target="tpu_custom_call" | custom-call | tf_op jit(solution)/shard_map/pallas_call | solution.py:753
  9.9 8.4 %all-to-all-done.received = bf16[8,232,128]{2,1,0:T(8,128)(2,1)S(1)} async-done(((bf16[8,232,128]{2,1,0:T(8,128)(2,1)}), bf16[8,232,128]{2,1,0:T(8,128)(2,1)S(1)}, u32[]{:S(2)}, u32[]{:S(2)}) %all-to-all-start) | async-done | bytes 475168 | tf_op jit(solution)/shard_map/all_to_all | solution.py:790
  18.3 0.0 copy-done.3
  18.3 1.8 %shard_map.167 = (f32[2,6,64,128]{3,2,1,0:T(8,128)S(1)}, bf16[2,2,6,64,128]{4,3,2,1,0:T(8,128)(2,1)S(1)}, f32[2,20,8,128]{3,2,1,0:T(8,128)S(1)}, bf16[128,1024]{...) custom-call(bf16[8,232,128]{2,1,0:T(8,128)(2,1)S(1)} %all-to-all-don, ...), custom_call_target="tpu_custom_call" | custom-call | tf_op jit(solution)/shard_map/pallas_call | solution.py:753
  20.1 11.3 %all_to_all.20.received = bf16[32,8,128]{2,1,0:T(8,128)(2,1)S(1)} all-to-all(bf16[32,8,128]{2,1,0:T(8,128)(2,1)S(1)} %get-tuple-element.28), channel_id=1, replica_groups=mesh['fx'=2,'fy'=4,'st'=4] {'fx','fy','st'}, dimensions={0} | all-to-all | bytes 131072 | tf_op jit(solution)/shard_map/all_to_all | solution.py:806
  31.4 0.0 copy-done.2
  31.4 3.4 %shard_map.168 = (f32[2,6,64,128]{3,2,1,0:T(8,128)S(1)}, bf16[2,384,128]{2,1,0:T(8,128)(2,1)S(1)}, bf16[32,8,128]{2,1,0:T(8,128)(2,1)S(1)}) custom-call(bf16[32,8,128]{2,1,0:T(8,128)(2,1)S(1)} %all_to_all.20.received, f32[2,6,64,128]{3,2,1,0:T(8,128)S(1)} %get-tuple-element.29.adjoint_in, bf16[2,2,6,64,128]{4,3,2,1,0:T(8,128)(2,1)S(1)} %get-tuple-element.30.rhs, ...), custom_call_target="tpu_custom_call" | custom-call | tf_op jit(solution)/shard_map/pallas_call | solution.py:753
  34.8 9.2 %all_to_all.21.received = bf16[32,8,128]{2,1,0:T(8,128)(2,1)S(1)} all-to-all(bf16[32,8,128]{2,1,0:T(8,128)(2,1)S(1)} %get-tuple-element.37), channel_id=1, replica_groups=mesh['fx'=2,'fy'=4,'st'=4] {'fx','fy','st'}, dimensions={0} | all-to-all | bytes 131072 | tf_op jit(solution)/shard_map/all_to_all | solution.py:817
  44.0 2.1 %shard_map.169 = bf16[8,120,128]{2,1,0:T(8,128)(2,1)S(1)} custom-call(bf16[32,8,128]{2,1,0:T(8,128)(2,1)S(1)} %all_to_all.21.received, f32[2,6,64,128]{3,2,1,0:T(8,128)S(1)} %get-tuple-element.38.tangent_in, bf16[2,384,128]{2,1,0:T(8,128)(2,1)S(1)} %get-tuple-element.39.adjoint_last, bf16[2,2,6,64,128]{4,3,2,1,0:T(8,128)(2,1)S(1)} %get-tuple-element.30.rhs, ...), custom_call_target="tpu_custom_call" | custom-call | tf_op jit(solution)/shard_map/pallas_call | solution.py:753
  46.1 9.1 %all_to_all.22.received = bf16[8,120,128]{2,1,0:T(8,128)(2,1)S(1)} all-to-all(bf16[8,120,128]{2,1,0:T(8,128)(2,1)S(1)} %shard_map.169), channel_id=1, replica_groups=mesh['fx'=2,'fy'=4,'st'=4] {'fx','fy'}, dimensions={0} | all-to-all | bytes 491520 | tf_op jit(solution)/shard_map/all_to_all | solution.py:828
  55.2 1.0 %shard_map.170 = (bf16[6,64,128]{2,1,0:T(8,128)(2,1)}, bf16[6,64,128]{2,1,0:T(8,128)(2,1)}, f32[4,4,384]{2,1,0:T(4,128)}, f32[4,4,384]{2,1,0:T(4,128)}) custom-call(bf16[8,120,128]{2,1,0:T(8,128)(2,1)S(1)} %all_to_all.22.received), custom_call_target="tpu_custom_call" | custom-call | tf_op jit(solution)/shard_map/pallas_call | solution.py:753
Async XLA Ops:
  0.6 8.5 %copy-start.1 = (f32[4,4,384]{2,1,0:T(4,128)S(1)}, f32[4,4,384]{2,1,0:T(4,128)}, u32[]{:S(2)}) copy-start(f32[4,4,384]{2,1,0:T(4,128)} %load.5) | copy-start | bytes 73732
  0.6 8.5 %copy-start = (bf16[4,384,384]{2,1,0:T(8,128)(2,1)S(1)}, bf16[4,384,384]{2,1,0:T(8,128)(2,1)}, u32[]{:S(2)}) copy-start(bf16[4,384,384]{2,1,0:T(8,128)(2,1)} %inverse.5) | copy-start | bytes 3538948
  0.7 8.5 %copy-start.5 = (f32[6]{0:T(128)S(1)}, f32[6]{0:T(128)}, u32[]{:S(2)}) copy-start(f32[6]{0:T(128)} %penalty.1) | copy-start | bytes 76
  0.7 8.5 %copy-start.4 = (bf16[3,64,64]{2,1,0:T(8,128)(2,1)S(1)}, bf16[3,64,64]{2,1,0:T(8,128)(2,1)}, u32[]{:S(2)}) copy-start(bf16[3,64,64]{2,1,0:T(8,128)(2,1)} %deriv.1) | copy-start | bytes 73732
  3.9 14.4 %copy-start.3 = (bf16[6,384]{1,0:T(8,128)(2,1)S(1)}, bf16[6,384]{1,0:T(8,128)(2,1)}, u32[]{:S(2)}) copy-start(bf16[6,384]{1,0:T(8,128)(2,1)} %coupling.5) | copy-start | bytes 13828
  3.9 14.4 %all-to-all-start = ((bf16[8,232,128]{2,1,0:T(8,128)(2,1)}), bf16[8,232,128]{2,1,0:T(8,128)(2,1)S(1)}, u32[]{:S(2)}, u32[]{:S(2)}) async-start(bf16[8,232,128]{2,1,0:T(8,128)(2,1)} %shard_map.165), calls=%async_computation | async-start | bytes 950272 | tf_op jit(solution)/shard_map/all_to_all | solution.py:790
  9.1 22.2 %copy-start.2 = (f32[4,4,384]{2,1,0:T(4,128)S(1)}, f32[4,4,384]{2,1,0:T(4,128)}, u32[]{:S(2)}) copy-start(f32[4,4,384]{2,1,0:T(4,128)} %shell_rhs.3) | copy-start | bytes 73732

commit v6 on v5

--- a/solution.py
+++ b/solution.py
@@ -284,7 +284,7 @@
         self.shell_rows = 2 * ns * self.tiles
 
     def rank(self):
-        return lax.axis_index("fx") * self.ny + lax.axis_index("fy")
+        return lax.axis_index("fy") * self.nx + lax.axis_index("fx")
 
 
 def fits(nx, ny, ns, local_shape, slots, panels, width):
@@ -613,17 +613,17 @@
         for f in range(2):
             for a in range(nv):
                 first = (f * nv + a) * 16
-                parts = [received[h * ny + y, pl.ds(first, 16), :] for y in range(ny)]
+                parts = [received[y * nx + h, pl.ds(first, 16), :] for y in range(ny)]
                 for k, part in enumerate(swap_groups(parts, masks)):
                     rhs[f, h, a, pl.ds(16 * k, 16), :] = part
         first = 2 * plan.field_rows
         count = plan.rows - first
-        tails = [received[h * ny + y, pl.ds(first, count), :] for y in range(ny)]
+        tails = [received[y * nx + h, pl.ds(first, count), :] for y in range(ny)]
         info = [x.astype(F32).reshape(plan.per, 8, LANES) for x in tails]
         pieces = [[] for _ in range(ny)]
         for r in range(0, count, 16):
             size = min(16, count - r)
-            parts = [received[h * ny + y, pl.ds(first + r, size), :] for y in range(ny)]
+            parts = [received[y * nx + h, pl.ds(first + r, size), :] for y in range(ny)]
             short = [(a[:size], b[:size]) for a, b in masks]
             for k, part in enumerate(swap_groups(parts, short)):
                 pieces[k] += [part.astype(F32)[i : i + 8] for i in range(0, size, 8)]
@@ -722,7 +722,7 @@
                     shift = plan.own * n - plan.window * y - plan.halo
                     term = _roll(parts[n], shift) * group[n]
                     total = term if total is None else total + term
-                out[h * ny + y, pl.ds(16 * a, 16), :] = total
+                out[y * nx + h, pl.ds(16 * a, 16), :] = total
 
 
 def last_kernel(plan, received, tangent, adjoint, shell_tangent, shell_adjoint):
@@ -766,7 +766,7 @@
     iface_count,
 ):
     nv, nx, ns, groups = plan.nv, plan.nx, plan.ns, plan.groups
-    flow, everyone = ("fx", "fy"), ("fx", "fy", "st")
+    flow, everyone = ("fy", "fx"), ("fy", "fx", "st")
     state = ((nx, nv, NP, LANES), F32)
     coef = ((nv, NP, LANES), F32)
     scr = ((8, 8, LANES), F32)

time: 56.5 us -> 55.2 us (0.977)
  waiting for transfers between devices: 8.36 us -> 7.46 us
    all_to_all x1, blocking collectives: 9.14 us -> 8.23 us  [slab_body(): lax.all_to_all(sent, flow, split_axis=0, concat_axis=0, tiled=True)]
    all_to_all x1, waiting for transfers between devices: 8.36 us -> 7.46 us  [slab_body(): slab = lax.all_to_all(packed, flow, split_axis=0, concat_axis=0, tiled=True)]
where the time goes in v6:
time: 55.2 us; the launch traced here: 54.9 us
  blocking collectives  29.2 us (53%)
  Pallas kernels  11.5 us (21%)
  waiting for transfers between devices  7.46 us (14%)
  starting transfers between devices  5.21 us (9%)
  between operations  1.48 us (3%)
    all_to_all x2, blocking collectives, slab_body(): lax.all_to_all(sent, everyone, split_axis=0, concat_axis=0, tiled=True)  20.9 us
    pallas_call x6, Pallas kernels, call(): pl.pallas_call(functools.partial(kernel, plan), out_shape=[jax.ShapeDtype...  11.5 us
    all_to_all x1, blocking collectives, slab_body(): lax.all_to_all(sent, flow, split_axis=0, concat_axis=0, tiled=True)  8.23 us
    all_to_all x1, waiting for transfers between devices, slab_body(): slab = lax.all_to_all(packed, flow, split_axis=0, concat_axis=0, tiled=True)  7.46 us
    all_to_all x1, starting transfers between devices, slab_body(): slab = lax.all_to_all(packed, flow, split_axis=0, concat_axis=0, tiled=True)  5.21 us
  transfers between devices with their start and end apart: 1, of which 1 were waited for; matrix products, arithmetic and copies ran while one was open for 0% of the time, Pallas kernels for 1%

profile of v6, /device:TPU:0, one launch (start us, length us, event | category | flops | bytes accessed | tf_op | source)
XLA Modules:
  0.0 54.9 jit_solution(5459710749491658600)
XLA Ops:
  0.6 0.0 copy-start.1
  0.6 0.0 copy-start
  0.7 0.0 copy-start.5
  0.7 0.0 copy-start.4
  1.4 2.5 %shard_map.165 = bf16[8,232,128]{2,1,0:T(8,128)(2,1)} custom-call(bf16[6,64,128]{2,1,0:T(8,128)(2,1)} %bitcast.12, bf16[6,64,128]{2,1,0:T(8,128)(2,1)} %bitcast.13, bf16[3,6,6,128]{3,2,1,0:T(8,128)(2,1)} %bitcast.14, f32[6,1,128]{2,1,0:T(1,128)} %bitcast.15, s32[1,128]{1,0:T(1,128)} %elem_hbm.1, s32[1,128]{1,0:T(1,128)} %node_hbm.1, f32[1,128]{1,0:T(1,128)} %weight_hbm.1, ...), custom_call_target="tpu_custom_call" | custom-call | tf_op jit(solution)/shard_map/pallas_call | solution.py:753
  3.9 0.0 copy-start.3
  3.9 5.2 %all-to-all-start = ((bf16[8,232,128]{2,1,0:T(8,128)(2,1)}), bf16[8,232,128]{2,1,0:T(8,128)(2,1)S(1)}, u32[]{:S(2)}, u32[]{:S(2)}) async-start(bf16[8,232,128]{2,1,0:T(8,128)(2,1)} %shard_map.165), calls=%async_computation | async-start | bytes 950272 | tf_op jit(solution)/shard_map/all_to_all | solution.py:790
  9.1 0.0 copy-done.1
  9.1 0.0 copy-done
  9.1 0.0 copy-done.5
  9.1 0.0 copy-done.4
  9.1 0.0 copy-start.2
  9.2 0.8 %shard_map.166 = (bf16[64,480]{1,0:T(8,128)(2,1)S(1)}, bf16[64,480]{1,0:T(8,128)(2,1)S(1)}, f32[8,384]{1,0:T(8,128)S(1)}, f32[6,64,128]{2,1,0:T(8,128)S(1)}, f32[6,16,128]{2,1,0:T(8,128)S(1)}) custom-call(bf16[3,64,64]{2,1,0:T(8,128)(2,1)S(1)} %copy-done.4, f32[4,4,384]{2,1,0:T(4,128)S(1)} %copy-done.1, bf16[4,384,384]{2,1,0:T(8,128)(2,1)S(1)} %copy-done, ...), custom_call_target="tpu_custom_call" | custom-call | tf_op jit(solution)/shard_map/pallas_call | solution.py:753
  9.9 7.5 %all-to-all-done.received = bf16[8,232,128]{2,1,0:T(8,128)(2,1)S(1)} async-done(((bf16[8,232,128]{2,1,0:T(8,128)(2,1)}), bf16[8,232,128]{2,1,0:T(8,128)(2,1)S(1)}, u32[]{:S(2)}, u32[]{:S(2)}) %all-to-all-start) | async-done | bytes 475168 | tf_op jit(solution)/shard_map/all_to_all | solution.py:790
  17.4 0.0 copy-done.3
  17.4 1.8 %shard_map.167 = (f32[2,6,64,128]{3,2,1,0:T(8,128)S(1)}, bf16[2,2,6,64,128]{4,3,2,1,0:T(8,128)(2,1)S(1)}, f32[2,20,8,128]{3,2,1,0:T(8,128)S(1)}, bf16[128,1024]{...) custom-call(bf16[8,232,128]{2,1,0:T(8,128)(2,1)S(1)} %all-to-all-don, ...), custom_call_target="tpu_custom_call" | custom-call | tf_op jit(solution)/shard_map/pallas_call | solution.py:753
  19.2 11.9 %all_to_all.20.received = bf16[32,8,128]{2,1,0:T(8,128)(2,1)S(1)} all-to-all(bf16[32,8,128]{2,1,0:T(8,128)(2,1)S(1)} %get-tuple-element.28), channel_id=1, replica_groups=mesh['fx'=2,'fy'=4,'st'=4] {'fy','fx','st'}, dimensions={0} | all-to-all | bytes 131072 | tf_op jit(solution)/shard_map/all_to_all | solution.py:806
  31.1 0.0 copy-done.2
  31.2 3.4 %shard_map.168 = (f32[2,6,64,128]{3,2,1,0:T(8,128)S(1)}, bf16[2,384,128]{2,1,0:T(8,128)(2,1)S(1)}, bf16[32,8,128]{2,1,0:T(8,128)(2,1)S(1)}) custom-call(bf16[32,8,128]{2,1,0:T(8,128)(2,1)S(1)} %all_to_all.20.received, f32[2,6,64,128]{3,2,1,0:T(8,128)S(1)} %get-tuple-element.29.adjoint_in, bf16[2,2,6,64,128]{4,3,2,1,0:T(8,128)(2,1)S(1)} %get-tuple-element.30.rhs, ...), custom_call_target="tpu_custom_call" | custom-call | tf_op jit(solution)/shard_map/pallas_call | solution.py:753
  34.6 9.0 %all_to_all.21.received = bf16[32,8,128]{2,1,0:T(8,128)(2,1)S(1)} all-to-all(bf16[32,8,128]{2,1,0:T(8,128)(2,1)S(1)} %get-tuple-element.37), channel_id=1, replica_groups=mesh['fx'=2,'fy'=4,'st'=4] {'fy','fx','st'}, dimensions={0} | all-to-all | bytes 131072 | tf_op jit(solution)/shard_map/all_to_all | solution.py:817
  43.5 2.1 %shard_map.169 = bf16[8,120,128]{2,1,0:T(8,128)(2,1)S(1)} custom-call(bf16[32,8,128]{2,1,0:T(8,128)(2,1)S(1)} %all_to_all.21.received, f32[2,6,64,128]{3,2,1,0:T(8,128)S(1)} %get-tuple-element.38.tangent_in, bf16[2,384,128]{2,1,0:T(8,128)(2,1)S(1)} %get-tuple-element.39.adjoint_last, bf16[2,2,6,64,128]{4,3,2,1,0:T(8,128)(2,1)S(1)} %get-tuple-element.30.rhs, ...), custom_call_target="tpu_custom_call" | custom-call | tf_op jit(solution)/shard_map/pallas_call | solution.py:753
  45.6 8.2 %all_to_all.22.received = bf16[8,120,128]{2,1,0:T(8,128)(2,1)S(1)} all-to-all(bf16[8,120,128]{2,1,0:T(8,128)(2,1)S(1)} %shard_map.169), channel_id=1, replica_groups=mesh['fx'=2,'fy'=4,'st'=4] {'fy','fx'}, dimensions={0} | all-to-all | bytes 491520 | tf_op jit(solution)/shard_map/all_to_all | solution.py:828
  53.9 1.0 %shard_map.170 = (bf16[6,64,128]{2,1,0:T(8,128)(2,1)}, bf16[6,64,128]{2,1,0:T(8,128)(2,1)}, f32[4,4,384]{2,1,0:T(4,128)}, f32[4,4,384]{2,1,0:T(4,128)}) custom-call(bf16[8,120,128]{2,1,0:T(8,128)(2,1)S(1)} %all_to_all.22.received), custom_call_target="tpu_custom_call" | custom-call | tf_op jit(solution)/shard_map/pallas_call | solution.py:753
Async XLA Ops:
  0.6 8.5 %copy-start.1 = (f32[4,4,384]{2,1,0:T(4,128)S(1)}, f32[4,4,384]{2,1,0:T(4,128)}, u32[]{:S(2)}) copy-start(f32[4,4,384]{2,1,0:T(4,128)} %load.5) | copy-start | bytes 73732
  0.6 8.5 %copy-start = (bf16[4,384,384]{2,1,0:T(8,128)(2,1)S(1)}, bf16[4,384,384]{2,1,0:T(8,128)(2,1)}, u32[]{:S(2)}) copy-start(bf16[4,384,384]{2,1,0:T(8,128)(2,1)} %inverse.5) | copy-start | bytes 3538948
  0.7 8.5 %copy-start.5 = (f32[6]{0:T(128)S(1)}, f32[6]{0:T(128)}, u32[]{:S(2)}) copy-start(f32[6]{0:T(128)} %penalty.1) | copy-start | bytes 76
  0.7 8.5 %copy-start.4 = (bf16[3,64,64]{2,1,0:T(8,128)(2,1)S(1)}, bf16[3,64,64]{2,1,0:T(8,128)(2,1)}, u32[]{:S(2)}) copy-start(bf16[3,64,64]{2,1,0:T(8,128)(2,1)} %deriv.1) | copy-start | bytes 73732
  3.9 13.5 %copy-start.3 = (bf16[6,384]{1,0:T(8,128)(2,1)S(1)}, bf16[6,384]{1,0:T(8,128)(2,1)}, u32[]{:S(2)}) copy-start(bf16[6,384]{1,0:T(8,128)(2,1)} %coupling.5) | copy-start | bytes 13828
  3.9 13.5 %all-to-all-start = ((bf16[8,232,128]{2,1,0:T(8,128)(2,1)}), bf16[8,232,128]{2,1,0:T(8,128)(2,1)S(1)}, u32[]{:S(2)}, u32[]{:S(2)}) async-start(bf16[8,232,128]{2,1,0:T(8,128)(2,1)} %shard_map.165), calls=%async_computation | async-start | bytes 950272 | tf_op jit(solution)/shard_map/all_to_all | solution.py:790
  9.1 22.0 %copy-start.2 = (f32[4,4,384]{2,1,0:T(4,128)S(1)}, f32[4,4,384]{2,1,0:T(4,128)}, u32[]{:S(2)}) copy-start(f32[4,4,384]{2,1,0:T(4,128)} %shell_rhs.3) | copy-start | bytes 73732

commit v7 on v6

--- a/solution.py
+++ b/solution.py
@@ -281,7 +281,7 @@
         self.rows = 2 * self.field_rows + self.per * 8
         self.depth = 7 * NP + 32
         self.slots = ny * LANES
-        self.shell_rows = 2 * ns * self.tiles
+        self.shell_rows = -(-ns * self.tiles // 8) * 8
 
     def rank(self):
         return lax.axis_index("fy") * self.nx + lax.axis_index("fx")
@@ -707,7 +707,8 @@
     tangent = states[-1]
     shell = jnp.where(lax.rem(rank, share) == 0, result[0], result[1])
     tiles = [shell[:ns, LANES * t : LANES * (t + 1)] for t in range(plan.tiles)]
-    shell = _split(jnp.concatenate(tiles, axis=0))
+    tiles.append(jnp.zeros((plan.shell_rows - ns * plan.tiles, LANES), F32))
+    shell = jnp.concatenate(tiles, axis=0).astype(BF16)
     for dest in range(plan.groups):
         out[dest, pl.ds(plan.field_rows, shell.shape[0]), :] = shell
     lane = _iota((16, LANES), 1)
@@ -730,7 +731,7 @@
     for panel in range(plan.held):
         for i, ref in enumerate((shell_adjoint, shell_tangent)):
             block = received[panel * share + i, pl.ds(plan.field_rows, plan.shell_rows), :]
-            block = _fold(block.astype(F32))
+            block = block.astype(F32)
             for t in range(plan.tiles):
                 columns = pl.ds(LANES * t, LANES)
                 ref[:, panel, columns] = block[ns * t : ns * (t + 1)]

time: 55.2 us -> 55 us (level)
  no operation moved by 1% of the time
where the time goes in v7:
time: 55 us; the launch traced here: 54.7 us
  blocking collectives  29 us (53%)
  Pallas kernels  11.5 us (21%)
  waiting for transfers between devices  7.46 us (14%)
  starting transfers between devices  5.21 us (9%)
  between operations  1.48 us (3%)
    all_to_all x2, blocking collectives, slab_body(): lax.all_to_all(sent, everyone, split_axis=0, concat_axis=0, tiled=True)  20.9 us
    pallas_call x6, Pallas kernels, call(): pl.pallas_call(functools.partial(kernel, plan), out_shape=[jax.ShapeDtype...  11.5 us
    all_to_all x1, blocking collectives, slab_body(): lax.all_to_all(sent, flow, split_axis=0, concat_axis=0, tiled=True)  8.06 us
    all_to_all x1, waiting for transfers between devices, slab_body(): slab = lax.all_to_all(packed, flow, split_axis=0, concat_axis=0, tiled=True)  7.46 us
    all_to_all x1, starting transfers between devices, slab_body(): slab = lax.all_to_all(packed, flow, split_axis=0, concat_axis=0, tiled=True)  5.21 us
  transfers between devices with their start and end apart: 1, of which 1 were waited for; matrix products, arithmetic and copies ran while one was open for 0% of the time, Pallas kernels for 1%

profile of v7, /device:TPU:0, one launch (start us, length us, event | category | flops | bytes accessed | tf_op | source)
XLA Modules:
  0.0 54.7 jit_solution(11670349001487081660)
XLA Ops:
  0.6 0.0 copy-start.1
  0.6 0.0 copy-start
  0.7 0.0 copy-start.5
  0.7 0.0 copy-start.4
  1.4 2.5 %shard_map.165 = bf16[8,232,128]{2,1,0:T(8,128)(2,1)} custom-call(bf16[6,64,128]{2,1,0:T(8,128)(2,1)} %bitcast.12, bf16[6,64,128]{2,1,0:T(8,128)(2,1)} %bitcast.13, bf16[3,6,6,128]{3,2,1,0:T(8,128)(2,1)} %bitcast.14, f32[6,1,128]{2,1,0:T(1,128)} %bitcast.15, s32[1,128]{1,0:T(1,128)} %elem_hbm.1, s32[1,128]{1,0:T(1,128)} %node_hbm.1, f32[1,128]{1,0:T(1,128)} %weight_hbm.1, ...), custom_call_target="tpu_custom_call" | custom-call | tf_op jit(solution)/shard_map/pallas_call | solution.py:754
  3.9 0.0 copy-start.3
  3.9 5.2 %all-to-all-start = ((bf16[8,232,128]{2,1,0:T(8,128)(2,1)}), bf16[8,232,128]{2,1,0:T(8,128)(2,1)S(1)}, u32[]{:S(2)}, u32[]{:S(2)}) async-start(bf16[8,232,128]{2,1,0:T(8,128)(2,1)} %shard_map.165), calls=%async_computation | async-start | bytes 950272 | tf_op jit(solution)/shard_map/all_to_all | solution.py:791
  9.1 0.0 copy-done.1
  9.1 0.0 copy-done
  9.1 0.0 copy-done.5
  9.1 0.0 copy-done.4
  9.1 0.0 copy-start.2
  9.2 0.8 %shard_map.166 = (bf16[64,480]{1,0:T(8,128)(2,1)S(1)}, bf16[64,480]{1,0:T(8,128)(2,1)S(1)}, f32[8,384]{1,0:T(8,128)S(1)}, f32[6,64,128]{2,1,0:T(8,128)S(1)}, f32[6,16,128]{2,1,0:T(8,128)S(1)}) custom-call(bf16[3,64,64]{2,1,0:T(8,128)(2,1)S(1)} %copy-done.4, f32[4,4,384]{2,1,0:T(4,128)S(1)} %copy-done.1, bf16[4,384,384]{2,1,0:T(8,128)(2,1)S(1)} %copy-done, ...), custom_call_target="tpu_custom_call" | custom-call | tf_op jit(solution)/shard_map/pallas_call | solution.py:754
  9.9 7.5 %all-to-all-done.received = bf16[8,232,128]{2,1,0:T(8,128)(2,1)S(1)} async-done(((bf16[8,232,128]{2,1,0:T(8,128)(2,1)}), bf16[8,232,128]{2,1,0:T(8,128)(2,1)S(1)}, u32[]{:S(2)}, u32[]{:S(2)}) %all-to-all-start) | async-done | bytes 475168 | tf_op jit(solution)/shard_map/all_to_all | solution.py:791
  17.4 0.0 copy-done.3
  17.4 1.8 %shard_map.167 = (f32[2,6,64,128]{3,2,1,0:T(8,128)S(1)}, bf16[2,2,6,64,128]{4,3,2,1,0:T(8,128)(2,1)S(1)}, f32[2,20,8,128]{3,2,1,0:T(8,128)S(1)}, bf16[128,1024]{...) custom-call(bf16[8,232,128]{2,1,0:T(8,128)(2,1)S(1)} %all-to-all-don, ...), custom_call_target="tpu_custom_call" | custom-call | tf_op jit(solution)/shard_map/pallas_call | solution.py:754
  19.2 11.9 %all_to_all.20.received = bf16[32,8,128]{2,1,0:T(8,128)(2,1)S(1)} all-to-all(bf16[32,8,128]{2,1,0:T(8,128)(2,1)S(1)} %get-tuple-element.28), channel_id=1, replica_groups=mesh['fx'=2,'fy'=4,'st'=4] {'fy','fx','st'}, dimensions={0} | all-to-all | bytes 131072 | tf_op jit(solution)/shard_map/all_to_all | solution.py:807
  31.1 0.0 copy-done.2
  31.2 3.4 %shard_map.168 = (f32[2,6,64,128]{3,2,1,0:T(8,128)S(1)}, bf16[2,384,128]{2,1,0:T(8,128)(2,1)S(1)}, bf16[32,8,128]{2,1,0:T(8,128)(2,1)S(1)}) custom-call(bf16[32,8,128]{2,1,0:T(8,128)(2,1)S(1)} %all_to_all.20.received, f32[2,6,64,128]{3,2,1,0:T(8,128)S(1)} %get-tuple-element.29.adjoint_in, bf16[2,2,6,64,128]{4,3,2,1,0:T(8,128)(2,1)S(1)} %get-tuple-element.30.rhs, ...), custom_call_target="tpu_custom_call" | custom-call | tf_op jit(solution)/shard_map/pallas_call | solution.py:754
  34.6 9.0 %all_to_all.21.received = bf16[32,8,128]{2,1,0:T(8,128)(2,1)S(1)} all-to-all(bf16[32,8,128]{2,1,0:T(8,128)(2,1)S(1)} %get-tuple-element.37), channel_id=1, replica_groups=mesh['fx'=2,'fy'=4,'st'=4] {'fy','fx','st'}, dimensions={0} | all-to-all | bytes 131072 | tf_op jit(solution)/shard_map/all_to_all | solution.py:818
  43.5 2.1 %shard_map.169 = bf16[8,112,128]{2,1,0:T(8,128)(2,1)S(1)} custom-call(bf16[32,8,128]{2,1,0:T(8,128)(2,1)S(1)} %all_to_all.21.received, f32[2,6,64,128]{3,2,1,0:T(8,128)S(1)} %get-tuple-element.38.tangent_in, bf16[2,384,128]{2,1,0:T(8,128)(2,1)S(1)} %get-tuple-element.39.adjoint_last, bf16[2,2,6,64,128]{4,3,2,1,0:T(8,128)(2,1)S(1)} %get-tuple-element.30.rhs, ...), custom_call_target="tpu_custom_call" | custom-call | tf_op jit(solution)/shard_map/pallas_call | solution.py:754
  45.6 8.1 %all_to_all.22.received = bf16[8,112,128]{2,1,0:T(8,128)(2,1)S(1)} all-to-all(bf16[8,112,128]{2,1,0:T(8,128)(2,1)S(1)} %shard_map.169), channel_id=1, replica_groups=mesh['fx'=2,'fy'=4,'st'=4] {'fy','fx'}, dimensions={0} | all-to-all | bytes 458752 | tf_op jit(solution)/shard_map/all_to_all | solution.py:829
  53.7 1.0 %shard_map.170 = (bf16[6,64,128]{2,1,0:T(8,128)(2,1)}, bf16[6,64,128]{2,1,0:T(8,128)(2,1)}, f32[4,4,384]{2,1,0:T(4,128)}, f32[4,4,384]{2,1,0:T(4,128)}) custom-call(bf16[8,112,128]{2,1,0:T(8,128)(2,1)S(1)} %all_to_all.22.received), custom_call_target="tpu_custom_call" | custom-call | tf_op jit(solution)/shard_map/pallas_call | solution.py:754
Async XLA Ops:
  0.6 8.5 %copy-start.1 = (f32[4,4,384]{2,1,0:T(4,128)S(1)}, f32[4,4,384]{2,1,0:T(4,128)}, u32[]{:S(2)}) copy-start(f32[4,4,384]{2,1,0:T(4,128)} %load.5) | copy-start | bytes 73732
  0.6 8.5 %copy-start = (bf16[4,384,384]{2,1,0:T(8,128)(2,1)S(1)}, bf16[4,384,384]{2,1,0:T(8,128)(2,1)}, u32[]{:S(2)}) copy-start(bf16[4,384,384]{2,1,0:T(8,128)(2,1)} %inverse.5) | copy-start | bytes 3538948
  0.7 8.5 %copy-start.5 = (f32[6]{0:T(128)S(1)}, f32[6]{0:T(128)}, u32[]{:S(2)}) copy-start(f32[6]{0:T(128)} %penalty.1) | copy-start | bytes 76
  0.7 8.5 %copy-start.4 = (bf16[3,64,64]{2,1,0:T(8,128)(2,1)S(1)}, bf16[3,64,64]{2,1,0:T(8,128)(2,1)}, u32[]{:S(2)}) copy-start(bf16[3,64,64]{2,1,0:T(8,128)(2,1)} %deriv.1) | copy-start | bytes 73732
  3.9 13.5 %copy-start.3 = (bf16[6,384]{1,0:T(8,128)(2,1)S(1)}, bf16[6,384]{1,0:T(8,128)(2,1)}, u32[]{:S(2)}) copy-start(bf16[6,384]{1,0:T(8,128)(2,1)} %coupling.5) | copy-start | bytes 13828
  3.9 13.5 %all-to-all-start = ((bf16[8,232,128]{2,1,0:T(8,128)(2,1)}), bf16[8,232,128]{2,1,0:T(8,128)(2,1)S(1)}, u32[]{:S(2)}, u32[]{:S(2)}) async-start(bf16[8,232,128]{2,1,0:T(8,128)(2,1)} %shard_map.165), calls=%async_computation | async-start | bytes 950272 | tf_op jit(solution)/shard_map/all_to_all | solution.py:791
  9.1 22.0 %copy-start.2 = (f32[4,4,384]{2,1,0:T(4,128)S(1)}, f32[4,4,384]{2,1,0:T(4,128)}, u32[]{:S(2)}) copy-start(f32[4,4,384]{2,1,0:T(4,128)} %shell_rhs.3) | copy-start | bytes 73732
